TPU v7x, 32 devices: a whole 2x2x4 slice. The times are simulated.
32 devices in a mesh: dp: 2 (over y), expert: 16 (over z, x, core).
Axes of the slice: x: 2, y: 2, z: 4, core: 2. Of those that a mesh axis runs over, the one named last changes fastest.
Arguments:
- tokens_in: bfloat16 [32, 512, 1536], P('expert', 'dp'), may hold values from -6 to 6
- out_grad: bfloat16 [32, 512, 1536], P('expert', 'dp'), may hold values from -6 to 6
- seq_lengths: int32 [32], P('expert'), may hold values from 1 to 512, 12288 in all
- seq_order: int32 [32], P('expert'), may hold values from 0 to 1, as said below
- routes_top: int32 [32, 512, 6], P(('dp', 'expert')), may hold values from 0 to 15, all different within a row; in each aligned block of 512 rows (0 to 511, 512 to 1023, ..., all dimensions but the last counted through in order) at most 216 rows name the same one
- norm_gain: float32 [1536], P(('dp', 'expert')), may hold values from 0.5 to 1.5
- in_weight: float32 [1536, 6448], P(('dp', 'expert')), may hold values from -0.15625 to 0.15625
- conv_weight: float32 [3328, 4], P(('dp', 'expert')), may hold values from -3 to 3
- conv_bias: float32 [3328], P(('dp', 'expert')), may hold values from -1.8 to 1.8
- step_bias: float32 [48], replicated, may hold values from -5 to -1
- decay_log: float32 [48], replicated, may hold values from 0 to 2.7
- skip_gain: float32 [48], replicated, may hold values from 0.5 to 1.5
- gated_gain: float32 [3072], P(('dp', 'expert')), may hold values from 0.5 to 1.5
- out_weight: float32 [3072, 1536], P(('dp', 'expert')), may hold values from -0.109375 to 0.109375
- ffn_gain: float32 [1536], P(('dp', 'expert')), may hold values from 0.5 to 1.5
- router_weight: float32 [1536, 16], P(('dp', 'expert')), may hold values from -0.078125 to 0.078125
- expert_gate_up: float32 [16, 1536, 1024], P('expert', 'dp'), may hold values from -0.15625 to 0.15625
- expert_down: float32 [16, 512, 1536], P('expert', 'dp'), may hold values from -0.5 to 0.5
- shared_gate_up: float32 [1536, 2048], P(('dp', 'expert')), may hold values from -0.15625 to 0.15625
- shared_down: float32 [1024, 1536], P(('dp', 'expert')), may hold values from -0.375 to 0.375
Outputs:
- block_out: bfloat16 [32, 512, 1536], P('expert', 'dp')
- input_grad: bfloat16 [32, 512, 1536], P('expert', 'dp')
- grad_norm_gain: float32 [1536], P(('dp', 'expert'))
- grad_in_weight: float32 [1536, 6448], P(('dp', 'expert'))
- grad_conv_weight: float32 [3328, 4], P(('dp', 'expert'))
- grad_conv_bias: float32 [3328], P(('dp', 'expert'))
- grad_step_bias: float32 [48], replicated
- grad_decay_log: float32 [48], replicated
- grad_skip_gain: float32 [48], replicated
- grad_gated_gain: float32 [3072], P(('dp', 'expert'))
- grad_out_weight: float32 [3072, 1536], P(('dp', 'expert'))
- grad_ffn_gain: float32 [1536], P(('dp', 'expert'))
- grad_router_weight: float32 [1536, 16], P(('dp', 'expert'))
- grad_expert_gate_up: float32 [16, 1536, 1024], P('expert', 'dp')
- grad_expert_down: float32 [16, 512, 1536], P('expert', 'dp')
- grad_shared_gate_up: float32 [1536, 2048], P(('dp', 'expert'))
- grad_shared_down: float32 [1024, 1536], P(('dp', 'expert'))
Inputs may be any that keep to these rules, and one draw needn't show every extreme that they name: `routes_top`: each row names 6 different experts; among the rows of one device's tile no expert is named more than 216 times, a bound that some block reaches. `seq_lengths`: some sequence is exactly 512 long. `seq_order`: each aligned group of 2 entries (the sequences of one index of expert) is a permutation of 0 to 1.
All inputs are finite; a program needn't handle non-finite values. No bound on the sum of `seq_lengths` on one device may be relied on, other than what follows from the above.
Results may differ from a plain program's by a relative error of at most 0.012.
The roundings to bfloat16 on the way count: a program that leaves them out, or rounds other values in their place, can miss the bound.
Values may be sent and summed in bfloat16 or wider, within the bound.
No kernel may reach another device: no remote copies, remote signals or barrier semaphores. Data moves between devices by JAX's collectives and lax.ppermute only.
A program may use at most 576 MiB of HBM per device.

v0:
```python
from functools import partial
import math

import jax
import jax.numpy as jnp
from jax import lax
from jax.sharding import PartitionSpec as P

BLK = 128


EPSILON = 1e-05
FULL_PRECISION = lax.Precision.HIGHEST


def rms_scale(values, gain_row):
    return (
        values * lax.rsqrt(jnp.mean(values * values, axis=-1, keepdims=True) + EPSILON) * gain_row
    )


def swiglu(pre_act):
    half_width = pre_act.shape[-1] // 2
    return jax.nn.silu(pre_act[..., :half_width]) * pre_act[..., half_width:]


def ssd_blocks(head_inputs, step_sizes, decay_rates, state_in, state_out, block_len):
    seq_count, length, head_count, head_width = head_inputs.shape
    blocks = length // block_len
    head_inputs = head_inputs.reshape(seq_count, blocks, block_len, head_count, head_width)
    step_sizes = step_sizes.reshape(seq_count, blocks, block_len, head_count)
    state_in = state_in.reshape(seq_count, blocks, block_len, -1)
    state_out = state_out.reshape(seq_count, blocks, block_len, -1)
    log_decay = step_sizes * -jnp.exp(decay_rates)
    running = jnp.cumsum(log_decay, axis=2)
    spread = running[:, :, :, None, :] - running[:, :, None, :, :]
    causal = (
        lax.broadcasted_iota(jnp.int32, (block_len, block_len), 0)
        >= lax.broadcasted_iota(jnp.int32, (block_len, block_len), 1)
    )[None, None, :, :, None]
    decay_mat = jnp.where(causal, jnp.exp(jnp.where(causal, spread, 0.0)), 0.0)
    scores = jnp.einsum("sktn,skjn->sktj", state_out, state_in, precision=FULL_PRECISION)
    mixing = scores[..., None] * decay_mat * step_sizes[:, :, None, :, :]
    inside = jnp.einsum("sktjh,skjhp->skthp", mixing, head_inputs, precision=FULL_PRECISION)
    tail_decay = jnp.exp(running[:, :, -1:, :] - running) * step_sizes
    states = jnp.einsum(
        "skjh,skjhp,skjn->skhpn", tail_decay, head_inputs, state_in, precision=FULL_PRECISION
    )
    totals = jnp.exp(running[:, :, -1, :])

    def carry_step(previous, carried):
        block_state, factor = carried
        return (previous * factor[:, :, None, None] + block_state, previous)

    initial = jnp.zeros((seq_count, head_count, head_width, state_in.shape[-1]), jnp.float32)
    _, before = lax.scan(
        carry_step, initial, (jnp.moveaxis(states, 1, 0), jnp.moveaxis(totals, 1, 0))
    )
    before = jnp.moveaxis(before, 0, 1)
    across = (
        jnp.einsum("sktn,skhpn->skthp", state_out, before, precision=FULL_PRECISION)
        * jnp.exp(running)[..., None]
    )
    return (inside + across).reshape(seq_count, length, head_count, head_width)


def mixer_local(
    projected,
    conv_kernel,
    conv_shift,
    step_shift,
    decay_rates,
    skip_weights,
    gated_scale,
    seq_count,
    block_len,
):
    inner_width = gated_scale.shape[0]
    head_count = decay_rates.shape[0]
    total_rows, proj_width = projected.shape
    length = total_rows // seq_count
    gate_part = projected[:, :inner_width]
    conv_input = projected[:, inner_width : proj_width - head_count].reshape(seq_count, length, -1)
    step_raw = projected[:, proj_width - head_count :]
    kernel_len = conv_kernel.shape[1]
    padded = jnp.pad(conv_input, ((0, 0), (kernel_len - 1, 0), (0, 0)))
    convolved = conv_shift
    for offset in range(kernel_len):
        convolved = convolved + conv_kernel[:, offset] * padded[:, offset : offset + length]
    convolved = jax.nn.silu(convolved)
    state_width = (convolved.shape[-1] - inner_width) // 2
    head_inputs = convolved[..., :inner_width].reshape(
        seq_count, length, head_count, inner_width // head_count
    )
    state_in = convolved[..., inner_width : inner_width + state_width]
    state_out = convolved[..., inner_width + state_width :]
    step_sizes = jax.nn.softplus(step_raw + step_shift).reshape(seq_count, length, head_count)
    scanned = ssd_blocks(head_inputs, step_sizes, decay_rates, state_in, state_out, block_len)
    scanned = scanned + skip_weights[:, None] * head_inputs
    gated_in = scanned.reshape(total_rows, inner_width) * jax.nn.silu(gate_part)
    return rms_scale(gated_in, gated_scale)


def dot_right(left_mat, right_mat):
    return lax.dot_general(
        left_mat, right_mat, (((1,), (1,)), ((), ())), preferred_element_type=jnp.float32
    )


def dot_left(left_mat, right_mat):
    return lax.dot_general(
        left_mat, right_mat, (((0,), (0,)), ((), ())), preferred_element_type=jnp.float32
    )


def to_low(weight):
    return weight.astype(jnp.bfloat16)


def pad_row(row_block):
    return jnp.concatenate([row_block, jnp.zeros((1, row_block.shape[1]), row_block.dtype)], axis=0)


def pack_shares(members, shares):
    pieces = [jnp.moveaxis(matrix, axis_at, 0).reshape(shares, -1) for matrix, axis_at in members]
    return jnp.concatenate(pieces, axis=1)


def unpack_share(row_block, members, shares):
    results = []
    offset = 0
    for matrix, axis_at in members:
        shape_list = list(matrix.shape)
        lead_len = shape_list[axis_at] // shares
        others = shape_list[:axis_at] + shape_list[axis_at + 1 :]
        amount = lead_len * math.prod(others)
        piece = row_block[0, offset : offset + amount].reshape(tuple([lead_len] + others))
        results.append(jnp.moveaxis(piece, 0, axis_at))
        offset = offset + amount
    return results


def local(
    tokens_in,
    out_grad,
    seq_lengths,
    seq_order,
    routes_top,
    norm_gain,
    in_weight,
    conv_weight,
    conv_bias,
    step_bias,
    decay_log,
    skip_gain,
    gated_gain,
    out_weight,
    ffn_gain,
    router_weight,
    expert_gate_up,
    expert_down,
    shared_gate_up,
    shared_down,
):
    group_count = lax.axis_size("dp")
    my_rank = lax.axis_index("dp")
    slot_rows = lax.broadcasted_iota(jnp.int32, (group_count, group_count), 0)
    slot_cols = lax.broadcasted_iota(jnp.int32, (group_count, group_count), 1)
    picks = (seq_order[None, :] == slot_rows).astype(jnp.int32)
    inverse = jnp.sum(picks * slot_cols, axis=1)
    my_length = jnp.sum(jnp.where(seq_order == my_rank, seq_lengths, 0))
    dealt_in, dealt_grad = (
        lax.all_to_all(
            jnp.take(tokens_in, inverse, axis=0), "dp", split_axis=0, concat_axis=1, tiled=True
        ),
        lax.all_to_all(
            jnp.take(out_grad, inverse, axis=0), "dp", split_axis=0, concat_axis=1, tiled=True
        ),
    )
    seq_count, length, model_width = dealt_in.shape
    row_count = seq_count * length
    top_count = routes_top.shape[2]
    (
        gain_one,
        w_in,
        kernel_low,
        shift_low,
        gated_scale_low,
        w_out,
        gain_two,
        w_router,
        w_shared_up,
        w_shared_down,
    ) = (
        lax.all_gather(to_low(norm_gain), ("dp", "expert"), axis=0, tiled=True),
        lax.all_gather(to_low(in_weight), ("dp", "expert"), axis=0, tiled=True),
        lax.all_gather(to_low(conv_weight), ("dp", "expert"), axis=0, tiled=True),
        lax.all_gather(to_low(conv_bias), ("dp", "expert"), axis=0, tiled=True),
        lax.all_gather(to_low(gated_gain), ("dp", "expert"), axis=0, tiled=True),
        lax.all_gather(to_low(out_weight), ("dp", "expert"), axis=0, tiled=True),
        lax.all_gather(to_low(ffn_gain), ("dp", "expert"), axis=0, tiled=True),
        lax.all_gather(to_low(router_weight), ("dp", "expert"), axis=0, tiled=True),
        lax.all_gather(to_low(shared_gate_up), ("dp", "expert"), axis=0, tiled=True),
        lax.all_gather(to_low(shared_down), ("dp", "expert"), axis=0, tiled=True),
    )
    w_expert_up, w_expert_down = (
        lax.all_gather(to_low(expert_gate_up), "dp", axis=1, tiled=True),
        lax.all_gather(to_low(expert_down), "dp", axis=1, tiled=True),
    )
    flat_in = dealt_in.reshape(row_count, model_width).astype(jnp.float32)
    positions = lax.broadcasted_iota(jnp.int32, (seq_count, length), 1)
    valid_rows = (positions < my_length).astype(jnp.float32).reshape(row_count, 1)
    normed, norm_one_back = jax.vjp(rms_scale, flat_in, gain_one.astype(jnp.float32))
    normed_low = normed.astype(jnp.bfloat16)
    projected = jnp.dot(normed_low, w_in, preferred_element_type=jnp.float32)
    mixer_fn = partial(mixer_local, seq_count=seq_count, block_len=BLK)
    gated_out, mixer_back = jax.vjp(
        mixer_fn,
        projected,
        kernel_low.astype(jnp.float32),
        shift_low.astype(jnp.float32),
        step_bias,
        decay_log,
        skip_gain,
        gated_scale_low.astype(jnp.float32),
    )
    gated_low = gated_out.astype(jnp.bfloat16)
    branch = jnp.dot(gated_low, w_out, preferred_element_type=jnp.float32)
    middle = flat_in + branch
    normed_two, norm_two_back = jax.vjp(rms_scale, middle, gain_two.astype(jnp.float32))
    mid_low = normed_two.astype(jnp.bfloat16)
    logits = jnp.dot(mid_low, w_router, preferred_element_type=jnp.float32)
    routes = routes_top.reshape(row_count, top_count)
    gate_weights = jax.nn.softmax(jnp.take_along_axis(logits, routes, axis=1), axis=-1)
    shared_pre = jnp.dot(mid_low, w_shared_up, preferred_element_type=jnp.float32)
    shared_full, shared_back = jax.vjp(swiglu, shared_pre)
    shared_act = shared_full.astype(jnp.bfloat16)
    shared_out = jnp.dot(shared_act, w_shared_down, preferred_element_type=jnp.float32)
    expert_count = w_router.shape[1]
    rank_count = lax.axis_size("expert")
    local_count = expert_count // rank_count
    capacity = min(row_count, 9 * row_count * top_count // (8 * expert_count))
    pair_count = row_count * top_count
    slot_total = expert_count * capacity
    pair_expert = routes.reshape(pair_count)
    pair_valid = jnp.broadcast_to(valid_rows > 0, (row_count, top_count)).reshape(pair_count)
    expert_ids = lax.broadcasted_iota(jnp.int32, (1, expert_count), 1)
    member = ((pair_expert[:, None] == expert_ids) & pair_valid[:, None]).astype(jnp.int32)
    ordinal = jnp.sum((jnp.cumsum(member, axis=0) - 1) * member, axis=1)
    pair_slot = jnp.where(pair_valid, pair_expert * capacity + ordinal, slot_total)
    slot_pair = (
        jnp.full((slot_total + 1,), pair_count, jnp.int32)
        .at[pair_slot]
        .set(lax.iota(jnp.int32, pair_count))[:slot_total]
    )
    send_rows = jnp.take(pad_row(mid_low), slot_pair // top_count, axis=0).reshape(
        rank_count, local_count, capacity, model_width
    )
    received = lax.all_to_all(send_rows, "expert", split_axis=0, concat_axis=0, tiled=True)
    expert_pre = jnp.einsum(
        "slcd,ldf->slcf", received, w_expert_up, preferred_element_type=jnp.float32
    )
    expert_full, expert_back = jax.vjp(swiglu, expert_pre)
    expert_act = expert_full.astype(jnp.bfloat16)
    expert_res = jnp.einsum(
        "slcf,lfd->slcd", expert_act, w_expert_down, preferred_element_type=jnp.float32
    ).astype(jnp.bfloat16)
    returned = lax.all_to_all(expert_res, "expert", split_axis=0, concat_axis=0, tiled=True)
    pair_out = jnp.take(
        pad_row(returned.reshape(slot_total, model_width)), pair_slot, axis=0
    ).reshape(row_count, top_count, model_width)
    moe_out = jnp.sum(gate_weights[:, :, None] * pair_out.astype(jnp.float32), axis=1)
    block_out = (
        (valid_rows * (middle + moe_out + shared_out))
        .astype(jnp.bfloat16)
        .reshape(seq_count, length, model_width)
    )
    w_in, w_out, w_router, w_shared_up, w_shared_down = (
        lax.all_gather(to_low(in_weight), ("dp", "expert"), axis=0, tiled=True),
        lax.all_gather(to_low(out_weight), ("dp", "expert"), axis=0, tiled=True),
        lax.all_gather(to_low(router_weight), ("dp", "expert"), axis=0, tiled=True),
        lax.all_gather(to_low(shared_gate_up), ("dp", "expert"), axis=0, tiled=True),
        lax.all_gather(to_low(shared_down), ("dp", "expert"), axis=0, tiled=True),
    )
    w_expert_up, w_expert_down = (
        lax.all_gather(to_low(expert_gate_up), "dp", axis=1, tiled=True),
        lax.all_gather(to_low(expert_down), "dp", axis=1, tiled=True),
    )
    row_cot = dealt_grad.reshape(row_count, model_width).astype(jnp.float32) * valid_rows
    pair_cot = (gate_weights[:, :, None] * row_cot[:, None, :]).astype(jnp.bfloat16)
    gate_cot = jnp.sum(row_cot[:, None, :] * pair_out.astype(jnp.float32), axis=2)
    grad_send = jnp.take(
        pad_row(pair_cot.reshape(pair_count, model_width)), slot_pair, axis=0
    ).reshape(rank_count, local_count, capacity, model_width)
    grad_received = lax.all_to_all(grad_send, "expert", split_axis=0, concat_axis=0, tiled=True)
    act_cot = jnp.einsum(
        "slcd,lfd->slcf", grad_received, w_expert_down, preferred_element_type=jnp.float32
    )
    grad_down_local = jnp.einsum(
        "slcf,slcd->lfd", expert_act, grad_received, preferred_element_type=jnp.float32
    )
    pre_cot = expert_back(act_cot)[0].astype(jnp.bfloat16)
    grad_up_local = jnp.einsum(
        "slcd,slcf->ldf", received, pre_cot, preferred_element_type=jnp.float32
    )
    input_cot = jnp.einsum(
        "slcf,ldf->slcd", pre_cot, w_expert_up, preferred_element_type=jnp.float32
    ).astype(jnp.bfloat16)
    input_back = lax.all_to_all(input_cot, "expert", split_axis=0, concat_axis=0, tiled=True)
    expert_members = [(grad_up_local, 1), (grad_down_local, 1)]
    expert_packed = pack_shares(expert_members, group_count)
    expert_row = lax.psum_scatter(
        expert_packed.astype(jnp.bfloat16), "dp", scatter_dimension=0, tiled=True
    ).astype(jnp.float32)
    expert_sums = unpack_share(expert_row, expert_members, group_count)
    mid_cot = jnp.sum(
        jnp.take(pad_row(input_back.reshape(slot_total, model_width)), pair_slot, axis=0)
        .reshape(row_count, top_count, model_width)
        .astype(jnp.float32),
        axis=1,
    )
    chosen_cot = gate_weights * (gate_cot - jnp.sum(gate_weights * gate_cot, axis=1, keepdims=True))
    logit_cot = jnp.sum(
        jnp.where(routes[:, :, None] == expert_ids[None], chosen_cot[:, :, None], 0.0), axis=1
    ).astype(jnp.bfloat16)
    grad_router = dot_left(mid_low, logit_cot)
    shared_cot = row_cot.astype(jnp.bfloat16)
    grad_shared_down = dot_left(shared_act, shared_cot)
    shared_pre_cot = shared_back(dot_right(shared_cot, w_shared_down))[0].astype(jnp.bfloat16)
    grad_shared_up = dot_left(mid_low, shared_pre_cot)
    mid_cot = mid_cot + dot_right(logit_cot, w_router) + dot_right(shared_pre_cot, w_shared_up)
    middle_norm_cot, gain_two_cot = norm_two_back(mid_cot)
    middle_cot = row_cot + middle_norm_cot
    branch_cot = middle_cot.astype(jnp.bfloat16)
    grad_out = dot_left(gated_low, branch_cot)
    proj_cot, kernel_cot, shift_cot, step_cot, decay_cot, skip_cot, gated_gain_cot = mixer_back(
        dot_right(branch_cot, w_out)
    )
    proj_low = proj_cot.astype(jnp.bfloat16)
    grad_in = dot_left(normed_low, proj_low)
    flat_norm_cot, gain_one_cot = norm_one_back(dot_right(proj_low, w_in))
    input_grad = (
        (middle_cot + flat_norm_cot).astype(jnp.bfloat16).reshape(seq_count, length, model_width)
    )
    device_total = lax.axis_size(("dp", "expert"))
    dense_members = [
        (gain_one_cot, 0),
        (grad_in, 0),
        (kernel_cot, 0),
        (shift_cot, 0),
        (gated_gain_cot, 0),
        (grad_out, 0),
        (gain_two_cot, 0),
        (grad_router, 0),
        (grad_shared_up, 0),
        (grad_shared_down, 0),
    ]
    dense_packed = pack_shares(dense_members, device_total)
    dense_row = lax.psum_scatter(dense_packed, ("dp", "expert"), scatter_dimension=0, tiled=True)
    dense_sums = unpack_share(dense_row, dense_members, device_total)
    head_sums = lax.psum((step_cot, decay_cot, skip_cot), ("dp", "expert"))
    back_out, back_grad = (
        lax.all_to_all(block_out, "dp", split_axis=1, concat_axis=0, tiled=True),
        lax.all_to_all(input_grad, "dp", split_axis=1, concat_axis=0, tiled=True),
    )
    final_out = jnp.take(back_out, seq_order, axis=0)
    final_grad = jnp.take(back_grad, seq_order, axis=0)
    return (
        final_out,
        final_grad,
        dense_sums[0],
        dense_sums[1],
        dense_sums[2],
        dense_sums[3],
        head_sums[0],
        head_sums[1],
        head_sums[2],
        dense_sums[4],
        dense_sums[5],
        dense_sums[6],
        dense_sums[7],
        expert_sums[0],
        expert_sums[1],
        dense_sums[8],
        dense_sums[9],
    )


def solution(mesh):
    in_specs = (
        P("expert", "dp", None),
        P("expert", "dp", None),
        P("expert"),
        P("expert"),
        P(("dp", "expert"), None, None),
        P(("dp", "expert")),
        P(("dp", "expert"), None),
        P(("dp", "expert"), None),
        P(("dp", "expert")),
        P(),
        P(),
        P(),
        P(("dp", "expert")),
        P(("dp", "expert"), None),
        P(("dp", "expert")),
        P(("dp", "expert"), None),
        P("expert", "dp", None),
        P("expert", "dp", None),
        P(("dp", "expert"), None),
        P(("dp", "expert"), None),
    )
    out_specs = (
        P("expert", "dp", None),
        P("expert", "dp", None),
        P(("dp", "expert")),
        P(("dp", "expert"), None),
        P(("dp", "expert"), None),
        P(("dp", "expert")),
        P(),
        P(),
        P(),
        P(("dp", "expert")),
        P(("dp", "expert"), None),
        P(("dp", "expert")),
        P(("dp", "expert"), None),
        P("expert", "dp", None),
        P("expert", "dp", None),
        P(("dp", "expert"), None),
        P(("dp", "expert"), None),
    )
    return jax.shard_map(local, mesh=mesh, in_specs=in_specs, out_specs=out_specs, check_vma=False)
```

profile of v0, /device:TPU:0, one launch (start us, length us, event | category | flops | bytes accessed | tf_op | source)
XLA Modules:
  0.0 3493.1 jit_solution(17786981504397929994)
XLA Ops:
  28.6 52.2 %all-reduce.32 = (bf16[1536]{0:T(1024)(128)(2,1)S(1)}, bf16[3328]{0:T(1024)(128)(2,1)S(1)}, bf16[3072]{0:T(1024)(128)(2,1)S(1)}, bf16[1536]{0:T(1024)(128)(2,1)S(1)}) all-reduce(bf16[1536]{0:T(1024)(128)(2,1)S(1)} %dynamic-update-slice.1, bf16[3328]{0:T(1024)(128)(2,1)S(1)} %dynamic-update-slice, ...), channel_id=1, replica_groups=mesh['dp'=2,'expert'=16] {'dp','expert'}, use_global_device_ids=true, to_apply=%add.26 | all-reduce | flops 9472 | bytes 37888
  84.0 41.0 %all-gather = bf16[32,104,4]{1,2,0:T(4,128)(2,1)S(1)} all-gather(bf16[1,104,4]{1,2,0:T(4,128)(2,1)S(1)} %convert_bitcast_fusion.1), channel_id=1, replica_groups=mesh['dp'=2,'expert'=16] {'dp','expert'}, dimensions={0}, use_global_device_ids=true | all-gather | bytes 27456 | tf_op jit(solution)/shard_map/all_gather | solution.py:197
  133.6 12.1 scatter_custom_fusion
  153.5 18.0 fusion.183
  190.7 9.9 fusion.27
  226.2 9.9 fusion.98
  239.6 14.3 while.34
  264.6 28.8 bitcast_add_fusion.6
  310.7 10.2 multiply_reduce_fusion.14
  323.0 12.8 gather_fusion
  355.0 184.9 %all-to-all-done.1 = bf16[16,1,216,1536]{3,2,1,0:T(8,128)(2,1)} async-done(((bf16[16,1,216,1536]{3,2,1,0:T(8,128)(2,1)}), bf16[16,1,216,1536]{3,2,1,0:T(8,128)(2,1)}, u32[]{:S(2)}, u32[]{:S(2)}) %all-to-all-start.1) | async-done | bytes 10616864 | tf_op jit(solution)/shard_map/all_to_all | solution.py:259
  543.6 14.9 fusion.17
  567.0 10.1 fusion.15
  577.2 45.6 %all-to-all-start.2 = ((bf16[16,1,216,1536]{3,2,1,0:T(8,128)(2,1)}), bf16[16,1,216,1536]{3,2,1,0:T(8,128)(2,1)}, u32[]{:S(2)}, u32[]{:S(2)}) async-start(bf16[16,1,216,1536]{3,2,1,0:T(8,128)(2,1)} %fusion.15), calls=%async_computation.2 | async-start | bytes 21233664 | tf_op jit(solution)/shard_map/all_to_all | solution.py:268
  623.6 287.0 %all-gather.1 = bf16[32,48,16]{1,2,0:T(8,128)(2,1)S(1)} all-gather(bf16[1,48,16]{1,2,0:T(8,128)(2,1)S(1)} %convert_bitcast_fusion), channel_id=1, replica_groups=mesh['dp'=2,'expert'=16] {'dp','expert'}, dimensions={0}, use_global_device_ids=true | all-gather | bytes 50688 | tf_op jit(solution)/shard_map/all_gather | solution.py:202
  923.3 22.2 mul.729
  946.0 24.9 gather_fusion.2
  972.2 9.9 concatenate.20
  982.1 24.7 gather_fusion.4
  1006.7 14.5 multiply_convert_fusion
  1029.0 27.1 gather_fusion.1
  1056.2 9.7 broadcast_select_fusion
  1081.3 209.5 %all-gather.19.cloned.1.call-done = bf16[1024,1536]{1,0:T(8,128)(2,1)} async-done(((bf16[32,1536]{1,0:T(8,128)(2,1)}), bf16[1024,1536]{1,0:T(8,128)(2,1)}) %all-gather.19.cloned.1.call-update) | async-done | bytes 3145744 | tf_op jit(solution)/shard_map/all_gather | solution.py:204
  1319.9 10.1 reshape.984
  1342.8 16.7 bitcast_multiply_fusion.4
  1362.3 17.5 bitcast_convert_fusion
  1385.5 9.8 fusion.92
  1396.4 18.1 fusion.16
  1419.4 26.6 pad_maximum_fusion
  1446.1 162.7 %all-to-all-done.6 = bf16[16,1,216,1536]{3,2,1,0:T(8,128)(2,1)} async-done(((bf16[16,1,216,1536]{3,2,1,0:T(8,128)(2,1)}), bf16[16,1,216,1536]{3,2,1,0:T(8,128)(2,1)}, u32[]{:S(2)}, u32[]{:S(2)}) %all-to-all-start.6) | async-done | bytes 10616864 | tf_op jit(solution)/shard_map/all_to_all | solution.py:309
  1608.8 9.8 concatenate.22
  1618.6 24.7 gather_fusion.7
  1643.3 19.2 select_convert_fusion
  1662.5 21.2 reshape.989
  1683.7 14.7 reduce_sum.330
  1705.2 13.9 multiply_reduce_fusion.8
  1719.3 13.5 fusion.40
  1746.8 12.4 fusion.113
  1770.3 17.7 while.35
  1788.0 15.0 fusion.116
  1818.0 11.9 multiply_reduce_fusion.7
  1830.0 32.0 fusion.29
  1862.1 16.1 bitcast_add_fusion.5
  1899.5 21.0 multiply_reduce_fusion.5
  1930.0 11.8 fusion.26
  1941.8 24.7 fusion.85
  1966.5 12.4 fusion.124
  1980.3 21.6 reshape.981
  2002.0 21.8 fusion.173
  2023.7 52.1 %reshape.977 = f32[32,309504]{1,0:T(8,128)} reshape(f32[1536,6448]{1,0:T(8,128)} %fusion.173) | data formatting | bytes 79233024 | tf_op jit(solution)/shard_map/reshape | solution.py:125
  2077.2 106.6 %dynamic-update-slice.5 = f32[32,605896]{1,0:T(8,128)} dynamic-update-slice(f32[32,605896]{1,0:T(8,128)} %dynamic-update-slice.4, f32[32,309504]{1,0:T(8,128)} %reshape.977, s32[]{} %constant.331, s32[]{} %constant.332) | dynamic-update-slice | bytes 79233024
  2188.5 53.7 %dynamic-update-slice.9 = f32[32,605896]{1,0:T(8,128)} dynamic-update-slice(f32[32,605896]{1,0:T(8,128)} %dynamic-update-slice.8, f32[32,147456]{1,0:T(8,128)} %reshape.981, s32[]{} %constant.331, s32[]{} %constant.336) | dynamic-update-slice | bytes 37748740
  2245.5 37.1 %dynamic-update-slice.12 = f32[32,605896]{1,0:T(8,128)} dynamic-update-slice(f32[32,605896]{1,0:T(8,128)} %dynamic-update-slice.11, f32[32,98304]{1,0:T(8,128)} %reshape.984, s32[]{} %constant.331, s32[]{} %constant.339) | dynamic-update-slice | bytes 25165828
  2282.6 19.8 dynamic-update-slice.13
  2309.3 21.3 reshape.987
  2330.6 33.4 multiply_reduce_fusion
  2370.6 11.5 reduce.70
  2395.9 11.7 reduce.69
  2409.7 12.1 all-to-all-done.3
  2426.4 35.2 %slice_reduce_fusion = f32[786432]{0:T(1024)} fusion(f32[1,1179648]{1,0:T(1,128)} %dynamic-slice_convert_fusion), kind=kLoop, calls=%fused_computation.157 | loop fusion | bytes 6291456 | tf_op jit(solution)/shard_map/slice | solution.py:137
  2466.2 17.3 slice_reduce_fusion.1
  2485.1 78.4 %all-reduce.31 = (f32[48]{0:T(128)}, f32[48]{0:T(128)}, f32[48]{0:T(128)}) all-reduce(f32[48]{0:T(128)S(1)} %copy-done.129, f32[48]{0:T(128)S(1)} %negate_multiply_fusion, f32[48]{0:T(128)S(1)} %reduce_sum.375), channel_id=1, replica_groups=mesh['dp'=2,'expert'=16] {'dp','expert'}, use_global_device_ids=true, to_apply=%region_42.45 | all-reduce | flops 144 | bytes 1152 | tf_op jit(solution)/shard_map/psum | solution.py:361
  2583.0 863.3 %all-reduce.36.cloned.1.call-done = f32[32,605896]{1,0:T(8,128)} async-done(((f32[32,605896]{1,0:T(8,128)}), f32[32,605896]{1,0:T(8,128)}) %all-reduce.36.cloned.1.call-update) | async-done | bytes 77554704
  3464.9 15.0 dynamic-slice_reduce_fusion
  (608 shorter events, 447.3 us)
Async XLA Ops:
  8.0 145.4 %all-gather.9.cloned.1.call-start = ((), (), s32[]{:S(2)}) async-start(), calls=%async_computation.8 | async-start | bytes 20680704 | tf_op jit(solution)/shard_map/all_gather | solution.py:196
  14.0 69.2 %copy-start.132 = (f32[48]{0:T(128)S(1)}, f32[48]{0:T(128)}, u32[]{:S(2)}) copy-start(f32[48]{0:T(128)} %param.39) | copy-start | bytes 580
  14.0 69.9 %copy-start.127 = (f32[104,4]{0,1:T(4,128)S(1)}, f32[104,4]{0,1:T(4,128)}, u32[]{:S(2)}) copy-start(f32[104,4]{0,1:T(4,128)} %param.35) | copy-start | bytes 4996
  16.1 134.7 %all-to-all-start = ((bf16[2,256,1536]{2,1,0:T(8,128)(2,1)}), bf16[2,256,1536]{2,1,0:T(8,128)(2,1)S(1)}, u32[]{:S(2)}, u32[]{:S(2)}) async-start(bf16[2,256,1536]{2,1,0:T(8,128)(2,1)} %get-tuple-element.504), calls=%async_computation | async-start | bytes 3145728 | tf_op jit(solution)/shard_map/all_to_all | solution.py:173
  20.3 290.3 %all-gather.11.cloned.1.call-start = ((), (), s32[]{:S(2)}) async-start(), calls=%async_computation.9 | async-start | bytes 9732096 | tf_op jit(solution)/shard_map/all_gather | solution.py:200
  24.3 147.2 %copy-start.93 = (pred[3072]{0:T(1024)(128)(4,1)}, pred[3072]{0:T(1024)(128)(4,1)S(1)}, u32[]{:S(2)}) copy-start(pred[3072]{0:T(1024)(128)(4,1)S(1)} %and.64) | copy-start | bytes 9220
  26.8 144.7 %copy-start.52 = (s32[3072]{0:T(1024)}, s32[3072]{0:T(1024)S(1)}, u32[]{:S(2)}) copy-start(s32[3072]{0:T(1024)S(1)} %eq.64) | copy-start | bytes 36868
  132.9 38.6 %copy-start.65 = (s32[3072]{0:T(1024)}, s32[3072]{0:T(1024)S(1)}, u32[]{:S(2)}) copy-start(s32[3072]{0:T(1024)S(1)} %fusion.143) | copy-start | bytes 36868
  148.9 36.5 %copy-start.69 = (f32[3328]{0:T(1024)}, f32[3328]{0:T(1024)S(1)}, u32[]{:S(2)}) copy-start(f32[3328]{0:T(1024)S(1)} %get-tuple-element.421) | copy-start | bytes 39940
  148.9 36.5 %copy-start.71 = (f32[3328]{0:T(1024)}, f32[3328]{0:T(1024)S(1)}, u32[]{:S(2)}) copy-start(f32[3328]{0:T(1024)S(1)} %get-tuple-element.422) | copy-start | bytes 39940
  150.7 159.9 %copy-start.15 = (bf16[2,256,1536]{2,1,0:T(8,128)(2,1)}, bf16[2,256,1536]{2,1,0:T(8,128)(2,1)S(1)}, u32[]{:S(2)}) copy-start(bf16[2,256,1536]{2,1,0:T(8,128)(2,1)S(1)} %all-to-all-done) | copy-start | bytes 4718596
  151.1 20.4 copy-start.108
  151.2 20.3 copy-start.110
  153.5 18.0 copy-start.121
  181.4 44.8 %copy-start.44 = (f32[4,128,48]{1,2,0:T(8,128)}, f32[4,128,48]{1,2,0:T(8,128)S(1)}, u32[]{:S(2)}) copy-start(f32[4,128,48]{1,2,0:T(8,128)S(1)} %copy.314) | copy-start | bytes 294916
  254.0 48.0 %slice-start = ((s8[6815744]{0:T(1024)(128)(4,1)}), s8[4194304]{0:T(1024)(128)(4,1)S(1)}, s32[]{:S(2)}) async-start(s8[6815744]{0:T(1024)(128)(4,1)} %bitcast.429), calls=%async_computation.16 | async-start | bytes 8388608
  264.6 37.4 %slice-start.1 = ((s8[6815744]{0:T(1024)(128)(4,1)}), s8[2621440]{0:T(1024)(128)(4,1)S(1)}, s32[]{:S(2)}) async-start(s8[6815744]{0:T(1024)(128)(4,1)} %bitcast.429), calls=%async_computation.17 | async-start | bytes 5242880
  345.4 194.5 %all-to-all-start.1 = ((bf16[16,1,216,1536]{3,2,1,0:T(8,128)(2,1)}), bf16[16,1,216,1536]{3,2,1,0:T(8,128)(2,1)}, u32[]{:S(2)}, u32[]{:S(2)}) async-start(bf16[16,1,216,1536]{3,2,1,0:T(8,128)(2,1)} %broadcast_select_fusion.1), calls=%async_computation.1 | async-start | bytes 21233664 | tf_op jit(solution)/shard_map/all_to_all | solution.py:259
  350.5 193.1 %all-gather.13.cloned.1.call-start = ((), (), s32[]{:S(2)}) async-start(), calls=%async_computation.10 | async-start | bytes 4718592 | tf_op jit(solution)/shard_map/all_gather | solution.py:207
  354.0 213.0 %all-gather.15.cloned.1.call-start = ((), (), s32[]{:S(2)}) async-start(), calls=%async_computation.11 | async-start | bytes 2359296 | tf_op jit(solution)/shard_map/all_gather | solution.py:208
  539.9 37.3 %all-to-all-start.4 = ((bf16[2,256,1536]{2,1,0:T(8,128)(2,1)}), bf16[2,256,1536]{2,1,0:T(8,128)(2,1)S(1)}, u32[]{:S(2)}, u32[]{:S(2)}) async-start(bf16[2,256,1536]{2,1,0:T(8,128)(2,1)} %get-tuple-element.503), calls=%async_computation.4 | async-start | bytes 3145728 | tf_op jit(solution)/shard_map/all_to_all | solution.py:176
  577.1 45.7 %copy-start.50 = (f32[48,2048]{1,0:T(8,128)S(1)}, f32[48,2048]{1,0:T(8,128)}, u32[]{:S(2)}) copy-start(f32[48,2048]{1,0:T(8,128)} %param.46) | copy-start | bytes 1179652
  577.1 46.5 %copy-start.120 = (f32[48,16]{0,1:T(8,128)S(1)}, f32[48,16]{0,1:T(8,128)}, u32[]{:S(2)}) copy-start(f32[48,16]{0,1:T(8,128)} %param.43) | copy-start | bytes 9220
  577.1 333.7 %copy-start.62 = (s32[1,512,6]{1,0,2:T(1,128)S(1)}, s32[1,512,6]{1,0,2:T(1,128)}, u32[]{:S(2)}) copy-start(s32[1,512,6]{1,0,2:T(1,128)} %param.32) | copy-start | bytes 36868
  577.1 334.8 %copy-start.53 = (s32[3072]{0:T(1024)S(1)}, s32[3072]{0:T(1024)}, u32[]{:S(2)}) copy-start(s32[3072]{0:T(1024)} %copy-done.52) | copy-start | bytes 36868
  577.1 334.8 %copy-start.66 = (s32[3072]{0:T(1024)S(1)}, s32[3072]{0:T(1024)}, u32[]{:S(2)}) copy-start(s32[3072]{0:T(1024)} %copy-done.65) | copy-start | bytes 36868
  577.1 334.8 %copy-start.94 = (pred[3072]{0:T(1024)(128)(4,1)S(1)}, pred[3072]{0:T(1024)(128)(4,1)}, u32[]{:S(2)}) copy-start(pred[3072]{0:T(1024)(128)(4,1)} %copy-done.93) | copy-start | bytes 9220
  577.2 334.8 %copy-start.21 = (bf16[2,256,1536]{2,1,0:T(8,128)(2,1)}, bf16[2,256,1536]{2,1,0:T(8,128)(2,1)S(1)}, u32[]{:S(2)}) copy-start(bf16[2,256,1536]{2,1,0:T(8,128)(2,1)S(1)} %all-to-all-done.4) | copy-start | bytes 4718596
  577.2 395.0 %all-to-all-start.2 = ((bf16[16,1,216,1536]{3,2,1,0:T(8,128)(2,1)}), bf16[16,1,216,1536]{3,2,1,0:T(8,128)(2,1)}, u32[]{:S(2)}, u32[]{:S(2)}) async-start(bf16[16,1,216,1536]{3,2,1,0:T(8,128)(2,1)} %fusion.15), calls=%async_computation.2 | async-start | bytes 21233664 | tf_op jit(solution)/shard_map/all_to_all | solution.py:268
  622.8 450.8 %all-gather.17.cloned.1.call-start = ((), (), s32[]{:S(2)}) async-start(), calls=%async_computation.12 | async-start | bytes 6488064 | tf_op jit(solution)/shard_map/all_gather | solution.py:203
  910.8 34.6 copy-start.48
  911.9 94.8 %copy-start.101 = (pred[3072]{0:T(1024)(128)(4,1)}, pred[3072]{0:T(1024)(128)(4,1)S(1)}, u32[]{:S(2)}) copy-start(pred[3072]{0:T(1024)(128)(4,1)S(1)} %compare_and_fusion.2) | copy-start | bytes 9220
  912.0 70.1 %copy-start.79 = (s32[3072]{0:T(1024)}, s32[3072]{0:T(1024)S(1)}, u32[]{:S(2)}) copy-start(s32[3072]{0:T(1024)S(1)} %broadcast_clamp_fusion) | copy-start | bytes 36868
  923.3 22.2 copy-start.19
  946.0 25.2 copy-start.27
  1029.0 27.1 copy-start.113
  1065.9 276.9 %all-to-all-start.5 = ((bf16[16,1,216,1536]{3,2,1,0:T(8,128)(2,1)}), bf16[16,1,216,1536]{3,2,1,0:T(8,128)(2,1)}, u32[]{:S(2)}, u32[]{:S(2)}) async-start(bf16[16,1,216,1536]{3,2,1,0:T(8,128)(2,1)} %broadcast_select_fusion), calls=%async_computation.5 | async-start | bytes 21233664 | tf_op jit(solution)/shard_map/all_to_all | solution.py:295
  1070.9 219.9 %all-gather.19.cloned.1.call-start = ((), (), s32[]{:S(2)}) async-start(), calls=%async_computation.13 | async-start | bytes 3244032 | tf_op jit(solution)/shard_map/all_gather | solution.py:204
  1414.5 194.3 %all-to-all-start.6 = ((bf16[16,1,216,1536]{3,2,1,0:T(8,128)(2,1)}), bf16[16,1,216,1536]{3,2,1,0:T(8,128)(2,1)}, u32[]{:S(2)}, u32[]{:S(2)}) async-start(bf16[16,1,216,1536]{3,2,1,0:T(8,128)(2,1)} %fusion.16), calls=%async_computation.6 | async-start | bytes 21233664 | tf_op jit(solution)/shard_map/all_to_all | solution.py:309
  1419.4 883.1 %all-reduce.38.cloned.1.call-start = ((), (), s32[]{:S(2)}) async-start(), calls=%async_computation.15 | async-start | bytes 9437184
  1446.0 2000.3 %all-reduce.36.cloned.1.call-start = ((), (), s32[]{:S(2)}) async-start(), calls=%async_computation.14 | async-start | bytes 155123712
  1618.6 24.7 copy-start.102
  1818.0 44.0 %slice-start.10 = ((s8[6291456]{0:T(1024)(128)(4,1)}), s8[2097152]{0:T(1024)(128)(4,1)S(1)}, s32[]{:S(2)}) async-start(s8[6291456]{0:T(1024)(128)(4,1)} %bitcast.443), calls=%async_computation.26 | async-start | bytes 4194304
  1830.0 32.1 slice-start.11
  1899.5 21.1 copy-start.70
  1899.5 21.1 copy-start.72
  1899.5 21.1 copy-start.74
  1899.5 21.1 copy-start.76
  1941.8 24.7 copy-start.58
  1941.8 24.7 copy-start.100
  1980.3 21.7 copy-start.43
  2188.5 55.2 %copy-start.51 = (f32[32,768]{1,0:T(8,128)S(1)}, f32[32,768]{1,0:T(8,128)}, u32[]{:S(2)}) copy-start(f32[32,768]{1,0:T(8,128)} %reshape.983) | copy-start | bytes 294916
  2309.3 21.3 copy-start.34
  2330.6 33.4 copy-start.13
  2330.6 33.5 copy-start.41
  2330.6 33.5 copy-start.105
  2330.6 33.5 copy-start.135
  2384.2 37.6 %all-to-all-start.3 = ((bf16[2,2,196608]{2,1,0:T(2,128)(2,1)}), bf16[2,2,196608]{2,1,0:T(2,128)(2,1)S(1)}, u32[]{:S(2)}, u32[]{:S(2)}) async-start(bf16[2,2,196608]{2,1,0:T(2,128)(2,1)} %reshape.1157), calls=%async_computation.3 | async-start | bytes 3145728 | tf_op jit(solution)/shard_map/all_to_all | solution.py:363
  2421.8 146.5 %all-to-all-start.7 = ((bf16[2,2,196608]{2,1,0:T(2,128)(2,1)}), bf16[2,2,196608]{2,1,0:T(2,128)(2,1)}, u32[]{:S(2)}, u32[]{:S(2)}) async-start(bf16[2,2,196608]{2,1,0:T(2,128)(2,1)} %reshape.1159), calls=%async_computation.7 | async-start | bytes 3145728 | tf_op jit(solution)/shard_map/all_to_all | solution.py:364
  2461.6 23.3 copy-start.92
  2461.6 23.5 copy-start.130
  2461.6 23.5 copy-start.140
  2461.6 23.5 copy-start.129
  2579.5 906.1 %copy-start.1 = (bf16[2,256,1536]{2,1,0:T(8,128)(2,1)S(1)}, bf16[2,256,1536]{2,1,0:T(8,128)(2,1)}, u32[]{:S(2)}) copy-start(bf16[2,256,1536]{2,1,0:T(8,128)(2,1)} %param.29) | copy-start | bytes 4718596
  (107 other events, 1064.5 us)
Sparse Core Ops, SparseCore 0:
  12.3 136.4 all-gather.8
  152.3 80.0 all-gather.10
  627.1 230.9 all-gather.16
  1074.9 215.8 all-gather.18
Sparse Core Ops, SparseCore 1:
  354.1 45.9 all-gather.12
  402.0 27.0 all-gather.14
  1446.1 120.3 all-reduce.37
  2302.5 1143.8 all-reduce.35
where the time goes:
time: 3510 us; the launch traced here: 3490 us
  waiting for transfers between devices  1430 us (41%)
  local copies, waits for them, and re-layouts  791 us (23%)
  blocking collectives  459 us (13%)
  matrix products  376 us (11%)
  other arithmetic  339 us (10%)
  starting transfers between devices  77.2 us (2%)
    unnamed x10, waiting for transfers between devices  863 us
    all_gather x1, blocking collectives, local(): lax.all_gather(to_low(router_weight), ('dp', 'expert'), axis=0, tiled=True)  287 us
    unnamed x340, local copies, waits for them, and re-layouts  251 us
    all_gather x1, waiting for transfers between devices, local(): lax.all_gather(to_low(shared_down), ('dp', 'expert'), axis=0, tiled=True)  209 us
    all_to_all x1, waiting for transfers between devices, local(): lax.all_to_all(send_rows, 'expert', split_axis=0, concat_axis=0, tiled=True)  185 us
    all_to_all x1, waiting for transfers between devices, local(): lax.all_to_all(input_cot, 'expert', split_axis=0, concat_axis=0, tiled=True)  163 us
    reshape x10, local copies, waits for them, and re-layouts, pack_shares(): jnp.moveaxis(matrix, axis_at, 0).reshape(shares, -1)  91.7 us
    slice x8, local copies, waits for them, and re-layouts, unpack_share(): row_block[0, offset:offset + amount].reshape(tuple([lead_len] + others))  82.1 us
  transfers between devices with their start and end apart: 16, of which 5 were waited for; matrix products, arithmetic and copies ran while one was open for 38% of the time, Pallas kernels for 0%

commit v1 on v0

v1 whole, which is shorter than its diff:
```python
from functools import partial
import math

import jax
import jax.numpy as jnp
from jax import lax
from jax.sharding import Mesh, PartitionSpec as P

BLK = 128
EPSILON = 1e-05
FULL_PRECISION = lax.Precision.HIGHEST
SPLIT = ("e3", "e2", "e1", "e0")
EVERY = ("dp",) + SPLIT
GROUP = SPLIT[1:]
HOLDERS = ("e3", "dp")


def rms_scale(values, gain_row):
    return (
        values * lax.rsqrt(jnp.mean(values * values, axis=-1, keepdims=True) + EPSILON) * gain_row
    )


def swiglu(pre_act):
    half_width = pre_act.shape[-1] // 2
    return jax.nn.silu(pre_act[..., :half_width]) * pre_act[..., half_width:]


def ssd_blocks(head_inputs, step_sizes, decay_rates, state_in, state_out, block_len):
    seq_count, length, head_count, head_width = head_inputs.shape
    blocks = length // block_len
    head_inputs = head_inputs.reshape(seq_count, blocks, block_len, head_count, head_width)
    step_sizes = step_sizes.reshape(seq_count, blocks, block_len, head_count)
    state_in = state_in.reshape(seq_count, blocks, block_len, -1)
    state_out = state_out.reshape(seq_count, blocks, block_len, -1)
    log_decay = step_sizes * -jnp.exp(decay_rates)
    running = jnp.cumsum(log_decay, axis=2)
    spread = running[:, :, :, None, :] - running[:, :, None, :, :]
    causal = (
        lax.broadcasted_iota(jnp.int32, (block_len, block_len), 0)
        >= lax.broadcasted_iota(jnp.int32, (block_len, block_len), 1)
    )[None, None, :, :, None]
    decay_mat = jnp.where(causal, jnp.exp(jnp.where(causal, spread, 0.0)), 0.0)
    scores = jnp.einsum("sktn,skjn->sktj", state_out, state_in, precision=FULL_PRECISION)
    mixing = scores[..., None] * decay_mat * step_sizes[:, :, None, :, :]
    inside = jnp.einsum("sktjh,skjhp->skthp", mixing, head_inputs, precision=FULL_PRECISION)
    tail_decay = jnp.exp(running[:, :, -1:, :] - running) * step_sizes
    states = jnp.einsum(
        "skjh,skjhp,skjn->skhpn", tail_decay, head_inputs, state_in, precision=FULL_PRECISION
    )
    totals = jnp.exp(running[:, :, -1, :])

    def carry_step(previous, carried):
        block_state, factor = carried
        return (previous * factor[:, :, None, None] + block_state, previous)

    initial = jnp.zeros((seq_count, head_count, head_width, state_in.shape[-1]), jnp.float32)
    _, before = lax.scan(
        carry_step, initial, (jnp.moveaxis(states, 1, 0), jnp.moveaxis(totals, 1, 0))
    )
    before = jnp.moveaxis(before, 0, 1)
    across = (
        jnp.einsum("sktn,skhpn->skthp", state_out, before, precision=FULL_PRECISION)
        * jnp.exp(running)[..., None]
    )
    return (inside + across).reshape(seq_count, length, head_count, head_width)


def mixer_local(
    projected,
    conv_kernel,
    conv_shift,
    step_shift,
    decay_rates,
    skip_weights,
    gated_scale,
    seq_count,
    block_len,
):
    inner_width = gated_scale.shape[0]
    head_count = decay_rates.shape[0]
    total_rows, proj_width = projected.shape
    length = total_rows // seq_count
    gate_part = projected[:, :inner_width]
    conv_input = projected[:, inner_width : proj_width - head_count].reshape(seq_count, length, -1)
    step_raw = projected[:, proj_width - head_count :]
    kernel_len = conv_kernel.shape[1]
    padded = jnp.pad(conv_input, ((0, 0), (kernel_len - 1, 0), (0, 0)))
    convolved = conv_shift
    for offset in range(kernel_len):
        convolved = convolved + conv_kernel[:, offset] * padded[:, offset : offset + length]
    convolved = jax.nn.silu(convolved)
    state_width = (convolved.shape[-1] - inner_width) // 2
    head_inputs = convolved[..., :inner_width].reshape(
        seq_count, length, head_count, inner_width // head_count
    )
    state_in = convolved[..., inner_width : inner_width + state_width]
    state_out = convolved[..., inner_width + state_width :]
    step_sizes = jax.nn.softplus(step_raw + step_shift).reshape(seq_count, length, head_count)
    scanned = ssd_blocks(head_inputs, step_sizes, decay_rates, state_in, state_out, block_len)
    scanned = scanned + skip_weights[:, None] * head_inputs
    gated_in = scanned.reshape(total_rows, inner_width) * jax.nn.silu(gate_part)
    return rms_scale(gated_in, gated_scale)


def dot_right(left_mat, right_mat):
    return lax.dot_general(
        left_mat, right_mat, (((1,), (1,)), ((), ())), preferred_element_type=jnp.float32
    )


def dot_left(left_mat, right_mat):
    return lax.dot_general(
        left_mat, right_mat, (((0,), (0,)), ((), ())), preferred_element_type=jnp.float32
    )


def to_low(weight):
    return weight.astype(jnp.bfloat16)


def gather_rows(block, axes):
    return lax.all_gather(block, axes, axis=0, tiled=True)


def scatter_rows(block, axes):
    return lax.psum_scatter(block, axes, scatter_dimension=0, tiled=True)


def dot(left_mat, right_mat):
    return jnp.dot(left_mat, right_mat, preferred_element_type=jnp.float32)


def local(
    tokens_in,
    out_grad,
    seq_lengths,
    seq_order,
    routes_top,
    norm_gain,
    in_weight,
    conv_weight,
    conv_bias,
    step_bias,
    decay_log,
    skip_gain,
    gated_gain,
    out_weight,
    ffn_gain,
    router_weight,
    expert_gate_up,
    expert_down,
    shared_gate_up,
    shared_down,
):
    group_count = lax.axis_size("dp")
    my_rank = lax.axis_index("dp")
    peers = lax.axis_size(GROUP)
    halves = lax.axis_size("e3")
    device_total = lax.axis_size(EVERY)

    small = [norm_gain, conv_weight, conv_bias, gated_gain, ffn_gain, router_weight]
    small_flat = jnp.concatenate([to_low(v).reshape(1, -1) for v in small], axis=1)
    small_all = gather_rows(small_flat, EVERY)
    smalls = []
    offset = 0
    for v in small:
        smalls.append(
            small_all[:, offset : offset + v.size].reshape((device_total * v.shape[0],) + v.shape[1:])
        )
        offset += v.size
    gain_one, kernel_low, shift_low, gated_scale_low, gain_two, w_router = smalls

    slot_rows = lax.broadcasted_iota(jnp.int32, (group_count, group_count), 0)
    slot_cols = lax.broadcasted_iota(jnp.int32, (group_count, group_count), 1)
    picks = (seq_order[None, :] == slot_rows).astype(jnp.int32)
    inverse = jnp.sum(picks * slot_cols, axis=1)
    my_length = jnp.sum(jnp.where(seq_order == my_rank, seq_lengths, 0))
    dealt_in, dealt_grad = (
        lax.all_to_all(
            jnp.take(tokens_in, inverse, axis=0), "dp", split_axis=0, concat_axis=1, tiled=True
        ),
        lax.all_to_all(
            jnp.take(out_grad, inverse, axis=0), "dp", split_axis=0, concat_axis=1, tiled=True
        ),
    )
    seq_count, length, model_width = dealt_in.shape
    row_count = seq_count * length
    top_count = routes_top.shape[2]
    expert_count = w_router.shape[1]
    positions = lax.broadcasted_iota(jnp.int32, (row_count, 1), 0)
    valid = positions < my_length
    valid_rows = valid.astype(jnp.float32)
    cot_low = jnp.where(valid, dealt_grad.reshape(row_count, model_width), 0)
    row_cot = cot_low.astype(jnp.float32)

    w_in = gather_rows(to_low(in_weight), EVERY)

    routes = routes_top.reshape(row_count, top_count)
    expert_ids = lax.broadcasted_iota(jnp.int32, (1, expert_count), 1)
    chosen = jnp.any(routes[:, :, None] == expert_ids[:, None, :], axis=1)
    routes_all = gather_rows(jnp.where(valid, routes, -1), GROUP).reshape(
        peers, row_count, top_count
    )
    my_place = lax.axis_index(GROUP)
    mine = my_place + peers * lax.broadcasted_iota(jnp.int32, (1, halves, 1, 1), 1)
    member = jnp.any(routes_all[:, None] == mine, axis=3)
    order = (
        jnp.sum(
            (
                member[:, :, None, :]
                & (
                    lax.broadcasted_iota(jnp.int32, (row_count, row_count), 0)
                    >= lax.broadcasted_iota(jnp.int32, (row_count, row_count), 1)
                )
            ).astype(jnp.float32),
            axis=3,
        ).astype(jnp.int32)
        - 1
    )
    capacity = min(row_count, 9 * row_count * top_count // (8 * expert_count))
    capacity = -(-capacity // 32) * 32
    slot_of = jnp.where(member, order, -1)
    slot_ids = lax.broadcasted_iota(jnp.int32, (1, 1, capacity, 1), 2)
    select = (slot_of[:, :, None, :] == slot_ids).astype(jnp.bfloat16)

    cot_all = gather_rows(cot_low, GROUP).reshape(peers, row_count, model_width)

    w_out = gather_rows(to_low(out_weight), EVERY)
    w_shared_up = gather_rows(to_low(shared_gate_up), EVERY)
    w_shared_down = gather_rows(to_low(shared_down), EVERY)
    w_expert_up = gather_rows(to_low(expert_gate_up), HOLDERS)
    w_expert_up = w_expert_up.reshape(halves, model_width, w_expert_up.shape[2])
    w_expert_down = gather_rows(to_low(expert_down), HOLDERS)
    w_expert_down = w_expert_down.reshape(halves, -1, model_width)

    flat_in = dealt_in.reshape(row_count, model_width).astype(jnp.float32)
    normed, norm_one_back = jax.vjp(rms_scale, flat_in, gain_one.astype(jnp.float32))
    normed_low = normed.astype(jnp.bfloat16)
    projected = dot(normed_low, w_in)
    mixer_fn = partial(mixer_local, seq_count=seq_count, block_len=BLK)
    gated_out, mixer_back = jax.vjp(
        mixer_fn,
        projected,
        kernel_low.astype(jnp.float32),
        shift_low.astype(jnp.float32),
        step_bias,
        decay_log,
        skip_gain,
        gated_scale_low.astype(jnp.float32),
    )
    gated_low = gated_out.astype(jnp.bfloat16)
    middle = flat_in + dot(gated_low, w_out)
    normed_two, norm_two_back = jax.vjp(rms_scale, middle, gain_two.astype(jnp.float32))
    mid_low = normed_two.astype(jnp.bfloat16)

    rows_all = gather_rows(mid_low, GROUP).reshape(peers, row_count, model_width)
    logits = dot(mid_low, w_router)
    masked = jnp.where(chosen, logits, -jnp.inf)
    lifted = jnp.where(chosen, jnp.exp(masked - jnp.max(masked, axis=1, keepdims=True)), 0.0)
    gates = lifted / jnp.sum(lifted, axis=1, keepdims=True)
    gates_all = gather_rows(gates, GROUP).reshape(peers, row_count, expert_count)
    gates_mine = jnp.sum(
        jnp.where(
            lax.broadcasted_iota(jnp.int32, (1, halves, 1, expert_count), 3) == mine,
            gates_all[:, None],
            0.0,
        ),
        axis=3,
    )
    slot_gate = jnp.sum(jnp.where(slot_of[:, :, None, :] == slot_ids, gates_mine[:, :, None, :], 0.0), axis=3)

    def pick(rows):
        return jnp.einsum(
            "sect,std->escd", select, rows, preferred_element_type=jnp.float32
        ).astype(jnp.bfloat16)

    def place(slots):
        return (
            jnp.einsum("sect,escd->std", select, slots, preferred_element_type=jnp.float32)
            .astype(jnp.bfloat16)
            .reshape(peers * row_count, model_width)
        )

    slot_gate = jnp.moveaxis(slot_gate, 1, 0)[..., None]
    expert_in = pick(rows_all)
    expert_pre = jnp.einsum(
        "escd,edf->escf", expert_in, w_expert_up, preferred_element_type=jnp.float32
    )
    expert_full, expert_back = jax.vjp(swiglu, expert_pre)
    expert_act = expert_full.astype(jnp.bfloat16)
    expert_res = jnp.einsum(
        "escf,efd->escd", expert_act, w_expert_down, preferred_element_type=jnp.float32
    ).astype(jnp.bfloat16)
    expert_cot = pick(cot_all).astype(jnp.float32)
    slot_cot = (slot_gate * expert_cot).astype(jnp.bfloat16)
    slot_gate_cot = jnp.sum(expert_cot * expert_res.astype(jnp.float32), axis=3)
    gate_cot_rows = jnp.sum(
        jnp.where(
            slot_of[:, :, None, :] == slot_ids, jnp.moveaxis(slot_gate_cot, 0, 1)[..., None], 0.0
        ),
        axis=2,
    )
    act_cot = jnp.einsum(
        "escd,efd->escf", slot_cot, w_expert_down, preferred_element_type=jnp.float32
    )
    pre_cot = expert_back(act_cot)[0].astype(jnp.bfloat16)
    input_cot = jnp.einsum(
        "escf,edf->escd", pre_cot, w_expert_up, preferred_element_type=jnp.float32
    ).astype(jnp.bfloat16)
    rows_back = scatter_rows(place(input_cot), GROUP)
    gate_cot_back = lax.all_to_all(gate_cot_rows, GROUP, split_axis=0, concat_axis=0, tiled=True)
    gate_cot = jnp.moveaxis(gate_cot_back, 2, 0)
    gate_cot = jnp.moveaxis(gate_cot, 2, 1).reshape(row_count, expert_count)
    moe_out = scatter_rows(
        place((slot_gate * expert_res.astype(jnp.float32)).astype(jnp.bfloat16)), GROUP
    ).astype(jnp.float32)
    grad_down_local = jnp.einsum(
        "escf,escd->efd", expert_act, slot_cot, preferred_element_type=jnp.float32
    ).astype(jnp.bfloat16)
    grad_up_local = jnp.einsum(
        "escd,escf->edf", expert_in, pre_cot, preferred_element_type=jnp.float32
    ).astype(jnp.bfloat16)
    grad_expert_up = scatter_rows(
        grad_up_local.reshape((-1,) + expert_gate_up.shape[1:]), HOLDERS
    ).astype(jnp.float32)
    grad_expert_down = scatter_rows(
        grad_down_local.reshape((-1,) + expert_down.shape[1:]), HOLDERS
    ).astype(jnp.float32)

    shared_pre = dot(mid_low, w_shared_up)
    shared_full, shared_back = jax.vjp(swiglu, shared_pre)
    shared_act = shared_full.astype(jnp.bfloat16)
    shared_out = dot(shared_act, w_shared_down)
    grad_shared_down = dot_left(shared_act, cot_low).astype(jnp.bfloat16)
    shared_pre_cot = shared_back(dot_right(cot_low, w_shared_down))[0].astype(jnp.bfloat16)
    grad_shared_up = dot_left(mid_low, shared_pre_cot).astype(jnp.bfloat16)
    shared_in_cot = dot_right(shared_pre_cot, w_shared_up)
    sum_shared_down = scatter_rows(grad_shared_down, EVERY).astype(jnp.float32)
    sum_shared_up = scatter_rows(grad_shared_up, EVERY).astype(jnp.float32)

    logit_cot = (gates * (gate_cot - jnp.sum(gates * gate_cot, axis=1, keepdims=True))).astype(
        jnp.bfloat16
    )
    grad_router = dot_left(mid_low, logit_cot)
    mid_cot = rows_back.astype(jnp.float32) + dot_right(logit_cot, w_router) + shared_in_cot
    middle_norm_cot, gain_two_cot = norm_two_back(mid_cot)
    middle_cot = row_cot + middle_norm_cot
    branch_cot = middle_cot.astype(jnp.bfloat16)
    block_out = (
        (valid_rows * (middle + moe_out + shared_out))
        .astype(jnp.bfloat16)
        .reshape(seq_count, length, model_width)
    )
    back_out = lax.all_to_all(block_out, "dp", split_axis=1, concat_axis=0, tiled=True)
    grad_out = dot_left(gated_low, branch_cot).astype(jnp.bfloat16)
    sum_out = scatter_rows(grad_out, EVERY).astype(jnp.float32)
    proj_cot, kernel_cot, shift_cot, step_cot, decay_cot, skip_cot, gated_gain_cot = mixer_back(
        dot_right(branch_cot, w_out)
    )
    proj_low = proj_cot.astype(jnp.bfloat16)
    grad_in = dot_left(normed_low, proj_low).astype(jnp.bfloat16)
    sum_in = scatter_rows(grad_in, EVERY).astype(jnp.float32)
    flat_norm_cot, gain_one_cot = norm_one_back(dot_right(proj_low, w_in))
    input_grad = (
        (middle_cot + flat_norm_cot).astype(jnp.bfloat16).reshape(seq_count, length, model_width)
    )
    back_grad = lax.all_to_all(input_grad, "dp", split_axis=1, concat_axis=0, tiled=True)

    heads = jnp.concatenate([step_cot, decay_cot, skip_cot])
    small_cots = [gain_one_cot, kernel_cot, shift_cot, gated_gain_cot, gain_two_cot, grad_router]
    shares = [v.reshape(device_total, -1) for v in small_cots]
    shares.append(jnp.broadcast_to(heads[None], (device_total, heads.shape[0])))
    small_sum = scatter_rows(jnp.concatenate(shares, axis=1), EVERY)[0]
    sums = []
    offset = 0
    for v in small:
        sums.append(small_sum[offset : offset + v.size].reshape(v.shape))
        offset += v.size
    head_count = step_bias.shape[0]
    head_sums = small_sum[offset:].reshape(3, head_count)
    final_out = jnp.take(back_out, seq_order, axis=0)
    final_grad = jnp.take(back_grad, seq_order, axis=0)
    return (
        final_out,
        final_grad,
        sums[0],
        sum_in,
        sums[1],
        sums[2],
        head_sums[0],
        head_sums[1],
        head_sums[2],
        sums[3],
        sum_out,
        sums[4],
        sums[5],
        grad_expert_up,
        grad_expert_down,
        sum_shared_up,
        sum_shared_down,
    )


def solution(mesh):
    fine = Mesh(
        mesh.devices.reshape((mesh.shape["dp"], 2, 2, 2, mesh.shape["expert"] // 8)), EVERY
    )
    rows = P(SPLIT, "dp", None)
    flat = P(EVERY)
    split = P(EVERY, None)
    in_specs = (
        rows,
        rows,
        P(SPLIT),
        P(SPLIT),
        P(EVERY, None, None),
        flat,
        split,
        split,
        flat,
        P(),
        P(),
        P(),
        flat,
        split,
        flat,
        split,
        rows,
        rows,
        split,
        split,
    )
    out_specs = (
        rows,
        rows,
        flat,
        split,
        split,
        flat,
        P(),
        P(),
        P(),
        flat,
        split,
        flat,
        split,
        rows,
        rows,
        split,
        split,
    )
    return jax.shard_map(local, mesh=fine, in_specs=in_specs, out_specs=out_specs, check_vma=False)
```

time: 3510 us -> 1890 us (0.54)
  local copies, waits for them, and re-layouts: 791 us -> 130 us
  waiting for transfers between devices: 1430 us -> 996 us
  blocking collectives: 459 us -> 69.2 us
  other arithmetic: 339 us -> 215 us
  matrix products: 376 us -> 434 us
  starting transfers between devices: 77.2 us -> 21.2 us
    unnamed x10 -> x18, waiting for transfers between devices: 863 us -> 126 us
    reduce_scatter x0 -> x8, waiting for transfers between devices: none -> 577 us  [scatter_rows(): return lax.psum_scatter(block, axes, scatter_dimension=0, tiled=True)]
    all_to_all x4 -> x1, waiting for transfers between devices: 348 us -> 0.01 us  [local(): lax.all_to_all(gate_cot_rows, GROUP, split_axis=0, concat_axis=0, tiled=T...]
    all_gather x2 -> x3, blocking collectives: 328 us -> 69.2 us  [gather_rows(): return lax.all_gather(block, axes, axis=0, tiled=True)]
    unnamed x340 -> x247, local copies, waits for them, and re-layouts: 251 us -> 33.5 us
    gather x8 -> x0, local copies, waits for them, and re-layouts: 115 us -> none  [the longest x1 27.1 us: local(): jnp.take(pad_row(pair_cot.reshape(pair_count, model_width)), slot_pair, a...]
    reshape x12 -> x11, local copies, waits for them, and re-layouts: 92.5 us -> 3.68 us  [the longest x6 2.99 us: local(): shares = [v.reshape(device_total, -1) for v in small_cots]]
    psum x1 -> x0, blocking collectives: 78.4 us -> none  [local(): head_sums = lax.psum((step_cot, decay_cot, skip_cot), ('dp', 'expert'))]
  transfers between devices with their start and end apart: 16 -> 22, of which waited for: 5 -> 13; matrix products, arithmetic and copies ran while one was open for 38% -> 40% of each run, Pallas kernels for 0% -> 0%
where the time goes in v1:
time: 1890 us; the launch traced here: 1880 us
  waiting for transfers between devices  996 us (53%)
  matrix products  434 us (23%)
  other arithmetic  215 us (11%)
  local copies, waits for them, and re-layouts  130 us (7%)
  blocking collectives  69.2 us (4%)
  starting transfers between devices  21.2 us (1%)
    reduce_scatter x8, waiting for transfers between devices, scatter_rows(): return lax.psum_scatter(block, axes, scatter_dimension=0, tiled=True)  577 us
    all_gather x8, waiting for transfers between devices, gather_rows(): return lax.all_gather(block, axes, axis=0, tiled=True)  270 us
    unnamed x18, waiting for transfers between devices  126 us
    dot_general x3, matrix products, ssd_blocks(): jnp.einsum('sktjh,skjhp->skthp', mixing, head_inputs, precision=FULL_PREC...  78.3 us
    all_gather x3, blocking collectives, gather_rows(): return lax.all_gather(block, axes, axis=0, tiled=True)  69.2 us
    dot_general x5, matrix products, dot_right(): lax.dot_general(left_mat, right_mat, (((1,), (1,)), ((), ())), preferred_...  61.3 us
    dot_general x5, matrix products, dot_left(): lax.dot_general(left_mat, right_mat, (((0,), (0,)), ((), ())), preferred_...  42.8 us
    dot_general x5, matrix products, dot(): return jnp.dot(left_mat, right_mat, preferred_element_type=jnp.float32)  41.9 us
  transfers between devices with their start and end apart: 22, of which 13 were waited for; matrix products, arithmetic and copies ran while one was open for 40% of the time, Pallas kernels for 0%

profile of v1, /device:TPU:0, one launch (start us, length us, event | category | flops | bytes accessed | tf_op | source)
XLA Modules:
  0.0 1880.9 jit_solution(18159914567057627201)
XLA Ops:
  23.3 22.8 %all-to-all-done.2 = bf16[2,256,1536]{2,1,0:T(8,128)(2,1)S(1)} async-done(((bf16[2,256,1536]{2,1,0:T(8,128)(2,1)}), bf16[2,256,1536]{2,1,0:T(8,128)(2,1)S(1)}, u32[]{:S(2)}, u32[]{:S(2)}) %all-to-all-start.2) | async-done | bytes 1572896 | tf_op jit(solution)/shard_map/all_to_all | solution.py:183
  53.2 43.9 %all-gather = bf16[32,1,1480]{2,1,0:T(2,128)(2,1)S(1)} all-gather(bf16[1,1,1480]{2,1,0:T(2,128)(2,1)S(1)} %bitcast.451), channel_id=1, replica_groups=mesh['dp'=2,'e3'=2,'e2'=2,'e1'=2,'e0'=2] {'dp','e3','e2','e1','e0'}, dimensions={0}, use_global_device_ids=true | all-gather | bytes 97680 | tf_op jit(solution)/shard_map/all_gather | solution.py:123
  108.4 40.2 %all-gather.10.cloned.1.call-done = bf16[1536,6448]{1,0:T(8,128)(2,1)} async-done(((bf16[48,6448]{1,0:T(8,128)(2,1)}), bf16[1536,6448]{1,0:T(8,128)(2,1)}) %all-gather.10.cloned.1.call-update) | async-done | bytes 19808272 | tf_op jit(solution)/shard_map/all_gather | solution.py:123
  148.6 17.8 fusion.158
  173.2 5.3 copy-done.4
  178.6 9.9 fusion.25
  194.6 7.9 reshape.742
  206.4 9.9 fusion.95
  219.8 14.2 while.34
  234.0 8.0 fusion.44
  245.2 28.8 %bitcast_add_fusion.6 = f32[1,4,128,48,64]{2,4,3,1,0:T(8,128)} fusion(f32[4,128,48,64]{1,3,2,0:T(8,128)S(1)} %fusion.44, f32[4,128,48]{1,2,0:T(8,128)S(1)} %copy.267, f32[4,128,48]{1,2,0:T(8,128)S(1)} %copy_bitcast_fusion.2, f32[4,128,48]{1,2,0:T(8,128)S(1)} %copy.256, f32[4,128,128]{2,1,0:T(8,128)S(1)} %fusion.159, pred[128,128]{1,0:T(8,128)(4,1)S(1)} %copy-done.79, ...), kind=kOutput, calls=%fused_computation.92 | convolution fusion | flops 2434793472 | bytes 19447808 | tf_op jit(solution)/shard_map/jvp(sktjh,skjhp->skthp)/dot_general | solution.py:46
  274.0 8.7 copy.268
  282.8 8.7 multiply_reduce_fusion.9
  291.6 10.5 multiply_reduce_fusion.12
  311.6 12.5 all_gather.36
  327.1 11.3 convolution_convert_fusion.4
  339.0 12.7 all_gather.37
  351.9 19.5 %all-gather.14.cloned.1.call-done = bf16[4096,1536]{1,0:T(8,128)(2,1)} async-done(((bf16[512,1536]{1,0:T(8,128)(2,1)}), bf16[4096,1536]{1,0:T(8,128)(2,1)}) %all-gather.14.cloned.1.call-update) | async-done | bytes 12582928 | tf_op jit(solution)/shard_map/all_gather | solution.py:123
  371.5 11.8 fusion.13
  383.3 111.9 %all-gather.16.cloned.1.call-done = bf16[4,768,1024]{2,1,0:T(8,128)(2,1)} async-done(((bf16[1,768,1024]{2,1,0:T(8,128)(2,1)}), bf16[4,768,1024]{2,1,0:T(8,128)(2,1)}) %all-gather.16.cloned.1.call-update) | async-done | bytes 6291472 | tf_op jit(solution)/shard_map/all_gather | solution.py:123
  495.2 19.1 %fusion.11 = f32[2,8,224,1024]{3,2,1,0:T(8,128)} fusion(bf16[2,1536,1024,1]{2,1,3,0:T(8,128)(2,1)} %bitcast.458, bf16[2,8,224,1536]{3,2,0,1:T(8,128)(2,1)} %fusion.13), kind=kOutput, calls=%fused_computation.43 | convolution fusion | flops 11274289152 | bytes 31981568 | tf_op jit(solution)/shard_map/escd,edf->escf/dot_general | solution.py:287
  514.3 7.7 multiply_convert_fusion
  521.9 44.7 %all-gather.18.cloned.1.call-done = bf16[4,256,1536]{2,1,0:T(8,128)(2,1)} async-done(((bf16[1,256,1536]{2,1,0:T(8,128)(2,1)}), bf16[4,256,1536]{2,1,0:T(8,128)(2,1)}) %all-gather.18.cloned.1.call-update) | async-done | bytes 3145744 | tf_op jit(solution)/shard_map/all_gather | solution.py:123
  566.6 12.7 fusion.4
  582.6 17.3 fusion.117
  599.9 24.5 %bitcast_convert_fusion = bf16[8,512,1536]{2,1,0:T(8,128)(2,1)} fusion(s32[8,2,512]{2,1,0:T(2,128)S(1)} %copy.271, bf16[2,1536,1024,1]{2,1,0,3:T(8,128)(2,1)} %bitcast.459, f32[2,8,224,512]{3,2,1,0:T(8,128)} %get-tuple-element.435, f32[2,8,224,512]{3,2,1,0:T(8,128)} %get-tuple-element.434), kind=kOutput, calls=%fused_computation.19 | convolution fusion | flops 16932405248 | bytes 33587200 | tf_op jit(solution)/shard_map/sect,escd->std/dot_general | solution.py:280
  624.5 12.6 bitcast_convert_fusion.1
  638.6 7.9 fusion.160
  646.5 52.5 %all-gather.22.cloned.1.call-done = bf16[1024,1536]{1,0:T(8,128)(2,1)} async-done(((bf16[32,1536]{1,0:T(8,128)(2,1)}), bf16[1024,1536]{1,0:T(8,128)(2,1)}) %all-gather.22.cloned.1.call-update) | async-done | bytes 3145744 | tf_op jit(solution)/shard_map/all_gather | solution.py:123
  699.0 8.0 fusion.126
  711.5 7.8 convolution_convert_fusion.6
  719.4 12.5 bitcast_convert_fusion.3
  731.9 9.3 fusion.122
  745.3 19.8 %bitcast_convert_fusion.2 = bf16[2,1536,1024]{2,1,0:T(8,128)(2,1)} fusion(bf16[2,8,224,1536]{3,2,0,1:T(8,128)(2,1)} %fusion.13, f32[2,8,224,512]{3,2,1,0:T(8,128)} %get-tuple-element.435, f32[2,8,224,512]{3,2,1,0:T(8,128)} %get-tuple-element.434), kind=kOutput, calls=%fused_computation.30 | convolution fusion | flops 11284774912 | bytes 31981568 | tf_op jit(solution)/shard_map/escd,escf->edf/dot_general | solution.py:321
  770.6 50.7 %reduce-scatter.11.cloned.1.call-done = bf16[512,1536]{1,0:T(8,128)(2,1)} async-done(((bf16[4096,1536]{1,0:T(8,128)(2,1)}), bf16[512,1536]{1,0:T(8,128)(2,1)}) %reduce-scatter.11.cloned.1.call-update) | async-done | bytes 1572880 | tf_op jit(solution)/shard_map/reduce_scatter | solution.py:127
  821.3 5.3 multiply_reduce_fusion.10
  829.4 13.9 multiply_reduce_fusion.6
  843.4 12.7 fusion.41
  856.1 7.7 reshape.760
  863.8 9.6 fusion.94
  877.8 7.8 reshape.763
  885.6 14.9 fusion.108
  904.0 17.9 while.35
  921.9 8.7 fusion.98
  930.6 15.1 fusion.111
  945.8 10.4 multiply_reduce_fusion.5
  957.2 32.4 %fusion.27 = (f32[4,128,48]{1,2,0:T(8,128)S(1)}, f32[4,128,48]{1,2,0:T(8,128)S(1)}, f32[4,128,48]{1,2,0:T(8,128)S(1)}, f32[4,128,128]{2,1,0:T(8,128)S(1)}) fusion(f32[4,128,48]{1,2,0:T(8,128)S(1)} %copy-done.58, f32[4,128,48]{1,2,0:T(8,128)S(1)} %copy-done.60, f32[4,128,128]{2,1,0:T(8,128)S(1)} %copy-done.43, pred[128,128]{1,0:T(8,128)(4,1)S(1)} %copy-done.80, ...), kind=kOutput, calls=%fused_computation.81 | convolution fusion | flops 2462965760 | bytes 13615104 | tf_op jit(solution)/shard_map/transpose(jvp(sktjh,skjhp->skthp))/dot_general | solution.py:46
  998.2 17.1 bitcast_add_fusion.5
  1015.3 8.4 copy.303
  1023.7 6.2 fusion.33
  1030.0 21.2 %multiply_reduce_fusion.3 = (f32[3328]{0:T(1024)S(1)}, f32[3328]{0:T(1024)S(1)}, f32[3328]{0:T(1024)S(1)}, f32[3328]{0:T(1024)S(1)}, f32[3328]{0:T(1024)S(1)}, /*index=5*/f32[1,512,3328]{1,2,0:T(8,128)}) fusion(f32[1,512,3328]{1,2,0:T(8,128)} %copy-done.6, f32[512,6448]{0,1:T(8,128)} %fusion.158, f32[1,512,3328]{1,2,0:T(8,128)} %get-tuple-element.430, ...), kind=kLoop, calls=%fused_computation.76 | loop fusion | flops 34062080 | bytes 34145280 | tf_op jit(solution)/shard_map/transpose(jvp())/reduce_sum | solution.py:91
  1053.6 8.5 broadcast_multiply_fusion
  1062.1 9.6 fusion.24
  1071.8 24.8 %fusion.85 = (f32[1536]{0:T(1024)S(1)}, f32[512]{0:T(512)S(1)}, f32[512,1536]{1,0:T(8,128)}) fusion(bf16[2,256,1536]{2,1,0:T(8,128)(2,1)} %all-to-all-done, f32[512]{0:T(512)S(1)} %copy-done.78, f32[1536]{0:T(1024)S(1)} %copy-done.62, bf16[1536,6448]{1,0:T(8,128)(2,1)} %all-gather.10.cloned.1.call-done, f32[512,3072]{0,1:T(8,128)} %get-tuple-element.433, ...), kind=kOutput, calls=%fused_computation.166 | convolution fusion | flops 10157234176 | bytes 37748736 | tf_op jit(solution)/shard_map/dot_general | solution.py:107
  1098.0 11.0 convolution_convert_fusion.3
  1110.5 18.9 %convolution_convert_fusion = bf16[1536,6448]{1,0:T(8,128)(2,1)} fusion(bf16[512,1536]{1,0:T(8,128)(2,1)S(1)} %copy-done.32, f32[512,3072]{0,1:T(8,128)} %get-tuple-element.433, f32[512,3328]{0,1:T(8,128)} %fusion.24, f32[512,48]{0,1:T(8,128)S(1)} %get-tuple-element.423), kind=kOutput, calls=%fused_computation.18 | convolution fusion | flops 10161635328 | bytes 34586624 | tf_op jit(solution)/shard_map/dot_general | solution.py:113
  1130.6 5.1 fusion.93
  1140.3 11.5 reduce.45
  1165.9 11.5 reduce.44
  1186.5 69.8 %reduce-scatter.19.cloned.1.call-done = bf16[1,256,1536]{2,1,0:T(8,128)(2,1)} async-done(((bf16[4,256,1536]{2,1,0:T(8,128)(2,1)}), bf16[1,256,1536]{2,1,0:T(8,128)(2,1)}) %reduce-scatter.19.cloned.1.call-update) | async-done | bytes 786448 | tf_op jit(solution)/shard_map/reduce_scatter | solution.py:127
  1258.8 121.0 %reduce-scatter.17.cloned.1.call-done = bf16[1,768,1024]{2,1,0:T(8,128)(2,1)} async-done(((bf16[4,768,1024]{2,1,0:T(8,128)(2,1)}), bf16[1,768,1024]{2,1,0:T(8,128)(2,1)}) %reduce-scatter.17.cloned.1.call-update) | async-done | bytes 1572880 | tf_op jit(solution)/shard_map/reduce_scatter | solution.py:127
  1383.3 125.5 %all-reduce.24.cloned.1.call-done = f32[32,1624]{1,0:T(8,128)} async-done(((f32[32,1624]{1,0:T(8,128)}), f32[32,1624]{1,0:T(8,128)}) %all-reduce.24.cloned.1.call-update) | async-done | bytes 207888
  1534.1 117.9 %reduce-scatter.15.cloned.1.call-done = bf16[96,1536]{1,0:T(8,128)(2,1)} async-done(((bf16[3072,1536]{1,0:T(8,128)(2,1)}), bf16[96,1536]{1,0:T(8,128)(2,1)}) %reduce-scatter.15.cloned.1.call-update) | async-done | bytes 294928 | tf_op jit(solution)/shard_map/reduce_scatter | solution.py:127
  1653.8 217.9 %reduce-scatter.13.cloned.1.call-done = bf16[48,6448]{1,0:T(8,128)(2,1)} async-done(((bf16[1536,6448]{1,0:T(8,128)(2,1)}), bf16[48,6448]{1,0:T(8,128)(2,1)}) %reduce-scatter.13.cloned.1.call-update) | async-done | bytes 619024 | tf_op jit(solution)/shard_map/reduce_scatter | solution.py:127
  (490 shorter events, 210.7 us)
Async XLA Ops:
  7.2 141.4 %all-gather.10.cloned.1.call-start = ((), (), s32[]{:S(2)}) async-start(), calls=%async_computation.13 | async-start | bytes 20680704 | tf_op jit(solution)/shard_map/all_gather | solution.py:123
  9.6 282.0 %all-gather.12.cloned.1.call-start = ((), (), s32[]{:S(2)}) async-start(), calls=%async_computation.14 | async-start | bytes 9732096 | tf_op jit(solution)/shard_map/all_gather | solution.py:123
  17.0 35.5 %copy-start.96 = (f32[104,4]{0,1:T(4,128)S(1)}, f32[104,4]{0,1:T(4,128)}, u32[]{:S(2)}) copy-start(f32[104,4]{0,1:T(4,128)} %param.33) | copy-start | bytes 4996
  17.0 35.8 %copy-start.84 = (f32[48,16]{0,1:T(8,128)S(1)}, f32[48,16]{0,1:T(8,128)}, u32[]{:S(2)}) copy-start(f32[48,16]{0,1:T(8,128)} %param.41) | copy-start | bytes 9220
  17.0 36.0 %copy-start.103 = (f32[96]{0:T(128)S(1)}, f32[96]{0:T(128)}, u32[]{:S(2)}) copy-start(f32[96]{0:T(128)} %param.38) | copy-start | bytes 1156
  17.0 36.0 %copy-start.104 = (f32[104]{0:T(128)S(1)}, f32[104]{0:T(128)}, u32[]{:S(2)}) copy-start(f32[104]{0:T(128)} %param.34) | copy-start | bytes 1252
  17.0 36.0 %copy-start.101 = (f32[48]{0:T(128)S(1)}, f32[48]{0:T(128)}, u32[]{:S(2)}) copy-start(f32[48]{0:T(128)} %param.40) | copy-start | bytes 580
  17.1 36.0 %copy-start.102 = (f32[48]{0:T(128)S(1)}, f32[48]{0:T(128)}, u32[]{:S(2)}) copy-start(f32[48]{0:T(128)} %param.31) | copy-start | bytes 580
  17.1 81.6 %copy-start.98 = (f32[48]{0:T(128)S(1)}, f32[48]{0:T(128)}, u32[]{:S(2)}) copy-start(f32[48]{0:T(128)} %param.37) | copy-start | bytes 580
  17.1 83.8 %copy-start.105 = (f32[48]{0:T(128)S(1)}, f32[48]{0:T(128)}, u32[]{:S(2)}) copy-start(f32[48]{0:T(128)} %param.36) | copy-start | bytes 580
  17.1 29.0 %all-to-all-start.2 = ((bf16[2,256,1536]{2,1,0:T(8,128)(2,1)}), bf16[2,256,1536]{2,1,0:T(8,128)(2,1)S(1)}, u32[]{:S(2)}, u32[]{:S(2)}) async-start(bf16[2,256,1536]{2,1,0:T(8,128)(2,1)} %get-tuple-element.461), calls=%async_computation.3 | async-start | bytes 3145728 | tf_op jit(solution)/shard_map/all_to_all | solution.py:183
  21.5 305.6 %all-gather.24.cloned.1.call-start = ((), (), s32[]{:S(2)}) async-start(), calls=%async_computation.21 | async-start | bytes 14155776 | tf_op jit(solution)/shard_map/all_gather | solution.py:123
  23.3 29.2 %copy-start.90 = (pred[512]{0:T(512)(128)(4,1)}, pred[512]{0:T(512)(128)(4,1)S(1)}, u32[]{:S(2)}) copy-start(pred[512]{0:T(512)(128)(4,1)S(1)} %iota_compare_fusion.7) | copy-start | bytes 1540
  47.8 56.9 %all-to-all-start = ((bf16[2,256,1536]{2,1,0:T(8,128)(2,1)}), bf16[2,256,1536]{2,1,0:T(8,128)(2,1)}, u32[]{:S(2)}, u32[]{:S(2)}) async-start(bf16[2,256,1536]{2,1,0:T(8,128)(2,1)} %get-tuple-element.462), calls=%async_computation | async-start | bytes 3145728 | tf_op jit(solution)/shard_map/all_to_all | solution.py:180
  52.4 319.0 %all-gather.14.cloned.1.call-start = ((), (), s32[]{:S(2)}) async-start(), calls=%async_computation.15 | async-start | bytes 14155776 | tf_op jit(solution)/shard_map/all_gather | solution.py:123
  98.8 184.0 %copy-start.44 = (f32[3072]{0:T(1024)}, f32[3072]{0:T(1024)S(1)}, u32[]{:S(2)}) copy-start(f32[3072]{0:T(1024)S(1)} %mul.661) | copy-start | bytes 36868
  100.9 66.7 %copy-start.93 = (f32[48]{0:T(128)}, f32[48]{0:T(128)S(1)}, u32[]{:S(2)}) copy-start(f32[48]{0:T(128)S(1)} %exponential_negate_fusion) | copy-start | bytes 580
  104.6 68.6 %copy-start.47 = (f32[3328]{0:T(1024)}, f32[3328]{0:T(1024)S(1)}, u32[]{:S(2)}) copy-start(f32[3328]{0:T(1024)S(1)} %get-tuple-element.390) | copy-start | bytes 39940
  104.6 68.6 %copy-start.49 = (f32[3328]{0:T(1024)}, f32[3328]{0:T(1024)S(1)}, u32[]{:S(2)}) copy-start(f32[3328]{0:T(1024)S(1)} %get-tuple-element.391) | copy-start | bytes 39940
  106.5 60.0 %copy-start.75 = (f32[1,2,2,128]{3,1,2,0:T(2,128)}, f32[1,2,2,128]{3,1,2,0:T(2,128)S(1)}, u32[]{:S(2)}) copy-start(f32[1,2,2,128]{3,1,2,0:T(2,128)S(1)} %copy.354) | copy-start | bytes 6148
  106.5 59.9 %copy-start.77 = (f32[512]{0:T(512)}, f32[512]{0:T(512)S(1)}, u32[]{:S(2)}) copy-start(f32[512]{0:T(512)S(1)} %rsqrt.30) | copy-start | bytes 6148
  108.4 58.1 %copy-start.31 = (bf16[512,1536]{1,0:T(8,128)(2,1)}, bf16[512,1536]{1,0:T(8,128)(2,1)S(1)}, u32[]{:S(2)}) copy-start(bf16[512,1536]{1,0:T(8,128)(2,1)S(1)} %fusion.84) | copy-start | bytes 4718596
  108.4 58.1 %copy-start.88 = (f32[48]{0:T(128)S(1)}, f32[48]{0:T(128)}, u32[]{:S(2)}) copy-start(f32[48]{0:T(128)} %param.35) | copy-start | bytes 580
  167.9 36.6 %copy-start.15 = (f32[1,4,128,48]{3,2,1,0:T(8,128)}, f32[1,4,128,48]{3,2,1,0:T(8,128)S(1)}, u32[]{:S(2)}) copy-start(f32[1,4,128,48]{3,2,1,0:T(8,128)S(1)} %reduce_window_sum.26) | copy-start | bytes 294916
  169.2 37.2 %copy-start.33 = (f32[4,128,48]{1,2,0:T(8,128)}, f32[4,128,48]{1,2,0:T(8,128)S(1)}, u32[]{:S(2)}) copy-start(f32[4,128,48]{1,2,0:T(8,128)S(1)} %copy.261) | copy-start | bytes 294916
  204.4 29.6 %copy-start.24 = (f32[4,128,128,1]{2,1,3,0:T(8,128)}, f32[4,128,128,1]{2,1,3,0:T(8,128)S(1)}, u32[]{:S(2)}) copy-start(f32[4,128,128,1]{2,1,3,0:T(8,128)S(1)} %copy.313) | copy-start | bytes 786436
  204.5 37.5 %copy-start.35 = (f32[4,128,48]{1,2,0:T(8,128)}, f32[4,128,48]{1,2,0:T(8,128)S(1)}, u32[]{:S(2)}) copy-start(f32[4,128,48]{1,2,0:T(8,128)S(1)} %copy.267) | copy-start | bytes 294916
  204.6 37.4 %copy-start.59 = (f32[4,128,48]{1,2,0:T(8,128)}, f32[4,128,48]{1,2,0:T(8,128)S(1)}, u32[]{:S(2)}) copy-start(f32[4,128,48]{1,2,0:T(8,128)S(1)} %copy.256) | copy-start | bytes 294916
  205.7 36.3 %copy-start.57 = (f32[4,128,48]{1,2,0:T(8,128)}, f32[4,128,48]{1,2,0:T(8,128)S(1)}, u32[]{:S(2)}) copy-start(f32[4,128,48]{1,2,0:T(8,128)S(1)} %copy_bitcast_fusion.2) | copy-start | bytes 294916
  206.4 35.6 %copy-start.42 = (f32[4,128,128]{2,1,0:T(8,128)}, f32[4,128,128]{2,1,0:T(8,128)S(1)}, u32[]{:S(2)}) copy-start(f32[4,128,128]{2,1,0:T(8,128)S(1)} %fusion.159) | copy-start | bytes 786436
  234.0 48.8 %slice-start = ((s8[6815744]{0:T(1024)(128)(4,1)}), s8[4194304]{0:T(1024)(128)(4,1)S(1)}, s32[]{:S(2)}) async-start(s8[6815744]{0:T(1024)(128)(4,1)} %bitcast.404), calls=%async_computation.30 | async-start | bytes 8388608
  245.2 37.6 %slice-start.1 = ((s8[6815744]{0:T(1024)(128)(4,1)}), s8[2621440]{0:T(1024)(128)(4,1)S(1)}, s32[]{:S(2)}) async-start(s8[6815744]{0:T(1024)(128)(4,1)} %bitcast.404), calls=%async_computation.31 | async-start | bytes 5242880
  305.4 189.8 %all-gather.16.cloned.1.call-start = ((), (), s32[]{:S(2)}) async-start(), calls=%async_computation.16 | async-start | bytes 7864320 | tf_op jit(solution)/shard_map/all_gather | solution.py:123
  308.8 257.8 %all-gather.18.cloned.1.call-start = ((), (), s32[]{:S(2)}) async-start(), calls=%async_computation.17 | async-start | bytes 3932160 | tf_op jit(solution)/shard_map/all_gather | solution.py:123
  309.8 328.8 %all-gather.20.cloned.1.call-start = ((), (), s32[]{:S(2)}) async-start(), calls=%async_computation.19 | async-start | bytes 6488064 | tf_op jit(solution)/shard_map/all_gather | solution.py:123
  310.6 388.4 %all-gather.22.cloned.1.call-start = ((), (), s32[]{:S(2)}) async-start(), calls=%async_computation.20 | async-start | bytes 3244032 | tf_op jit(solution)/shard_map/all_gather | solution.py:123
  311.3 509.9 %reduce-scatter.11.cloned.1.call-start = ((), (), s32[]{:S(2)}) async-start(), calls=%async_computation.22 | async-start | bytes 14155776 | tf_op jit(solution)/shard_map/reduce_scatter | solution.py:127
  624.4 505.8 %reduce-scatter.9.cloned.1.call-start = ((), (), s32[]{:S(2)}) async-start(), calls=%async_computation.18 | async-start | bytes 14155776 | tf_op jit(solution)/shard_map/reduce_scatter | solution.py:127
  637.0 61.9 %copy-start.19 = (bf16[512,1536]{1,0:T(8,128)(2,1)S(1)}, bf16[512,1536]{1,0:T(8,128)(2,1)}, u32[]{:S(2)}) copy-start(bf16[512,1536]{1,0:T(8,128)(2,1)} %bitcast_select_fusion) | copy-start | bytes 4718596
  637.0 546.2 %reduce-scatter.23.cloned.1.call-start = ((), (), s32[]{:S(2)}) async-start(), calls=%async_computation.28 | async-start | bytes 3244032 | tf_op jit(solution)/shard_map/reduce_scatter | solution.py:127
  711.4 473.4 %reduce-scatter.21.cloned.1.call-start = ((), (), s32[]{:S(2)}) async-start(), calls=%async_computation.27 | async-start | bytes 6488064 | tf_op jit(solution)/shard_map/reduce_scatter | solution.py:127
  719.4 536.9 %reduce-scatter.19.cloned.1.call-start = ((), (), s32[]{:S(2)}) async-start(), calls=%async_computation.26 | async-start | bytes 3932160 | tf_op jit(solution)/shard_map/reduce_scatter | solution.py:127
  741.3 24.1 %all-to-all-start.3 = ((f32[8,2,512]{2,1,0:T(2,128)}), f32[8,2,512]{2,1,0:T(2,128)}, u32[]{:S(2)}, u32[]{:S(2)}) async-start(f32[8,2,512]{2,1,0:T(2,128)} %get-tuple-element.394), calls=%async_computation.5 | async-start | bytes 65536 | tf_op jit(solution)/shard_map/all_to_all | solution.py:312
  745.2 634.6 %reduce-scatter.17.cloned.1.call-start = ((), (), s32[]{:S(2)}) async-start(), calls=%async_computation.25 | async-start | bytes 7864320 | tf_op jit(solution)/shard_map/reduce_scatter | solution.py:127
  765.1 56.2 %copy-start.21 = (bf16[1536,16]{1,0:T(8,128)(2,1)S(1)}, bf16[1536,16]{1,0:T(8,128)(2,1)}, u32[]{:S(2)}) copy-start(bf16[1536,16]{1,0:T(8,128)(2,1)} %copy-done.20) | copy-start | bytes 147460
  765.1 743.6 %all-reduce.24.cloned.1.call-start = ((), (), s32[]{:S(2)}) async-start(), calls=%async_computation.29 | async-start | bytes 425984
  768.4 58.2 %copy-start.14 = (bf16[2,256,1536]{2,1,0:T(8,128)(2,1)S(1)}, bf16[2,256,1536]{2,1,0:T(8,128)(2,1)}, u32[]{:S(2)}) copy-start(bf16[2,256,1536]{2,1,0:T(8,128)(2,1)} %copy-done.13) | copy-start | bytes 4718596
  957.2 39.4 %copy-start.29 = (f32[4,128,128]{2,1,0:T(8,128)S(1)}, f32[4,128,128]{2,1,0:T(8,128)}, u32[]{:S(2)}) copy-start(f32[4,128,128]{2,1,0:T(8,128)} %copy-done.28) | copy-start | bytes 786436
  1029.9 22.4 %copy-start.89 = (f32[48]{0:T(128)S(1)}, f32[48]{0:T(128)}, u32[]{:S(2)}) copy-start(f32[48]{0:T(128)} %param.35) | copy-start | bytes 580
  1029.9 23.6 %copy-start.48 = (f32[3328]{0:T(1024)S(1)}, f32[3328]{0:T(1024)}, u32[]{:S(2)}) copy-start(f32[3328]{0:T(1024)} %copy-done.47) | copy-start | bytes 39940
  1030.0 23.6 %copy-start.50 = (f32[3328]{0:T(1024)S(1)}, f32[3328]{0:T(1024)}, u32[]{:S(2)}) copy-start(f32[3328]{0:T(1024)} %copy-done.49) | copy-start | bytes 39940
  1030.0 23.6 %copy-start.52 = (f32[3328]{0:T(1024)S(1)}, f32[3328]{0:T(1024)}, u32[]{:S(2)}) copy-start(f32[3328]{0:T(1024)} %get-tuple-element.392) | copy-start | bytes 39940
  1030.0 23.6 %copy-start.54 = (f32[3328]{0:T(1024)S(1)}, f32[3328]{0:T(1024)}, u32[]{:S(2)}) copy-start(f32[3328]{0:T(1024)} %get-tuple-element.393) | copy-start | bytes 39940
  1071.7 25.0 %copy-start.81 = (f32[3072]{0:T(1024)S(1)}, f32[3072]{0:T(1024)}, u32[]{:S(2)}) copy-start(f32[3072]{0:T(1024)} %get-tuple-element.382) | copy-start | bytes 36868
  1071.7 25.1 %copy-start.70 = (f32[1536]{0:T(1024)S(1)}, f32[1536]{0:T(1024)}, u32[]{:S(2)}) copy-start(f32[1536]{0:T(1024)} %get-tuple-element.386) | copy-start | bytes 18436
  1071.7 25.3 %copy-start.106 = (f32[48]{0:T(128)S(1)}, f32[48]{0:T(128)}, u32[]{:S(2)}) copy-start(f32[48]{0:T(128)} %param.36) | copy-start | bytes 580
  1071.8 25.4 %copy-start.41 = (f32[32,768]{1,0:T(8,128)S(1)}, f32[32,768]{1,0:T(8,128)}, u32[]{:S(2)}) copy-start(f32[32,768]{1,0:T(8,128)} %reshape.777) | copy-start | bytes 294916
  1071.8 26.2 %copy-start.68 = (f32[3072]{0:T(1024)S(1)}, f32[3072]{0:T(1024)}, u32[]{:S(2)}) copy-start(f32[3072]{0:T(1024)} %reshape.786) | copy-start | bytes 36868
  1071.8 26.2 %copy-start.87 = (f32[512]{0:T(512)S(1)}, f32[512]{0:T(512)}, u32[]{:S(2)}) copy-start(f32[512]{0:T(512)} %copy-done.85) | copy-start | bytes 6148
  1098.0 554.0 %reduce-scatter.15.cloned.1.call-start = ((), (), s32[]{:S(2)}) async-start(), calls=%async_computation.24 | async-start | bytes 9732096 | tf_op jit(solution)/shard_map/reduce_scatter | solution.py:127
  1109.1 762.6 %reduce-scatter.13.cloned.1.call-start = ((), (), s32[]{:S(2)}) async-start(), calls=%async_computation.23 | async-start | bytes 20680704 | tf_op jit(solution)/shard_map/reduce_scatter | solution.py:127
  1153.8 25.7 %all-to-all-start.1 = ((bf16[2,2,196608]{2,1,0:T(2,128)(2,1)}), bf16[2,2,196608]{2,1,0:T(2,128)(2,1)S(1)}, u32[]{:S(2)}, u32[]{:S(2)}) async-start(bf16[2,2,196608]{2,1,0:T(2,128)(2,1)} %reshape.863), calls=%async_computation.2 | async-start | bytes 3145728 | tf_op jit(solution)/shard_map/all_to_all | solution.py:355
  1179.5 341.1 %all-to-all-start.4 = ((bf16[2,2,196608]{2,1,0:T(2,128)(2,1)}), bf16[2,2,196608]{2,1,0:T(2,128)(2,1)S(1)}, u32[]{:S(2)}, u32[]{:S(2)}) async-start(bf16[2,2,196608]{2,1,0:T(2,128)(2,1)} %reshape.865), calls=%async_computation.6 | async-start | bytes 3145728 | tf_op jit(solution)/shard_map/all_to_all | solution.py:368
  1526.7 347.2 %copy-start.1 = (bf16[2,256,1536]{2,1,0:T(8,128)(2,1)S(1)}, bf16[2,256,1536]{2,1,0:T(8,128)(2,1)}, u32[]{:S(2)}) copy-start(bf16[2,256,1536]{2,1,0:T(8,128)(2,1)} %param.26) | copy-start | bytes 4718596
  (75 other events, 678.4 us)
Sparse Core Ops, SparseCore 0:
  11.5 137.0 all-gather.9
  152.0 80.1 all-gather.11
  234.5 63.3 all-gather.23
  305.5 65.9 all-gather.13
  373.7 121.3 all-gather.15
  497.4 69.1 all-gather.17
  570.0 68.5 all-gather.19
  641.5 57.4 all-gather.21
  701.3 119.9 reduce-scatter.10
  823.4 127.5 reduce-scatter.8
  956.5 108.2 reduce-scatter.22
  1070.3 113.6 reduce-scatter.20
  1187.3 68.9 reduce-scatter.18
  1259.4 120.3 reduce-scatter.16
  1386.7 121.9 all-reduce.23
  1515.5 136.4 reduce-scatter.14
  1658.3 213.3 reduce-scatter.12

commit v2 on v1

v2 whole, which is shorter than its diff:
```python
from functools import partial

import jax
import jax.numpy as jnp
from jax import lax
from jax.experimental import pallas as pl
from jax.experimental.pallas import tpu as pltpu
from jax.sharding import Mesh, PartitionSpec as P

BLK = 128
LANES = 128
INTERPRET = False
NEVER = -1e30
EPSILON = 1e-05
FULL_PRECISION = lax.Precision.HIGHEST
SPLIT = ("e3", "e2", "e1", "e0")
EVERY = ("dp",) + SPLIT
GROUP = SPLIT[1:]


def rms_scale(values, gain_row):
    return (
        values * lax.rsqrt(jnp.mean(values * values, axis=-1, keepdims=True) + EPSILON) * gain_row
    )


def swiglu(pre_act):
    half_width = pre_act.shape[-1] // 2
    return jax.nn.silu(pre_act[..., :half_width]) * pre_act[..., half_width:]


def mm(left_mat, right_mat, left_dim=1, right_dim=0):
    return lax.dot_general(
        left_mat,
        right_mat,
        (((left_dim,), (right_dim,)), ((), ())),
        preferred_element_type=jnp.float32,
    )


def mm_parts(values, ones, right_dim=0):
    high = values.astype(jnp.bfloat16)
    rest = values - high.astype(jnp.float32)
    mid = rest.astype(jnp.bfloat16)
    low = (rest - mid.astype(jnp.float32)).astype(jnp.bfloat16)
    return (
        mm(high, ones, 1, right_dim) + mm(mid, ones, 1, right_dim) + mm(low, ones, 1, right_dim)
    )


def mm_full(left_mat, right_mat):
    return lax.dot_general(
        left_mat,
        right_mat,
        (((1,), (0,)), ((), ())),
        precision=FULL_PRECISION,
        preferred_element_type=jnp.float32,
    )


def iotas(size):
    return (
        lax.broadcasted_iota(jnp.int32, (size, LANES), 0),
        lax.broadcasted_iota(jnp.int32, (size, LANES), 1),
    )


def step_terms(raw, bias, decay, spread, ran, steps, run_rows):
    size = raw.shape[0]
    down, across = iotas(size)
    shifted = raw + bias
    step = jnp.maximum(shifted, 0.0) + jnp.log1p(jnp.exp(-jnp.abs(shifted)))
    rate = -jnp.exp(decay) * step
    run = mm_full((down >= across).astype(jnp.float32), rate)
    ran[...] = mm_parts(run, spread)
    steps[...] = mm_parts(step, spread)
    run_rows[...] = run.T
    return shifted, step, rate


def conv_at(ext, taps, shift, cols, size, width):
    total = shift[:, cols]
    for tap in range(width):
        total = total + taps[tap : tap + 1, cols] * ext[pl.ds(9 - width + tap, size), cols]
    return total


def scan_kernel(
    mixed, taps, shift, bias, decay, skip, spread, y_out, before_out,
    ext, state, ran, steps, run_rows, crossed, fed,
    *, width,
):
    size = mixed.shape[0]
    inner = skip.shape[1]
    channels = shift.shape[1]
    wide = inner // LANES
    head = channels

    @pl.when(pl.program_id(0) == 0)
    def _():
        ext[pl.ds(0, 8), :] = jnp.zeros((8, channels), jnp.float32)
        state[...] = jnp.zeros_like(state)

    @pl.when(pl.program_id(0) > 0)
    def _():
        ext[pl.ds(0, 8), :] = ext[pl.ds(size, 8), :]

    ext[pl.ds(8, size), :] = mixed[:, :channels]
    step_terms(mixed[:, head:], bias[...], decay[...], spread[...], ran, steps, run_rows)
    down, across = iotas(size)
    causal = down >= across
    first = across < LANES // 2
    keep = jax.nn.silu(conv_at(ext, taps, shift, pl.ds(inner, LANES), size, width))
    read = jax.nn.silu(conv_at(ext, taps, shift, pl.ds(inner + LANES, LANES), size, width))
    read_low = read.astype(jnp.bfloat16)
    scores = mm(read_low, keep.astype(jnp.bfloat16), 1, 1)
    crossed[...] = mm(read_low, state[...].astype(jnp.bfloat16))
    before_out[0] = state[...]

    def pair(number, carry):
        cols = pl.ds(pl.multiple_of(number * LANES, LANES), LANES)
        x = jax.nn.silu(conv_at(ext, taps, shift, cols, size, width))
        run = ran[:, cols]
        stepped = x * steps[:, cols]
        stepped_low = stepped.astype(jnp.bfloat16)
        inside = []
        for one in range(2):
            at_row = jnp.broadcast_to(run[:, one * (LANES // 2)][:, None], (size, LANES))
            at_col = run_rows[pl.ds(2 * number + one, 1), :]
            mix = scores * jnp.exp(jnp.where(causal, at_row - at_col, NEVER))
            inside.append(mm(mix.astype(jnp.bfloat16), stepped_low))
        y_out[:, cols] = (
            jnp.where(first, inside[0], inside[1])
            + jnp.exp(run) * crossed[:, cols]
            + skip[:, cols] * x
        )
        fed[:, cols] = (stepped * jnp.exp(run[size - 1 :, :] - run)).astype(jnp.bfloat16)
        return carry

    lax.fori_loop(0, wide, pair, 0)
    state[...] = jnp.exp(ran[pl.ds(size - 1, 1), :]) * state[...] + mm(
        keep.T.astype(jnp.bfloat16), fed[...]
    )


def scan_back_kernel(
    mixed, halo, y_cot, before, taps, shift, bias, decay, skip, spread,
    mixed_cot, taps_cot, shift_cot, skip_cot, bias_cot, decay_cot,
    ext, cot_ext, after, ran, steps, run_rows, crossed, kept, spill, turned, fed, heard, col_rows, scores_cot, ends,
    *, width,
):
    size = mixed.shape[0]
    inner = skip.shape[1]
    channels = shift.shape[1]
    wide = inner // LANES
    head = channels
    half = LANES // 2
    started = pl.program_id(0) == 0

    @pl.when(started)
    def _():
        cot_ext[pl.ds(size, 8), :] = jnp.zeros((8, channels), jnp.float32)
        after[...] = jnp.zeros_like(after)
        taps_cot[...] = jnp.zeros_like(taps_cot)
        shift_cot[...] = jnp.zeros_like(shift_cot)
        skip_cot[...] = jnp.zeros_like(skip_cot)
        bias_cot[...] = jnp.zeros_like(bias_cot)
        decay_cot[...] = jnp.zeros_like(decay_cot)

    @pl.when(jnp.logical_not(started))
    def _():
        cot_ext[pl.ds(size, 8), :] = cot_ext[pl.ds(0, 8), :]

    top = pl.program_id(0) == pl.num_programs(0) - 1
    ext[pl.ds(0, 8), :] = jnp.where(top, 0.0, halo[:, :channels])
    ext[pl.ds(8, size), :] = mixed[:, :channels]
    shifted, step, rate = step_terms(
        mixed[:, head:], bias[...], decay[...], spread[...], ran, steps, run_rows
    )
    down, across = iotas(size)
    later = across >= down
    first = across < half
    keep_cols = pl.ds(inner, LANES)
    read_cols = pl.ds(inner + LANES, LANES)
    keep_pre = conv_at(ext, taps, shift, keep_cols, size, width)
    read_pre = conv_at(ext, taps, shift, read_cols, size, width)
    keep, read = jax.nn.silu(keep_pre), jax.nn.silu(read_pre)
    keep_low, read_low = keep.astype(jnp.bfloat16), read.astype(jnp.bfloat16)
    scores = mm(keep_low, read_low, 1, 1)
    before_low = before[0].astype(jnp.bfloat16)
    after_low = after[...].astype(jnp.bfloat16)
    crossed[...] = mm(read_low, before_low)
    kept[...] = mm(keep_low, after_low)
    scores_cot[...] = jnp.zeros_like(scores_cot)
    col_rows[...] = jnp.zeros_like(col_rows)

    def finish(cols, pre, cot):
        gate = jax.nn.sigmoid(pre)
        cot = cot * (gate * (1.0 + pre * (1.0 - gate)))
        cot_ext[pl.ds(0, size), cols] = cot
        total = None
        for tap in range(width):
            part = taps[tap : tap + 1, cols] * cot_ext[pl.ds(width - 1 - tap, size), cols]
            total = part if total is None else total + part
            taps_cot[tap : tap + 1, cols] += jnp.sum(
                cot * ext[pl.ds(9 - width + tap, size), cols], axis=0, keepdims=True
            )
        shift_cot[:, cols] += jnp.sum(cot, axis=0, keepdims=True)
        mixed_cot[:, cols] = total.astype(jnp.bfloat16)

    def pair(number, carry):
        cols = pl.ds(pl.multiple_of(number * LANES, LANES), LANES)
        pre = conv_at(ext, taps, shift, cols, size, width)
        x = jax.nn.silu(pre)
        run = ran[:, cols]
        last = run[size - 1 :, :]
        steps_here = steps[:, cols]
        stepped = x * steps_here
        fade = jnp.exp(last - run)
        reach = jnp.exp(run)
        cot = y_cot[:, cols]
        cot_low = cot.astype(jnp.bfloat16)
        from_state = kept[:, cols] * fade
        sums, inside = [], []
        for one in range(2):
            at_row = jnp.broadcast_to(run[:, one * half][:, None], (size, LANES))
            at_col = run_rows[pl.ds(2 * number + one, 1), :]
            decayed = jnp.exp(jnp.where(later, at_col - at_row, NEVER))
            mine = first if one == 0 else jnp.logical_not(first)
            mix_cot = mm(jnp.where(mine, stepped, 0.0).astype(jnp.bfloat16), cot_low, 1, 1)
            decayed_cot = mix_cot * decayed
            scores_cot[...] += decayed_cot
            moved = decayed_cot * scores
            sums.append(jnp.sum(moved, axis=1, keepdims=True))
            col_rows[pl.ds(2 * number + one, 1), :] = jnp.sum(moved, axis=0, keepdims=True)
            inside.append(mm((scores * decayed).astype(jnp.bfloat16), cot_low))
        stepped_cot = jnp.where(first, inside[0], inside[1]) + from_state
        heard_here = reach * cot
        passed = stepped * from_state
        spill[:, cols] = (
            heard_here * crossed[:, cols]
            - passed
            - jnp.where(first, sums[0], sums[1]) * (1.0 / half)
        )
        turned[:, cols] = x * stepped_cot
        ends[:, cols] = jnp.sum(passed, axis=0, keepdims=True) + jnp.exp(last) * jnp.sum(
            before[0, :, cols] * after[:, cols], axis=0, keepdims=True
        )
        skip_cot[:, cols] += jnp.sum(x * cot, axis=0, keepdims=True)
        heard[:, cols] = heard_here.astype(jnp.bfloat16)
        fed[:, cols] = (stepped * fade).astype(jnp.bfloat16)
        finish(cols, pre, steps_here * stepped_cot + skip[:, cols] * cot)
        return carry

    lax.fori_loop(0, wide, pair, 0)
    scores_cot_low = scores_cot[...].astype(jnp.bfloat16)
    scores_cot_turned = scores_cot[...].T.astype(jnp.bfloat16)
    read_cot = mm(heard[...], before_low, 1, 1) + mm(scores_cot_turned, keep_low)
    keep_cot = mm(fed[...], after_low, 1, 1) + mm(scores_cot_low, read_low)
    finish(keep_cols, keep_pre, keep_cot)
    finish(read_cols, read_pre, read_cot)
    run_cot = mm_parts(spill[...], spread[...], 1) + col_rows[...].T
    end_cot = mm_parts(jnp.broadcast_to(ends[...], (8, inner)), spread[...], 1)[0:1]
    run_cot = run_cot + jnp.where(down == size - 1, end_cot, 0.0)
    rate_cot = mm_full(later.astype(jnp.float32), run_cot)
    step_cot = mm_parts(turned[...], spread[...], 1) - jnp.exp(decay[...]) * rate_cot
    raw_cot = step_cot * jax.nn.sigmoid(shifted)
    bias_cot[...] += jnp.sum(raw_cot, axis=0, keepdims=True)
    decay_cot[...] += jnp.sum(rate_cot * rate, axis=0, keepdims=True)
    mixed_cot[:, head:] = raw_cot.astype(jnp.bfloat16)
    after[...] = jnp.exp(ran[pl.ds(size - 1, 1), :]) * after[...] + mm(
        read.T.astype(jnp.bfloat16), heard[...]
    )


def whole(shape):
    return pl.BlockSpec(shape, lambda step: (0,) * len(shape))


def head_spread(heads, inner):
    return (
        lax.broadcasted_iota(jnp.int32, (LANES, inner), 0)
        == lax.broadcasted_iota(jnp.int32, (LANES, inner), 1) // (inner // heads)
    ).astype(jnp.bfloat16)


def scan_forward(mixed, taps, shift, bias, decay, skip, spread, block_len):
    rows, total = mixed.shape
    inner = skip.shape[1]
    channels = shift.shape[1]
    blocks = rows // block_len
    state_width = (channels - inner) // 2
    f32, low = jnp.float32, jnp.bfloat16
    return pl.pallas_call(
        partial(scan_kernel, width=taps.shape[0]),
        grid=(blocks,),
        in_specs=[
            pl.BlockSpec((block_len, total), lambda step: (step, 0)),
            whole(taps.shape),
            whole(shift.shape),
            whole(bias.shape),
            whole(decay.shape),
            whole(skip.shape),
            whole(spread.shape),
        ],
        out_specs=[
            pl.BlockSpec((block_len, inner), lambda step: (step, 0)),
            pl.BlockSpec((1, state_width, inner), lambda step: (step, 0, 0)),
        ],
        out_shape=[
            jax.ShapeDtypeStruct((rows, inner), f32),
            jax.ShapeDtypeStruct((blocks, state_width, inner), f32),
        ],
        scratch_shapes=[
            pltpu.VMEM((block_len + 8, channels), f32),
            pltpu.VMEM((state_width, inner), f32),
            pltpu.VMEM((block_len, inner), f32),
            pltpu.VMEM((block_len, inner), f32),
            pltpu.VMEM((LANES, block_len), f32),
            pltpu.VMEM((block_len, inner), f32),
            pltpu.VMEM((block_len, inner), low),
        ],
        compiler_params=pltpu.CompilerParams(vmem_limit_bytes=48 << 20),
        cost_estimate=pl.CostEstimate(
            flops=10**9, transcendentals=10**7, bytes_accessed=120 * 10**6
        ),
        interpret=INTERPRET,
        name="scan_forward",
    )(mixed, taps, shift, bias, decay, skip, spread)


def scan_backward(mixed, y_cot, before, taps, shift, bias, decay, skip, spread, block_len):
    rows, total = mixed.shape
    inner = skip.shape[1]
    channels = shift.shape[1]
    blocks = rows // block_len
    state_width = (channels - inner) // 2
    f32, low = jnp.float32, jnp.bfloat16
    eighths = block_len // 8
    back = blocks - 1
    return pl.pallas_call(
        partial(scan_back_kernel, width=taps.shape[0]),
        grid=(blocks,),
        in_specs=[
            pl.BlockSpec((block_len, total), lambda step: (back - step, 0)),
            pl.BlockSpec(
                (8, total), lambda step: (jnp.maximum((back - step) * eighths - 1, 0), 0)
            ),
            pl.BlockSpec((block_len, inner), lambda step: (back - step, 0)),
            pl.BlockSpec((1, state_width, inner), lambda step: (back - step, 0, 0)),
            whole(taps.shape),
            whole(shift.shape),
            whole(bias.shape),
            whole(decay.shape),
            whole(skip.shape),
            whole(spread.shape),
        ],
        out_specs=[
            pl.BlockSpec((block_len, total), lambda step: (back - step, 0)),
            whole(taps.shape),
            whole(shift.shape),
            whole(skip.shape),
            whole(bias.shape),
            whole(decay.shape),
        ],
        out_shape=[
            jax.ShapeDtypeStruct((rows, total), low),
            jax.ShapeDtypeStruct(taps.shape, f32),
            jax.ShapeDtypeStruct(shift.shape, f32),
            jax.ShapeDtypeStruct(skip.shape, f32),
            jax.ShapeDtypeStruct(bias.shape, f32),
            jax.ShapeDtypeStruct(decay.shape, f32),
        ],
        scratch_shapes=[
            pltpu.VMEM((block_len + 8, channels), f32),
            pltpu.VMEM((block_len + 8, channels), f32),
            pltpu.VMEM((state_width, inner), f32),
            pltpu.VMEM((block_len, inner), f32),
            pltpu.VMEM((block_len, inner), f32),
            pltpu.VMEM((LANES, block_len), f32),
            pltpu.VMEM((block_len, inner), f32),
            pltpu.VMEM((block_len, inner), f32),
            pltpu.VMEM((block_len, inner), f32),
            pltpu.VMEM((block_len, inner), f32),
            pltpu.VMEM((block_len, inner), low),
            pltpu.VMEM((block_len, inner), low),
            pltpu.VMEM((LANES, block_len), f32),
            pltpu.VMEM((block_len, block_len), f32),
            pltpu.VMEM((1, inner), f32),
        ],
        compiler_params=pltpu.CompilerParams(vmem_limit_bytes=56 << 20),
        cost_estimate=pl.CostEstimate(
            flops=2 * 10**9, transcendentals=10**7, bytes_accessed=240 * 10**6
        ),
        interpret=INTERPRET,
        name="scan_backward",
    )(mixed, mixed, y_cot, before, taps, shift, bias, decay, skip, spread)


def dot_right(left_mat, right_mat):
    return lax.dot_general(
        left_mat, right_mat, (((1,), (1,)), ((), ())), preferred_element_type=jnp.float32
    )


def dot_left(left_mat, right_mat):
    return lax.dot_general(
        left_mat, right_mat, (((0,), (0,)), ((), ())), preferred_element_type=jnp.float32
    )


def to_low(weight):
    return weight.astype(jnp.bfloat16)


def gather_rows(block, axes):
    return lax.all_gather(block, axes, axis=0, tiled=True)


def tell(row, axes):
    return lax.all_to_all(
        jnp.broadcast_to(row, (lax.axis_size(axes),) + row.shape[1:]),
        axes,
        split_axis=0,
        concat_axis=0,
        tiled=True,
    )


def scatter_rows(block, axes):
    return lax.psum_scatter(block, axes, scatter_dimension=0, tiled=True)


def dot(left_mat, right_mat):
    return jnp.dot(left_mat, right_mat, preferred_element_type=jnp.float32)


def swap(block, axis):
    return lax.ppermute(block, axis, [(0, 1), (1, 0)])


def after(value, *others):
    return lax.optimization_barrier((value,) + others)[0]


def spread_rows(block, second, third, gates):
    if lax.axis_size(second) != 2:
        second, third = third, second
    whole_block = block.reshape((1,) * len(EVERY) + block.shape)
    for axis, gate in zip(("e3", "e2", third, second, "e0"), gates):
        at = EVERY.index(axis)
        if lax.axis_size(axis) == 2:
            came = swap(whole_block, axis)
            if gate is not None:
                came = after(came, gate)
            whole_block = join(whole_block, came, lax.axis_index(axis), at)
        else:
            whole_block = lax.all_gather(whole_block, axis, axis=at, tiled=True)
    return whole_block.reshape(-1, block.shape[1])


def take(block, place, axis_at):
    return lax.dynamic_index_in_dim(block, place, axis_at, keepdims=False)


def fold(block, layout, order):
    layout = list(layout)
    for axis in order:
        at = layout.index(axis)
        if lax.axis_size(axis) == 2:
            place = lax.axis_index(axis)
            came = swap(take(block, 1 - place, at), axis)
            block = add(take(block, place, at), came)
        else:
            block = lax.psum_scatter(block, axis, scatter_dimension=at, tiled=False)
        layout.pop(at)
    return block


def add(one, other):
    return (one.astype(jnp.float32) + other.astype(jnp.float32)).astype(one.dtype)


class WeightGrad:
    def __init__(self, left_mat, right_mat, second, third):
        sizes = [lax.axis_size(axis) for axis in EVERY]
        if lax.axis_size(second) != 2:
            second, third = third, second
        self.second = second
        self.order = [third, "e2", "e3"]
        self.inner = left_mat.shape[0]
        self.left_rows = left_mat.T.reshape(sizes + [-1, self.inner])
        self.right_mat = right_mat
        self.layout = [axis for axis in EVERY if axis not in ("e0", second)]
        self.one, self.two = lax.axis_index("e0"), lax.axis_index(second)
        self.far = swap(self.piece(1 - self.one, 1 - self.two).astype(jnp.bfloat16), "e0")
        self.near = swap(self.piece(1 - self.one, self.two).astype(jnp.bfloat16), "e0")

    def piece(self, place_one, place_two):
        part = take(self.left_rows, place_one, EVERY.index("e0"))
        part = take(part, place_two, EVERY.index(self.second))
        return dot(part.reshape(-1, self.inner), self.right_mat)

    def send(self):
        far = self.piece(self.one, 1 - self.two) + self.far.astype(jnp.float32)
        self.sent = far.astype(jnp.bfloat16)
        near = self.piece(self.one, self.two) + self.near.astype(jnp.float32)
        self.kept = near.astype(jnp.bfloat16)
        self.axis = self.second
        return self

    def start(self, *gates):
        self.before = self.kept if self.sent is None else self.sent
        if self.sent is not None:
            self.sent = swap(after(self.sent, *gates) if gates else self.sent, self.axis)
        return self

    def step(self, *gates):
        block = self.kept
        if self.sent is not None:
            block = add(block, after(self.sent, *gates) if gates else self.sent)
        if self.axis == self.second:
            share = self.left_rows.shape[5]
            block = block.reshape([lax.axis_size(axis) for axis in self.layout] + [share, -1])
        if not self.order:
            self.total = block.astype(jnp.float32)
            return self
        self.axis = self.order.pop(0)
        at = self.layout.index(self.axis)
        self.layout.pop(at)
        if lax.axis_size(self.axis) == 2:
            place = lax.axis_index(self.axis)
            self.kept, self.sent = take(block, place, at), take(block, 1 - place, at)
        else:
            self.kept = lax.psum_scatter(block, self.axis, scatter_dimension=at, tiled=False)
            self.sent = None
        return self

    def finish(self):
        while self.order:
            self.step().start()
        return self.step().total


def join(mine, other, place, axis_at):
    return jnp.where(
        place == 0,
        jnp.concatenate([mine, other], axis=axis_at),
        jnp.concatenate([other, mine], axis=axis_at),
    )


def gather_halves(both, gate):
    if lax.axis_size("dp") == 2:
        return join(both, after(swap(both, "dp"), gate), lax.axis_index("dp"), 1)
    return lax.all_gather(both, "dp", axis=1, tiled=True)


def local(
    tokens_in,
    out_grad,
    seq_lengths,
    seq_order,
    routes_top,
    norm_gain,
    in_weight,
    conv_weight,
    conv_bias,
    step_bias,
    decay_log,
    skip_gain,
    gated_gain,
    out_weight,
    ffn_gain,
    router_weight,
    expert_gate_up,
    expert_down,
    shared_gate_up,
    shared_down,
):
    group_count = lax.axis_size("dp")
    my_rank = lax.axis_index("dp")
    peers = lax.axis_size(GROUP)
    halves = lax.axis_size("e3")
    device_total = lax.axis_size(EVERY)

    small = [norm_gain, conv_weight, conv_bias, gated_gain, ffn_gain, router_weight]
    small_flat = jnp.concatenate([to_low(v).reshape(1, -1) for v in small], axis=1)
    small_all = tell(small_flat, EVERY)
    smalls = []
    offset = 0
    for v in small:
        smalls.append(
            small_all[:, offset : offset + v.size].reshape((device_total * v.shape[0],) + v.shape[1:])
        )
        offset += v.size
    gain_one, kernel_low, shift_low, gated_scale_low, gain_two, w_router = smalls

    slot_rows = lax.broadcasted_iota(jnp.int32, (group_count, group_count), 0)
    slot_cols = lax.broadcasted_iota(jnp.int32, (group_count, group_count), 1)
    picks = (seq_order[None, :] == slot_rows).astype(jnp.int32)
    inverse = jnp.sum(picks * slot_cols, axis=1)
    my_length = jnp.sum(jnp.where(seq_order == my_rank, seq_lengths, 0))
    dealt_in, dealt_grad = (
        lax.all_to_all(
            jnp.take(block, inverse, axis=0), "dp", split_axis=0, concat_axis=0, tiled=True
        )
        for block in (tokens_in, out_grad)
    )
    model_width = tokens_in.shape[2]
    row_count = dealt_in.shape[0] * dealt_in.shape[1]
    top_count = routes_top.shape[2]
    expert_count = w_router.shape[1]
    positions = lax.broadcasted_iota(jnp.int32, (row_count, 1), 0)
    valid = positions < my_length
    valid_rows = valid.astype(jnp.float32)
    cot_low = jnp.where(valid, dealt_grad.reshape(row_count, model_width), 0)
    row_cot = cot_low.astype(jnp.float32)

    gate_width = gated_gain.shape[0] * device_total
    head_count = step_bias.shape[0]
    pad_heads = ((0, 0), (0, LANES - head_count))
    w_scan = gather_rows(jnp.pad(to_low(in_weight[:, gate_width:]), pad_heads), EVERY)
    w_gate = gather_rows(to_low(in_weight[:, :gate_width]), EVERY)
    routes = routes_top.reshape(row_count, top_count)
    expert_ids = lax.broadcasted_iota(jnp.int32, (1, expert_count), 1)
    chosen = jnp.any(routes[:, :, None] == expert_ids[:, None, :], axis=1)
    routes_all = tell(jnp.where(valid, routes, -1)[None], GROUP)
    up_low, down_low, out_low = lax.optimization_barrier(
        (
            to_low(expert_gate_up),
            to_low(expert_down),
            to_low(out_weight),
            small_all,
            routes_all,
            dealt_in,
        )
    )[:3]
    my_place = lax.axis_index(GROUP)
    mine = my_place + peers * (
        lax.axis_index("e3") ^ lax.broadcasted_iota(jnp.int32, (1, halves, 1, 1), 1)
    )
    member = jnp.any(routes_all[:, None] == mine, axis=3)
    order = (
        jnp.sum(
            (
                member[:, :, None, :]
                & (
                    lax.broadcasted_iota(jnp.int32, (row_count, row_count), 0)
                    >= lax.broadcasted_iota(jnp.int32, (row_count, row_count), 1)
                )
            ).astype(jnp.float32),
            axis=3,
        ).astype(jnp.int32)
        - 1
    )
    capacity = min(row_count, 9 * row_count * top_count // (8 * expert_count))
    capacity = -(-capacity // 32) * 32
    slot_of = jnp.where(member, order, -1)
    slot_ids = lax.broadcasted_iota(jnp.int32, (1, 1, capacity, 1), 2)
    select = (slot_of[:, :, None, :] == slot_ids).astype(jnp.bfloat16)


    w_shared_up = gather_rows(to_low(shared_gate_up), EVERY)
    w_shared_down = gather_rows(to_low(shared_down), EVERY)

    flat_in = dealt_in.reshape(row_count, model_width).astype(jnp.float32)
    normed, norm_one_back = jax.vjp(rms_scale, flat_in, gain_one.astype(jnp.float32))
    normed_low = normed.astype(jnp.bfloat16)
    normed_low = after(normed_low, slot_of)
    mixed = dot(normed_low, w_scan)
    scan_args = (
        kernel_low.astype(jnp.float32).T,
        shift_low.astype(jnp.float32)[None],
        jnp.pad(step_bias[None], pad_heads),
        jnp.pad(decay_log[None], pad_heads),
        jnp.repeat(skip_gain, gate_width // head_count)[None],
        head_spread(head_count, gate_width),
    )
    scanned, before = scan_forward(mixed, *scan_args, BLK)
    up_both = jnp.concatenate([up_low, after(swap(up_low, "e3"), mixed)], axis=0)
    down_both = jnp.concatenate([down_low, after(swap(down_low, "e3"), mixed)], axis=0)
    gate_part = dot(normed_low, w_gate)
    gated_out, gated_back = jax.vjp(
        lambda scan, gate, gain: rms_scale(scan * jax.nn.silu(gate), gain),
        scanned,
        gate_part,
        gated_scale_low.astype(jnp.float32),
    )
    gated_low = gated_out.astype(jnp.bfloat16)
    w_out = spread_rows(out_low, "e1", "dp", (None, None, None, scanned, gated_low))
    middle = flat_in + dot(gated_low, w_out)
    normed_two, norm_two_back = jax.vjp(rms_scale, middle, gain_two.astype(jnp.float32))
    mid_low = normed_two.astype(jnp.bfloat16)

    w_expert_up = gather_halves(up_both, mid_low)
    w_expert_down = gather_halves(down_both, mid_low)

    rows_all = gather_rows(mid_low, GROUP).reshape(peers, row_count, model_width)
    cot_all = gather_rows(after(cot_low, rows_all), GROUP).reshape(peers, row_count, model_width)
    logits = dot(mid_low, w_router)
    masked = jnp.where(chosen, logits, -jnp.inf)
    lifted = jnp.where(chosen, jnp.exp(masked - jnp.max(masked, axis=1, keepdims=True)), 0.0)
    gates = lifted / jnp.sum(lifted, axis=1, keepdims=True)
    by_peer = gates.T.reshape(halves, peers, row_count)
    by_peer = jnp.where(lax.axis_index("e3") == 0, by_peer, by_peer[::-1])
    gates_mine = lax.all_to_all(
        jnp.moveaxis(by_peer, 1, 0), GROUP, split_axis=0, concat_axis=0, tiled=True
    )
    slot_gate = jnp.sum(jnp.where(slot_of[:, :, None, :] == slot_ids, gates_mine[:, :, None, :], 0.0), axis=3)

    def pick(rows):
        return jnp.einsum(
            "sect,std->escd", select, rows, preferred_element_type=jnp.float32
        ).astype(jnp.bfloat16)

    def place(slots):
        return (
            jnp.einsum("sect,escd->std", select, slots, preferred_element_type=jnp.float32)
            .astype(jnp.bfloat16)
            .reshape(peers * row_count, model_width)
        )

    slot_gate = jnp.moveaxis(slot_gate, 1, 0)[..., None]
    expert_in = pick(rows_all)
    expert_pre = jnp.einsum(
        "escd,edf->escf", expert_in, w_expert_up, preferred_element_type=jnp.float32
    )
    expert_full, expert_back = jax.vjp(swiglu, expert_pre)
    expert_act = expert_full.astype(jnp.bfloat16)
    expert_res = jnp.einsum(
        "escf,efd->escd", expert_act, w_expert_down, preferred_element_type=jnp.float32
    ).astype(jnp.bfloat16)
    expert_cot = pick(cot_all).astype(jnp.float32)
    slot_cot = (slot_gate * expert_cot).astype(jnp.bfloat16)
    slot_gate_cot = jnp.sum(expert_cot * expert_res.astype(jnp.float32), axis=3)
    gate_cot_rows = jnp.sum(
        jnp.where(
            slot_of[:, :, None, :] == slot_ids, jnp.moveaxis(slot_gate_cot, 0, 1)[..., None], 0.0
        ),
        axis=2,
    )
    act_cot = jnp.einsum(
        "escd,efd->escf", slot_cot, w_expert_down, preferred_element_type=jnp.float32
    )
    pre_cot = expert_back(act_cot)[0].astype(jnp.bfloat16)
    input_cot = jnp.einsum(
        "escf,edf->escd", pre_cot, w_expert_up, preferred_element_type=jnp.float32
    ).astype(jnp.bfloat16)
    rows_back = scatter_rows(place(input_cot), GROUP)
    gate_cot_back = lax.all_to_all(gate_cot_rows, GROUP, split_axis=0, concat_axis=0, tiled=True)
    gate_cot = jnp.moveaxis(gate_cot_back, 2, 0)
    gate_cot = jnp.where(lax.axis_index("e3") == 0, gate_cot, gate_cot[:, :, ::-1])
    gate_cot = jnp.moveaxis(gate_cot, 2, 1).reshape(row_count, expert_count)
    moe_slots = (slot_gate * expert_res.astype(jnp.float32)).astype(jnp.bfloat16)
    moe_out = scatter_rows(after(place(moe_slots), rows_back), GROUP).astype(jnp.float32)
    grad_down_local = jnp.einsum(
        "escf,escd->efd", expert_act, slot_cot, preferred_element_type=jnp.float32
    ).astype(jnp.bfloat16)
    grad_up_local = jnp.einsum(
        "escd,escf->edf", expert_in, pre_cot, preferred_element_type=jnp.float32
    ).astype(jnp.bfloat16)
    shared_pre = dot(mid_low, w_shared_up)
    shared_full, shared_back = jax.vjp(swiglu, shared_pre)
    shared_act = shared_full.astype(jnp.bfloat16)
    shared_out = dot(shared_act, w_shared_down)
    shared_pre_cot = shared_back(dot_right(cot_low, w_shared_down))[0].astype(jnp.bfloat16)
    shared_in_cot = dot_right(shared_pre_cot, w_shared_up)

    share_down = WeightGrad(shared_act, cot_low, "dp", "e1")
    share_up = WeightGrad(mid_low, shared_pre_cot, "e1", "dp")
    expert_parts = []
    for block in (grad_up_local, grad_down_local):
        block = block.reshape((halves, group_count, -1, block.shape[2]))
        if group_count == 2:
            came = swap(take(block, 1 - my_rank, 1), "dp")
            expert_parts.append((take(block, my_rank, 1), came))
        else:
            block = lax.psum_scatter(block, "dp", scatter_dimension=1, tiled=False)
            expert_parts.append((block, None))

    logit_cot = (gates * (gate_cot - jnp.sum(gates * gate_cot, axis=1, keepdims=True))).astype(
        jnp.bfloat16
    )
    grad_router = dot_left(mid_low, logit_cot)
    shares = [share_down.send().start(rows_back), share_up.send().start(rows_back)]
    mid_cot = rows_back.astype(jnp.float32) + dot_right(logit_cot, w_router) + shared_in_cot
    middle_norm_cot, gain_two_cot = norm_two_back(mid_cot)
    middle_cot = row_cot + middle_norm_cot
    branch_cot = middle_cot.astype(jnp.bfloat16)
    block_out = (
        (valid_rows * (middle + moe_out + shared_out))
        .astype(jnp.bfloat16)
        .reshape(group_count, -1, model_width)
    )
    back_out = lax.all_to_all(block_out, "dp", split_axis=0, concat_axis=0, tiled=True)
    out_half, gate_half = model_width // 2, gate_width // 2
    outs = [
        WeightGrad(gated_low, branch_cot[:, :out_half], "e1", "dp").send().start(),
        WeightGrad(gated_low, branch_cot[:, out_half:], "dp", "e1").send().start(),
    ]
    scan_cot, gate_cot_full, gated_gain_cot = gated_back(dot_right(branch_cot, w_out))
    gate_cot_low = after(gate_cot_full.astype(jnp.bfloat16), *[grad.sent for grad in shares])
    ins = [
        WeightGrad(normed_low, gate_cot_low[:, :gate_half], "e1", "dp").send().start(),
        WeightGrad(normed_low, gate_cot_low[:, gate_half:], "dp", "e1").send().start(),
    ]
    ready = [grad.before for grad in shares + outs + ins]
    mixed_cot, kernel_cot, shift_cot, skip_cot, step_cot, decay_cot = scan_backward(
        mixed, after(scan_cot, *ready), before, *scan_args, BLK
    )
    firsts = shares + outs + ins
    mixed_cot = after(mixed_cot, moe_out, *[grad.sent for grad in outs + ins])
    half_columns = mixed_cot.shape[1] // (2 * LANES) * LANES
    lasts = [
        WeightGrad(normed_low, mixed_cot[:, :half_columns], "e1", "dp").send().start(),
        WeightGrad(normed_low, mixed_cot[:, half_columns:], "dp", "e1").send().start(),
    ]
    gone = [grad.before for grad in lasts]
    expert_sums = [
        kept if came is None else add(kept, after(came, *gone)) for kept, came in expert_parts
    ]
    expert_came = [swap(block[1], "e3") for block in expert_sums]
    for grad in firsts:
        grad.step(*gone).start()
    for grad in lasts:
        grad.step(*[block[1] for block in expert_sums]).start()
    gone = [grad.before for grad in lasts]
    flat_norm_cot, gain_one_cot = norm_one_back(
        dot_right(after(gate_cot_low, *gone), w_gate)
        + dot_right(after(mixed_cot, *gone), w_scan)
    )
    flat_norm_cot = after(flat_norm_cot, *expert_came)
    for grad in firsts:
        grad.step(*gone).start()
    for grad in lasts:
        grad.step().start()
    gone = [grad.before for grad in lasts]
    grad_expert_up, grad_expert_down = (
        add(block[0].astype(jnp.float32), after(came, *gone))[None]
        for block, came in zip(expert_sums, expert_came)
    )
    for grad in firsts:
        grad.step(*gone).start()
    sum_shared_down, sum_shared_up = (grad.finish() for grad in shares)
    sum_out = jnp.concatenate([grad.finish() for grad in outs], axis=1)
    sum_in = jnp.concatenate([grad.finish() for grad in ins + lasts], axis=1)
    sum_in = sum_in[:, : in_weight.shape[1]]
    kernel_cot, shift_cot = kernel_cot.T, shift_cot[0]
    step_cot, decay_cot = step_cot[0, :head_count], decay_cot[0, :head_count]
    skip_cot = jnp.sum(skip_cot.reshape(head_count, -1), axis=1)
    input_grad = (
        (middle_cot + flat_norm_cot).astype(jnp.bfloat16).reshape(group_count, -1, model_width)
    )
    back_grad = lax.all_to_all(input_grad, "dp", split_axis=0, concat_axis=0, tiled=True)

    heads = jnp.concatenate([step_cot, decay_cot, skip_cot])
    small_cots = [gain_one_cot, kernel_cot, shift_cot, gated_gain_cot, gain_two_cot, grad_router]
    parts = [v.reshape(device_total, -1) for v in small_cots]
    parts.append(jnp.broadcast_to(heads[None], (device_total, heads.shape[0])))
    small_came = lax.all_to_all(
        jnp.concatenate(parts, axis=1), EVERY, split_axis=0, concat_axis=0, tiled=True
    )
    small_sum = jnp.sum(after(small_came, *[grad.before for grad in lasts]), axis=0)
    sums = []
    offset = 0
    for v in small:
        sums.append(small_sum[offset : offset + v.size].reshape(v.shape))
        offset += v.size
    head_sums = small_sum[offset:].reshape(3, head_count)
    final_out = jnp.take(back_out, seq_order, axis=0)
    final_grad = jnp.take(back_grad, seq_order, axis=0)
    return (
        final_out,
        final_grad,
        sums[0],
        sum_in,
        sums[1],
        sums[2],
        head_sums[0],
        head_sums[1],
        head_sums[2],
        sums[3],
        sum_out,
        sums[4],
        sums[5],
        grad_expert_up,
        grad_expert_down,
        sum_shared_up,
        sum_shared_down,
    )


def solution(mesh):
    fine = Mesh(
        mesh.devices.reshape((mesh.shape["dp"], 2, 2, 2, mesh.shape["expert"] // 8)), EVERY
    )
    rows = P(SPLIT, "dp", None)
    flat = P(EVERY)
    split = P(EVERY, None)
    in_specs = (
        rows,
        rows,
        P(SPLIT),
        P(SPLIT),
        P(EVERY, None, None),
        flat,
        split,
        split,
        flat,
        P(),
        P(),
        P(),
        flat,
        split,
        flat,
        split,
        rows,
        rows,
        split,
        split,
    )
    out_specs = (
        rows,
        rows,
        flat,
        split,
        split,
        flat,
        P(),
        P(),
        P(),
        flat,
        split,
        flat,
        split,
        rows,
        rows,
        split,
        split,
    )
    return jax.shard_map(local, mesh=fine, in_specs=in_specs, out_specs=out_specs, check_vma=False)
```

time: 1890 us -> 1330 us (0.70)
  waiting for transfers between devices: 996 us -> 528 us
  matrix products: 434 us -> 319 us
  Pallas kernels: 0 us -> 112 us
  other arithmetic: 215 us -> 148 us
  starting transfers between devices: 21.2 us -> 83 us
  blocking collectives: 69.2 us -> 11.8 us
  local copies, waits for them, and re-layouts: 130 us -> 104 us
    reduce_scatter x8 -> x2, waiting for transfers between devices: 577 us -> 0.01 us  [scatter_rows(): return lax.psum_scatter(block, axes, scatter_dimension=0, tiled=True)]
    ppermute x0 -> x61, waiting for transfers between devices: none -> 452 us  [swap(): return lax.ppermute(block, axis, [(0, 1), (1, 0)])]
    all_gather x8 -> x6, waiting for transfers between devices: 270 us -> 0.04 us  [gather_rows(): return lax.all_gather(block, axes, axis=0, tiled=True)]
    unnamed x18 -> x8, waiting for transfers between devices: 126 us -> 0.13 us
    dot_general x12 -> x1, matrix products: 146 us -> 21.7 us  [local(): jnp.einsum('escf,edf->escd', pre_cot, w_expert_up, preferred_element_type...]
    pallas_call x0 -> x2, Pallas kernels: none -> 112 us  [the longest x1 74.6 us: scan_backward(): pl.pallas_call(partial(scan_back_kernel, width=taps.shape[0]), grid=(bloc...]
    dot_general x5 -> x38, matrix products: 41.9 us -> 113 us  [dot(): return jnp.dot(left_mat, right_mat, preferred_element_type=jnp.float32)]
    all_gather x3 -> x0, blocking collectives: 69.2 us -> none  [gather_rows(): return lax.all_gather(block, axes, axis=0, tiled=True)]
  transfers between devices with their start and end apart: 22 -> 77, of which waited for: 13 -> 27; matrix products, arithmetic and copies ran while one was open for 40% -> 41% of each run, Pallas kernels for 0% -> 8%
where the time goes in v2:
time: 1330 us; the launch traced here: 1320 us
  waiting for transfers between devices  528 us (40%)
  matrix products  319 us (24%)
  other arithmetic  148 us (11%)
  Pallas kernels  112 us (8%)
  local copies, waits for them, and re-layouts  104 us (8%)
  starting transfers between devices  83 us (6%)
  between operations  16.8 us (1%)
    ppermute x61, waiting for transfers between devices, swap(): return lax.ppermute(block, axis, [(0, 1), (1, 0)])  452 us
    dot_general x38, matrix products, dot(): return jnp.dot(left_mat, right_mat, preferred_element_type=jnp.float32)  113 us
    pallas_call x1, Pallas kernels, scan_backward(): pl.pallas_call(partial(scan_back_kernel, width=taps.shape[0]), grid=(bloc...  74.6 us
    all_to_all x2, waiting for transfers between devices, local(): lax.all_to_all(jnp.take(block, inverse, axis=0), 'dp', split_axis=0, conc...  53 us
    ppermute x61, starting transfers between devices, swap(): return lax.ppermute(block, axis, [(0, 1), (1, 0)])  50.6 us
    dot_general x6, matrix products, dot_right(): lax.dot_general(left_mat, right_mat, (((1,), (1,)), ((), ())), preferred_...  47.6 us
    pallas_call x1, Pallas kernels, scan_forward(): pl.pallas_call(partial(scan_kernel, width=taps.shape[0]), grid=(blocks,),...  37.8 us
    convert_element_type x28, other arithmetic, add(): (one.astype(jnp.float32) + other.astype(jnp.float32)).astype(one.dtype)  32.4 us
  transfers between devices with their start and end apart: 77, of which 27 were waited for; matrix products, arithmetic and copies ran while one was open for 41% of the time, Pallas kernels for 8%

profile of v2, /device:TPU:0, one launch (start us, length us, event | category | flops | bytes accessed | tf_op | source)
XLA Modules:
  0.0 1322.8 jit_solution(5847520069428786584)
XLA Ops:
  16.4 4.2 all-to-all-start.4
  21.4 21.7 %all-to-all-done.4 = bf16[2,256,1536]{2,1,0:T(8,128)(2,1)S(1)} async-done(((bf16[2,256,1536]{2,1,0:T(8,128)(2,1)}), bf16[2,256,1536]{2,1,0:T(8,128)(2,1)S(1)}, u32[]{:S(2)}, u32[]{:S(2)}) %all-to-all-start.4) | async-done | bytes 1572896 | tf_op jit(solution)/shard_map/all_to_all | solution.py:605
  45.6 4.0 all-to-all-start.2
  52.3 3.6 all-to-all-done.2
  55.9 11.8 all_to_all.56
  67.7 3.9 all-to-all-start
  77.0 31.3 %all-to-all-done = bf16[2,256,1536]{2,1,0:T(8,128)(2,1)S(1)} async-done(((bf16[2,256,1536]{2,1,0:T(8,128)(2,1)}), bf16[2,256,1536]{2,1,0:T(8,128)(2,1)S(1)}, u32[]{:S(2)}, u32[]{:S(2)}) %all-to-all-start) | async-done | bytes 1572896 | tf_op jit(solution)/shard_map/all_to_all | solution.py:605
  108.6 23.9 %collective-permute-done = bf16[1,1,1,1,1,96,1536]{6,5,4,3,2,1,0:T(8,128)(2,1)S(1)} collective-permute-done((bf16[1,1,1,1,1,96,1536]{6,5,4,3,2,1,0:T(8,128)(2,1)S(1)}, bf16[1,1,1,1,1,96,1536]{6,5,4,3,2,1,0:T(8,128)(2,1)S(1)}, u32[]{:S(2)}, u32[]{:S(2)}) %collective-permute-start) | collective-permute-done | bytes 294944 | tf_op jit(solution)/shard_map/ppermute | solution.py:439
  136.6 18.4 %collective-permute-done.1 = bf16[1,2,1,1,1,96,1536]{6,5,4,3,2,1,0:T(8,128)(2,1)S(1)} collective-permute-done((bf16[1,2,1,1,1,96,1536]{6,5,4,3,2,1,0:T(8,128)(2,1)}, bf16[1,2,1,1,1,96,1536]{6,5,4,3,2,1,0:T(8,128)(2,1)S(1)}, u32[]{:S(2)}, u32[]{:S(2)}) %collective-permute-start.1) | collective-permute-done | bytes 589856 | tf_op jit(solution)/shard_map/ppermute | solution.py:439
  163.2 22.8 %collective-permute-done.2 = bf16[1,2,2,1,1,96,1536]{6,5,4,3,2,1,0:T(8,128)(2,1)} collective-permute-done((bf16[1,2,2,1,1,96,1536]{6,5,4,3,2,1,0:T(8,128)(2,1)}, bf16[1,2,2,1,1,96,1536]{6,5,4,3,2,1,0:T(8,128)(2,1)}, u32[]{:S(2)}, u32[]{:S(2)}) %collective-permute-start.2) | collective-permute-done | bytes 1179680 | tf_op jit(solution)/shard_map/ppermute | solution.py:439
  185.9 3.5 fusion.67
  195.0 12.3 fusion.172.mixed.halo
  207.3 37.8 %scan_forward.1 = (f32[512,3072]{1,0:T(8,128)}, f32[4,128,3072]{2,1,0:T(8,128)}) custom-call(f32[512,3456]{1,0:T(8,128)} %fusion.172.mixed.halo, f32[4,3328]{1,0:T(4,128)S(1)} %bitcast.462, f32[1,3328]{1,0:T(1,128)S(1)} %reshape.1352.shift, f32[1,128]{1,0:T(1,128)S(1)} %pad.24.bias, f32[1,128]{1,0:T(1,128)S(1)} %pad.25.decay, ...), custom_call_target="tpu_custom_call" | custom-call | flops 1000000000 | bytes 120000000 | tf_op jit(solution)/shard_map/scan_forward/pallas_call | solution.py:294
  245.1 17.8 %collective-permute-done.3 = bf16[2,2,2,1,1,96,1536]{6,5,4,3,2,1,0:T(8,128)(2,1)} collective-permute-done((bf16[2,2,2,1,1,96,1536]{6,5,4,3,2,1,0:T(8,128)(2,1)}, bf16[2,2,2,1,1,96,1536]{6,5,4,3,2,1,0:T(8,128)(2,1)}, u32[]{:S(2)}, u32[]{:S(2)}) %collective-permute-start.3) | collective-permute-done | bytes 2359328 | tf_op jit(solution)/shard_map/ppermute | solution.py:439
  262.8 5.5 maximum_select_fusion.2
  268.6 11.4 multiply_reduce_fusion.2
  281.1 8.8 maximum_select_fusion
  289.9 5.2 multiply_reduce_fusion.5
  300.9 70.2 %collective-permute-done.5 = bf16[1,768,1024]{2,1,0:T(8,128)(2,1)S(1)} collective-permute-done((bf16[1,768,1024]{2,1,0:T(8,128)(2,1)S(1)}, bf16[1,768,1024]{2,1,0:T(8,128)(2,1)S(1)}, u32[]{:S(2)}, u32[]{:S(2)}) %collective-permute-start.5) | collective-permute-done | bytes 1572896 | tf_op jit(solution)/shard_map/ppermute | solution.py:439
  379.0 32.7 %collective-permute-done.7 = bf16[1,256,1536]{2,1,0:T(8,128)(2,1)S(1)} collective-permute-done((bf16[1,256,1536]{2,1,0:T(8,128)(2,1)S(1)}, bf16[1,256,1536]{2,1,0:T(8,128)(2,1)S(1)}, u32[]{:S(2)}, u32[]{:S(2)}) %collective-permute-start.7) | collective-permute-done | bytes 786464 | tf_op jit(solution)/shard_map/ppermute | solution.py:439
  412.8 11.4 convolution_convert_fusion.2
  424.3 20.9 %collective-permute-done.6 = bf16[2,768,1024]{2,1,0:T(8,128)(2,1)} collective-permute-done((bf16[2,768,1024]{2,1,0:T(8,128)(2,1)}, bf16[2,768,1024]{2,1,0:T(8,128)(2,1)}, u32[]{:S(2)}, u32[]{:S(2)}) %collective-permute-start.6) | collective-permute-done | bytes 3145760 | tf_op jit(solution)/shard_map/ppermute | solution.py:439
  445.1 42.5 %collective-permute-done.8 = bf16[2,256,1536]{2,1,0:T(8,128)(2,1)} collective-permute-done((bf16[2,256,1536]{2,1,0:T(8,128)(2,1)}, bf16[2,256,1536]{2,1,0:T(8,128)(2,1)}, u32[]{:S(2)}, u32[]{:S(2)}) %collective-permute-start.8) | collective-permute-done | bytes 1572896 | tf_op jit(solution)/shard_map/ppermute | solution.py:439
  493.4 11.3 fusion.6
  504.7 22.9 %fusion.4 = f32[2,8,224,1024]{3,2,1,0:T(8,128)} fusion(bf16[2,8,224,1536]{3,2,0,1:T(8,128)(2,1)} %fusion.6, bf16[2,768,1024]{2,1,0:T(8,128)(2,1)} %collective-permute-done.6, bf16[2,768,1024]{2,1,0:T(8,128)(2,1)} %constant_dynamic-update-slice_fusion, pred[]{:T(512)S(6)} %eq.49), kind=kOutput, calls=%fused_computation.18 | convolution fusion | flops 11302600704 | bytes 31981568 | tf_op jit(solution)/shard_map/escd,edf->escf/dot_general | solution.py:726
  527.6 7.8 multiply_convert_fusion
  535.4 14.1 %fusion.1 = (f32[2,8,224]{2,1,0:T(8,128)S(1)}, bf16[2,8,224,1536]{3,2,1,0:T(8,128)(2,1)}) fusion(bf16[8,1536,2,224]{1,3,0,2:T(8,128)(2,1)} %convolution_convert_fusion.2, bf16[2,8,224,512]{3,2,1,0:T(8,128)(2,1)} %multiply_convert_fusion, bf16[2,256,1536]{2,1,0:T(8,128)(2,1)} %collective-permute-done.8, ...), kind=kOutput, calls=%fused_computation.9 | convolution fusion | flops 5678821888 | bytes 28850176 | tf_op jit(solution)/shard_map/escf,efd->escd/dot_general | solution.py:731
  552.8 17.7 %fusion.99 = (f32[2,8,224,512]{3,2,1,0:T(8,128)}, f32[2,8,224,512]{3,2,1,0:T(8,128)}) fusion(f32[2,8,224,1024]{3,2,1,0:T(8,128)} %fusion.4, bf16[2,256,1536]{2,1,0:T(8,128)(2,1)} %collective-permute-done.8, bf16[2,256,1536]{2,1,0:T(8,128)(2,1)} %constant_dynamic-update-slice_fusion.2, pred[]{:T(512)S(6)} %eq.49, ...), kind=kOutput, calls=%fused_computation.208 | convolution fusion | flops 5689835520 | bytes 43530240 | tf_op jit(solution)/shard_map/escd,efd->escf/dot_general | solution.py:743
  570.5 21.7 %convolution_convert_fusion = bf16[2,8,224,1536]{3,2,0,1:T(8,128)(2,1)} fusion(bf16[2,768,1024]{2,1,0:T(8,128)(2,1)} %collective-permute-done.6, bf16[2,768,1024]{2,1,0:T(8,128)(2,1)} %constant_dynamic-update-slice_fusion, pred[]{:T(512)S(6)} %eq.49, f32[2,8,224,512]{3,2,1,0:T(8,128)} %get-tuple-element.201, f32[2,8,224,512]{3,2,1,0:T(8,128)} %get-tuple-element.200), kind=kOutput, calls=%fused_computation.14 | convolution fusion | flops 11315445760 | bytes 31981568 | tf_op jit(solution)/shard_map/escf,edf->escd/dot_general | solution.py:747
  592.3 14.1 %bitcast_convert_fusion = bf16[8,512,1536]{2,1,0:T(8,128)(2,1)} fusion(bf16[2,8,224,1536]{3,2,0,1:T(8,128)(2,1)} %convolution_convert_fusion, s32[8,2,512]{2,1,0:T(2,128)S(1)} %copy.218), kind=kOutput, calls=%fused_computation.6 | convolution fusion | flops 5645271040 | bytes 23625728 | tf_op jit(solution)/shard_map/sect,escd->std/dot_general | solution.py:719
  614.1 5.5 fusion.251
  626.4 8.7 fusion.173
  635.2 7.8 fusion.133
  668.5 5.1 fusion.174
  678.5 4.1 all-to-all-start.6
  682.6 20.1 %bitcast_convert_fusion.2 = bf16[2,1536,1024]{2,1,0:T(8,128)(2,1)} fusion(bf16[2,8,224,1536]{3,2,0,1:T(8,128)(2,1)} %fusion.6, f32[2,8,224,512]{3,2,1,0:T(8,128)} %get-tuple-element.201, f32[2,8,224,512]{3,2,1,0:T(8,128)} %get-tuple-element.200), kind=kOutput, calls=%fused_computation.16 | convolution fusion | flops 11284774912 | bytes 31981568 | tf_op jit(solution)/shard_map/escd,escf->edf/dot_general | solution.py:760
  702.7 3.9 dynamic-slice_bitcast_fusion
  708.9 12.7 bitcast_convert_fusion.1
  721.5 9.5 bitcast_convert_fusion.3
  745.0 4.4 multiply_reduce_fusion.3
  752.5 10.6 multiply_reduce_fusion
  769.4 14.7 %fusion.44 = (f32[512,3072]{1,0:T(8,128)}, bf16[512,3072]{1,0:T(8,128)(2,1)S(1)}) fusion(f32[512,3072]{1,0:T(8,128)} %copy-done.10, f32[512]{0:T(512)S(1)} %multiply_multiply_fusion.1, f32[512,3072]{1,0:T(8,128)} %get-tuple-element.274, f32[3072]{0:T(1024)S(1)} %copy-done.107, f32[512]{0:T(512)S(1)} %copy-done.121, f32[512,3072]{1,0:T(8,128)} %get-tuple-element.266, ...), kind=kLoop, calls=%fused_computation.92 | loop fusion | flops 28311552 | bytes 34619392 | tf_op jit(solution)/shard_map/transpose(jvp())/mul | solution.py:685
  786.6 8.0 collective-permute-done.10
  794.5 42.8 %collective-permute-done.12 = bf16[384,2048]{1,0:T(8,128)(2,1)} collective-permute-done((bf16[384,2048]{1,0:T(8,128)(2,1)}, bf16[384,2048]{1,0:T(8,128)(2,1)}, u32[]{:S(2)}, u32[]{:S(2)}) %collective-permute-start.12) | collective-permute-done | bytes 1572896 | tf_op jit(solution)/shard_map/ppermute | solution.py:439
  850.1 3.8 collective-permute-start.18
  861.5 3.7 fusion.118
  868.9 74.6 %scan_backward.1 = (bf16[512,3456]{1,0:T(8,128)(2,1)}, f32[4,3328]{1,0:T(4,128)}, f32[1,3328]{1,0:T(1,128)}, f32[1,3072]{1,0:T(1,128)}, f32[1,128]{1,0:T(1,128)}, /*index=5*/f32[1,128]{1,0:T(1,128)}) custom-call(f32[512,3456]{1,0:T(8,128)} %fusion.172.mixed.halo, f32[512,3456]{1,0:T(8,128)} %fusion.172.mixed.halo, f32[512,3072]{1,0:T(8,128)} %get-tuple-element.85.y_cot, ...), custom_call_target="tpu_custom_call" | custom-call | flops 2000000000 | bytes 240000000 | tf_op jit(solution)/shard_map/scan_backward/pallas_call | solution.py:341
  945.6 6.2 collective-permute-done.19
  1010.5 3.8 fusion.21
  1019.6 6.7 collective-permute-done.23
  1040.6 9.4 fusion.175
  1050.2 10.3 fusion.42
  1091.9 84.4 %collective-permute-done.30 = bf16[256,1536]{1,0:T(8,128)(2,1)} collective-permute-done((bf16[256,1536]{1,0:T(8,128)(2,1)}, bf16[256,1536]{1,0:T(8,128)(2,1)}, u32[]{:S(2)}, u32[]{:S(2)}) %collective-permute-start.30) | collective-permute-done | bytes 786464 | tf_op jit(solution)/shard_map/ppermute | solution.py:439
  1180.7 4.8 all-to-all-start.7
  1200.4 10.2 collective-permute-done.55
  1210.7 8.9 collective-permute-done.59
  1222.6 3.7 fusion.36
  1229.4 9.7 collective-permute-done.60
  1243.5 12.1 collective-permute-done.48
  1274.6 4.4 collective-permute-done.44
  1280.6 5.6 fusion.45
  1286.3 3.8 all-to-all-start.5
  1291.3 18.5 %all-to-all-done.5 = bf16[2,256,1536]{2,1,0:T(8,128)(2,1)S(1)} async-done(((bf16[2,256,1536]{2,1,0:T(8,128)(2,1)}), bf16[2,256,1536]{2,1,0:T(8,128)(2,1)S(1)}, u32[]{:S(2)}, u32[]{:S(2)}) %all-to-all-start.5) | async-done | bytes 1572896 | tf_op jit(solution)/shard_map/all_to_all | solution.py:796
  1311.8 3.9 broadcast_select_fusion
  (724 shorter events, 324.3 us)
Async XLA Ops:
  7.2 187.7 %all-gather.7.cloned.1.call-start = ((), (), s32[]{:S(2)}) async-start(), calls=%async_computation.11 | async-start | bytes 10948608 | tf_op jit(solution)/shard_map/all_gather | solution.py:417
  9.6 259.0 %all-gather.9.cloned.1.call-start = ((), (), s32[]{:S(2)}) async-start(), calls=%async_computation.12 | async-start | bytes 9732096 | tf_op jit(solution)/shard_map/all_gather | solution.py:417
  16.4 26.8 %all-to-all-start.4 = ((bf16[2,256,1536]{2,1,0:T(8,128)(2,1)}), bf16[2,256,1536]{2,1,0:T(8,128)(2,1)S(1)}, u32[]{:S(2)}, u32[]{:S(2)}) async-start(bf16[2,256,1536]{2,1,0:T(8,128)(2,1)} %get-tuple-element.264), calls=%async_computation.4 | async-start | bytes 3145728 | tf_op jit(solution)/shard_map/all_to_all | solution.py:605
  20.7 392.2 %all-gather.13.cloned.1.call-start = ((), (), s32[]{:S(2)}) async-start(), calls=%async_computation.14 | async-start | bytes 14155776 | tf_op jit(solution)/shard_map/all_gather | solution.py:417
  67.7 40.6 %all-to-all-start = ((bf16[2,256,1536]{2,1,0:T(8,128)(2,1)}), bf16[2,256,1536]{2,1,0:T(8,128)(2,1)S(1)}, u32[]{:S(2)}, u32[]{:S(2)}) async-start(bf16[2,256,1536]{2,1,0:T(8,128)(2,1)} %get-tuple-element.265), calls=%async_computation | async-start | bytes 3145728 | tf_op jit(solution)/shard_map/all_to_all | solution.py:605
  71.6 421.7 %all-gather.11.cloned.1.call-start = ((), (), s32[]{:S(2)}) async-start(), calls=%async_computation.13 | async-start | bytes 14155776 | tf_op jit(solution)/shard_map/all_gather | solution.py:417
  108.2 24.3 %collective-permute-start = (bf16[1,1,1,1,1,96,1536]{6,5,4,3,2,1,0:T(8,128)(2,1)S(1)}, bf16[1,1,1,1,1,96,1536]{6,5,4,3,2,1,0:T(8,128)(2,1)S(1)}, u32[]{:S(2)}, u32[]{:S(2)}) collective-permute-start(bf16[1,1,1,1,1,96,1536]{6,5,4,3,2,1,0:T(8,128)(2,1)S(1)} %bitcast.497), channel_id=1, source_target_pairs={{0,8},{8,0},{1,9},{9,1},{2,10},{10,2},{3,11},{11,3},{4,12},{12,4},... | collective-permute-start | bytes 884744 | tf_op jit(solution)/shard_map/ppermute | solution.py:439
  134.2 20.8 %collective-permute-start.1 = (bf16[1,2,1,1,1,96,1536]{6,5,4,3,2,1,0:T(8,128)(2,1)}, bf16[1,2,1,1,1,96,1536]{6,5,4,3,2,1,0:T(8,128)(2,1)S(1)}, u32[]{:S(2)}, u32[]{:S(2)}) collective-permute-start(bf16[1,2,1,1,1,96,1536]{6,5,4,3,2,1,0:T(8,128)(2,1)} %maximum_select_fusion.10), channel_id=1, source_target_pairs={{0,4},{4,0},{1,5},{5,1},{2,6},{6,2},{3,7},{7,3},{8,12},{12,8},{9,1... | collective-permute-start | bytes 1769480 | tf_op jit(solution)/shard_map/ppermute | solution.py:439
  156.3 29.6 %collective-permute-start.2 = (bf16[1,2,2,1,1,96,1536]{6,5,4,3,2,1,0:T(8,128)(2,1)}, bf16[1,2,2,1,1,96,1536]{6,5,4,3,2,1,0:T(8,128)(2,1)}, u32[]{:S(2)}, u32[]{:S(2)}) collective-permute-start(bf16[1,2,2,1,1,96,1536]{6,5,4,3,2,1,0:T(8,128)(2,1)} %maximum_select_fusion.6), channel_id=1, source_target_pairs={{0,16},{16,0},{1,17},{17,1},{2,18},{18,2},{3,19},{19,3},{4,20},{20... | collective-permute-start | bytes 3538952 | tf_op jit(solution)/shard_map/ppermute | solution.py:439
  189.4 73.5 %collective-permute-start.3 = (bf16[2,2,2,1,1,96,1536]{6,5,4,3,2,1,0:T(8,128)(2,1)}, bf16[2,2,2,1,1,96,1536]{6,5,4,3,2,1,0:T(8,128)(2,1)}, u32[]{:S(2)}, u32[]{:S(2)}) collective-permute-start(bf16[2,2,2,1,1,96,1536]{6,5,4,3,2,1,0:T(8,128)(2,1)} %fusion.67), channel_id=1, source_target_pairs={{0,2},{2,0},{1,3},{3,1},{4,6},{6,4},{5,7},{7,5},{8,10},{10,8},{9,1... | collective-permute-start | bytes 7077896 | tf_op jit(solution)/shard_map/ppermute | solution.py:439
  298.3 328.1 %all-gather.15.cloned.1.call-start = ((), (), s32[]{:S(2)}) async-start(), calls=%async_computation.17 | async-start | bytes 6488064 | tf_op jit(solution)/shard_map/all_gather | solution.py:417
  299.5 335.7 %all-gather.17.cloned.1.call-start = ((), (), s32[]{:S(2)}) async-start(), calls=%async_computation.18 | async-start | bytes 3244032 | tf_op jit(solution)/shard_map/all_gather | solution.py:417
  299.5 71.6 %collective-permute-start.5 = (bf16[1,768,1024]{2,1,0:T(8,128)(2,1)S(1)}, bf16[1,768,1024]{2,1,0:T(8,128)(2,1)S(1)}, u32[]{:S(2)}, u32[]{:S(2)}) collective-permute-start(bf16[1,768,1024]{2,1,0:T(8,128)(2,1)S(1)} %copy-done.33), channel_id=1, source_target_pairs={{0,8},{8,0},{1,9},{9,1},{2,10},{10,2},{3,11},{11,3},{4,12},{12,4},... | collective-permute-start | bytes 4718600 | tf_op jit(solution)/shard_map/ppermute | solution.py:439
  372.4 72.7 %collective-permute-start.6 = (bf16[2,768,1024]{2,1,0:T(8,128)(2,1)}, bf16[2,768,1024]{2,1,0:T(8,128)(2,1)}, u32[]{:S(2)}, u32[]{:S(2)}) collective-permute-start(bf16[2,768,1024]{2,1,0:T(8,128)(2,1)} %constant_dynamic-update-slice_fusion), channel_id=1, source_target_pairs={{0,16},{16,0},{1,17},{17,1},{2,18},{18,2},{3,19},{19,3},{4,20},{20... | collective-permute-start | bytes 9437192 | tf_op jit(solution)/shard_map/ppermute | solution.py:439
  375.2 36.4 %collective-permute-start.7 = (bf16[1,256,1536]{2,1,0:T(8,128)(2,1)S(1)}, bf16[1,256,1536]{2,1,0:T(8,128)(2,1)S(1)}, u32[]{:S(2)}, u32[]{:S(2)}) collective-permute-start(bf16[1,256,1536]{2,1,0:T(8,128)(2,1)S(1)} %copy-done.43), channel_id=1, source_target_pairs={{0,8},{8,0},{1,9},{9,1},{2,10},{10,2},{3,11},{11,3},{4,12},{12,4},... | collective-permute-start | bytes 2359304 | tf_op jit(solution)/shard_map/ppermute | solution.py:439
  412.6 75.1 %collective-permute-start.8 = (bf16[2,256,1536]{2,1,0:T(8,128)(2,1)}, bf16[2,256,1536]{2,1,0:T(8,128)(2,1)}, u32[]{:S(2)}, u32[]{:S(2)}) collective-permute-start(bf16[2,256,1536]{2,1,0:T(8,128)(2,1)} %constant_dynamic-update-slice_fusion.2), channel_id=1, source_target_pairs={{0,16},{16,0},{1,17},{17,1},{2,18},{18,2},{3,19},{19,3},{4,20},{20... | collective-permute-start | bytes 4718600 | tf_op jit(solution)/shard_map/ppermute | solution.py:439
  489.8 59.8 %all-to-all-start.3 = ((f32[8,2,512]{2,1,0:T(2,128)}), f32[8,2,512]{2,1,0:T(2,128)S(1)}, u32[]{:S(2)}, u32[]{:S(2)}) async-start(f32[8,2,512]{2,1,0:T(2,128)} %select_bitcast_fusion.1), calls=%async_computation.3 | async-start | bytes 65536 | tf_op jit(solution)/shard_map/all_to_all | solution.py:707
  493.1 251.9 %reduce-scatter.3.cloned.1.call-start = ((), (), s32[]{:S(2)}) async-start(), calls=%async_computation.15 | async-start | bytes 14155776 | tf_op jit(solution)/shard_map/reduce_scatter | solution.py:431
  650.4 23.3 %collective-permute-start.9 = (bf16[256,1536]{1,0:T(8,128)(2,1)}, bf16[256,1536]{1,0:T(8,128)(2,1)}, u32[]{:S(2)}, u32[]{:S(2)}) collective-permute-start(bf16[256,1536]{1,0:T(8,128)(2,1)} %convolution_convert_fusion.15), channel_id=1, source_target_pairs={{0,1},{1,0},{2,3},{3,2},{4,5},{5,4},{6,7},{7,6},{8,9},{9,8},{10,11... | collective-permute-start | bytes 2359304 | tf_op jit(solution)/shard_map/ppermute | solution.py:439
  678.5 55.5 %all-to-all-start.6 = ((f32[8,2,512]{2,1,0:T(2,128)}), f32[8,2,512]{2,1,0:T(2,128)}, u32[]{:S(2)}, u32[]{:S(2)}) async-start(f32[8,2,512]{2,1,0:T(2,128)} %get-tuple-element.196), calls=%async_computation.8 | async-start | bytes 65536 | tf_op jit(solution)/shard_map/all_to_all | solution.py:751
  682.6 598.1 %reduce-scatter.5.cloned.1.call-start = ((), (), s32[]{:S(2)}) async-start(), calls=%async_computation.16 | async-start | bytes 14155776 | tf_op jit(solution)/shard_map/reduce_scatter | solution.py:431
  706.6 279.1 %collective-permute-start.24 = (bf16[2,768,1024]{2,1,0:T(8,128)(2,1)}, bf16[2,768,1024]{2,1,0:T(8,128)(2,1)}, u32[]{:S(2)}, u32[]{:S(2)}) collective-permute-start(bf16[2,768,1024]{2,1,0:T(8,128)(2,1)} %dynamic-slice_bitcast_fusion), channel_id=1, source_target_pairs={{0,16},{16,0},{1,17},{17,1},{2,18},{18,2},{3,19},{19,3},{4,20},{20... | collective-permute-start | bytes 9437192 | tf_op jit(solution)/shard_map/ppermute | solution.py:439
  763.1 31.4 %collective-permute-start.10 = (bf16[256,1536]{1,0:T(8,128)(2,1)}, bf16[256,1536]{1,0:T(8,128)(2,1)}, u32[]{:S(2)}, u32[]{:S(2)}) collective-permute-start(bf16[256,1536]{1,0:T(8,128)(2,1)} %add_convert_fusion.14), channel_id=1, source_target_pairs={{0,16},{16,0},{1,17},{17,1},{2,18},{18,2},{3,19},{19,3},{4,20},{20... | collective-permute-start | bytes 2359304 | tf_op jit(solution)/shard_map/ppermute | solution.py:439
  763.4 73.9 %collective-permute-start.12 = (bf16[384,2048]{1,0:T(8,128)(2,1)}, bf16[384,2048]{1,0:T(8,128)(2,1)}, u32[]{:S(2)}, u32[]{:S(2)}) collective-permute-start(bf16[384,2048]{1,0:T(8,128)(2,1)} %add_convert_fusion.5), channel_id=1, source_target_pairs={{0,2},{2,0},{1,3},{3,1},{4,6},{6,4},{5,7},{7,5},{8,10},{10,8},{9,1... | collective-permute-start | bytes 4718600 | tf_op jit(solution)/shard_map/ppermute | solution.py:439
  767.0 74.3 %collective-permute-start.13 = (bf16[768,768]{1,0:T(8,128)(2,1)}, bf16[768,768]{1,0:T(8,128)(2,1)}, u32[]{:S(2)}, u32[]{:S(2)}) collective-permute-start(bf16[768,768]{1,0:T(8,128)(2,1)} %convolution_convert_fusion.19), channel_id=1, source_target_pairs={{0,1},{1,0},{2,3},{3,2},{4,5},{5,4},{6,7},{7,6},{8,9},{9,8},{10,11... | collective-permute-start | bytes 3538952 | tf_op jit(solution)/shard_map/ppermute | solution.py:439
  768.8 78.2 %collective-permute-start.14 = (bf16[768,768]{1,0:T(8,128)(2,1)}, bf16[768,768]{1,0:T(8,128)(2,1)}, u32[]{:S(2)}, u32[]{:S(2)}) collective-permute-start(bf16[768,768]{1,0:T(8,128)(2,1)} %convolution_convert_fusion.18), channel_id=1, source_target_pairs={{0,1},{1,0},{2,3},{3,2},{4,5},{5,4},{6,7},{7,6},{8,9},{9,8},{10,11... | collective-permute-start | bytes 3538952 | tf_op jit(solution)/shard_map/ppermute | solution.py:439
  844.5 99.0 %collective-permute-start.17 = (bf16[768,768]{1,0:T(8,128)(2,1)}, bf16[768,768]{1,0:T(8,128)(2,1)}, u32[]{:S(2)}, u32[]{:S(2)}) collective-permute-start(bf16[768,768]{1,0:T(8,128)(2,1)} %add_convert_fusion.11), channel_id=1, source_target_pairs={{0,2},{2,0},{1,3},{3,1},{4,6},{6,4},{5,7},{7,5},{8,10},{10,8},{9,1... | collective-permute-start | bytes 3538952 | tf_op jit(solution)/shard_map/ppermute | solution.py:439
  850.1 95.5 %collective-permute-start.18 = (bf16[768,768]{1,0:T(8,128)(2,1)}, bf16[768,768]{1,0:T(8,128)(2,1)}, u32[]{:S(2)}, u32[]{:S(2)}) collective-permute-start(bf16[768,768]{1,0:T(8,128)(2,1)} %add_convert_fusion.10), channel_id=1, source_target_pairs={{0,16},{16,0},{1,17},{17,1},{2,18},{18,2},{3,19},{19,3},{4,20},{20... | collective-permute-start | bytes 3538952 | tf_op jit(solution)/shard_map/ppermute | solution.py:439
  855.7 96.1 %collective-permute-start.19 = (bf16[384,1536]{1,0:T(8,128)(2,1)}, bf16[384,1536]{1,0:T(8,128)(2,1)}, u32[]{:S(2)}, u32[]{:S(2)}) collective-permute-start(bf16[384,1536]{1,0:T(8,128)(2,1)} %fusion.46), channel_id=1, source_target_pairs={{0,2},{2,0},{1,3},{3,1},{4,6},{6,4},{5,7},{7,5},{8,10},{10,8},{9,1... | collective-permute-start | bytes 3538952 | tf_op jit(solution)/shard_map/ppermute | solution.py:439
  857.6 94.2 %collective-permute-start.20 = (bf16[384,1536]{1,0:T(8,128)(2,1)}, bf16[384,1536]{1,0:T(8,128)(2,1)}, u32[]{:S(2)}, u32[]{:S(2)}) collective-permute-start(bf16[384,1536]{1,0:T(8,128)(2,1)} %fusion.47), channel_id=1, source_target_pairs={{0,16},{16,0},{1,17},{17,1},{2,18},{18,2},{3,19},{19,3},{4,20},{20... | collective-permute-start | bytes 3538952 | tf_op jit(solution)/shard_map/ppermute | solution.py:439
  943.5 42.7 %collective-permute-start.26 = (bf16[2,256,1536]{2,1,0:T(8,128)(2,1)}, bf16[2,256,1536]{2,1,0:T(8,128)(2,1)}, u32[]{:S(2)}, u32[]{:S(2)}) collective-permute-start(bf16[2,256,1536]{2,1,0:T(8,128)(2,1)} %dynamic-slice_bitcast_fusion.1), channel_id=1, source_target_pairs={{0,16},{16,0},{1,17},{17,1},{2,18},{18,2},{3,19},{19,3},{4,20},{20... | collective-permute-start | bytes 4718600 | tf_op jit(solution)/shard_map/ppermute | solution.py:439
  945.6 36.4 %collective-permute-start.39 = (bf16[384,1536]{1,0:T(8,128)(2,1)}, bf16[384,1536]{1,0:T(8,128)(2,1)}, u32[]{:S(2)}, u32[]{:S(2)}) collective-permute-start(bf16[384,1536]{1,0:T(8,128)(2,1)} %convolution_convert_fusion.4), channel_id=1, source_target_pairs={{0,1},{1,0},{2,3},{3,2},{4,5},{5,4},{6,7},{7,6},{8,9},{9,8},{10,11... | collective-permute-start | bytes 3538952 | tf_op jit(solution)/shard_map/ppermute | solution.py:439
  955.2 20.0 %collective-permute-start.22 = (bf16[384,1664]{1,0:T(8,128)(2,1)}, bf16[384,1664]{1,0:T(8,128)(2,1)}, u32[]{:S(2)}, u32[]{:S(2)}) collective-permute-start(bf16[384,1664]{1,0:T(8,128)(2,1)} %convolution_convert_fusion.6), channel_id=1, source_target_pairs={{0,1},{1,0},{2,3},{3,2},{4,5},{5,4},{6,7},{7,6},{8,9},{9,8},{10,11... | collective-permute-start | bytes 3833864 | tf_op jit(solution)/shard_map/ppermute | solution.py:439
  957.2 21.8 %collective-permute-start.25 = (bf16[384,1792]{1,0:T(8,128)(2,1)}, bf16[384,1792]{1,0:T(8,128)(2,1)}, u32[]{:S(2)}, u32[]{:S(2)}) collective-permute-start(bf16[384,1792]{1,0:T(8,128)(2,1)} %convolution_convert_fusion.11), channel_id=1, source_target_pairs={{0,1},{1,0},{2,3},{3,2},{4,5},{5,4},{6,7},{7,6},{8,9},{9,8},{10,11... | collective-permute-start | bytes 4128776 | tf_op jit(solution)/shard_map/ppermute | solution.py:439
  986.2 21.2 %collective-permute-start.57 = (bf16[256,1536]{1,0:T(8,128)(2,1)S(1)}, bf16[256,1536]{1,0:T(8,128)(2,1)S(1)}, u32[]{:S(2)}, u32[]{:S(2)}) collective-permute-start(bf16[256,1536]{1,0:T(8,128)(2,1)S(1)} %copy-done.71), channel_id=1, source_target_pairs={{0,1},{1,0},{2,3},{3,2},{4,5},{5,4},{6,7},{7,6},{8,9},{9,8},{10,11... | collective-permute-start | bytes 2359304 | tf_op jit(solution)/shard_map/ppermute | solution.py:439
  987.1 41.6 %collective-permute-start.21 = (bf16[384,1664]{1,0:T(8,128)(2,1)S(1)}, bf16[384,1664]{1,0:T(8,128)(2,1)}, u32[]{:S(2)}, u32[]{:S(2)}) collective-permute-start(bf16[384,1664]{1,0:T(8,128)(2,1)S(1)} %convolution_convert_fusion.7), channel_id=1, source_target_pairs={{0,1},{1,0},{2,3},{3,2},{4,5},{5,4},{6,7},{7,6},{8,9},{9,8},{10,11... | collective-permute-start | bytes 3833864 | tf_op jit(solution)/shard_map/ppermute | solution.py:439
  991.6 44.5 %collective-permute-start.27 = (bf16[384,1792]{1,0:T(8,128)(2,1)S(1)}, bf16[384,1792]{1,0:T(8,128)(2,1)S(1)}, u32[]{:S(2)}, u32[]{:S(2)}) collective-permute-start(bf16[384,1792]{1,0:T(8,128)(2,1)S(1)} %convolution_convert_fusion.10), channel_id=1, source_target_pairs={{0,1},{1,0},{2,3},{3,2},{4,5},{5,4},{6,7},{7,6},{8,9},{9,8},{10,11... | collective-permute-start | bytes 4128776 | tf_op jit(solution)/shard_map/ppermute | solution.py:439
  995.1 31.2 %collective-permute-start.23 = (bf16[384,1664]{1,0:T(8,128)(2,1)}, bf16[384,1664]{1,0:T(8,128)(2,1)}, u32[]{:S(2)}, u32[]{:S(2)}) collective-permute-start(bf16[384,1664]{1,0:T(8,128)(2,1)} %fusion.59), channel_id=1, source_target_pairs={{0,2},{2,0},{1,3},{3,1},{4,6},{6,4},{5,7},{7,5},{8,10},{10,8},{9,1... | collective-permute-start | bytes 3833864 | tf_op jit(solution)/shard_map/ppermute | solution.py:439
  1000.5 34.6 %collective-permute-start.28 = (bf16[384,1792]{1,0:T(8,128)(2,1)S(1)}, bf16[384,1792]{1,0:T(8,128)(2,1)S(1)}, u32[]{:S(2)}, u32[]{:S(2)}) collective-permute-start(bf16[384,1792]{1,0:T(8,128)(2,1)S(1)} %fusion.50), channel_id=1, source_target_pairs={{0,16},{16,0},{1,17},{17,1},{2,18},{18,2},{3,19},{19,3},{4,20},{20... | collective-permute-start | bytes 4128776 | tf_op jit(solution)/shard_map/ppermute | solution.py:439
  1007.4 59.5 %collective-permute-start.40 = (bf16[2,2,48,1536]{3,2,0,1:T(8,128)(2,1)}, bf16[2,2,48,1536]{3,2,0,1:T(8,128)(2,1)}, u32[]{:S(2)}, u32[]{:S(2)}) collective-permute-start(bf16[2,2,48,1536]{3,2,0,1:T(8,128)(2,1)} %bitcast.455), channel_id=1, source_target_pairs={{0,2},{2,0},{1,3},{3,1},{4,6},{6,4},{5,7},{7,5},{8,10},{10,8},{9,1... | collective-permute-start | bytes 1769480 | tf_op jit(solution)/shard_map/ppermute | solution.py:439
  1026.3 43.3 %collective-permute-start.36 = (bf16[2,2,48,1536]{3,2,0,1:T(8,128)(2,1)}, bf16[2,2,48,1536]{3,2,0,1:T(8,128)(2,1)}, u32[]{:S(2)}, u32[]{:S(2)}) collective-permute-start(bf16[2,2,48,1536]{3,2,0,1:T(8,128)(2,1)} %bitcast.456), channel_id=1, source_target_pairs={{0,16},{16,0},{1,17},{17,1},{2,18},{18,2},{3,19},{19,3},{4,20},{20... | collective-permute-start | bytes 1769480 | tf_op jit(solution)/shard_map/ppermute | solution.py:439
  1028.7 41.2 %collective-permute-start.50 = (bf16[2,2,96,768]{3,2,0,1:T(8,128)(2,1)}, bf16[2,2,96,768]{3,2,0,1:T(8,128)(2,1)}, u32[]{:S(2)}, u32[]{:S(2)}) collective-permute-start(bf16[2,2,96,768]{3,2,0,1:T(8,128)(2,1)} %bitcast.453), channel_id=1, source_target_pairs={{0,2},{2,0},{1,3},{3,1},{4,6},{6,4},{5,7},{7,5},{8,10},{10,8},{9,1... | collective-permute-start | bytes 1769480 | tf_op jit(solution)/shard_map/ppermute | solution.py:439
  1035.2 36.4 %collective-permute-start.54 = (bf16[2,2,48,2048]{3,2,0,1:T(8,128)(2,1)}, bf16[2,2,48,2048]{3,2,0,1:T(8,128)(2,1)}, u32[]{:S(2)}, u32[]{:S(2)}) collective-permute-start(bf16[2,2,48,2048]{3,2,0,1:T(8,128)(2,1)} %bitcast.450), channel_id=1, source_target_pairs={{0,16},{16,0},{1,17},{17,1},{2,18},{18,2},{3,19},{19,3},{4,20},{20... | collective-permute-start | bytes 2359304 | tf_op jit(solution)/shard_map/ppermute | solution.py:439
  1036.2 35.7 %collective-permute-start.58 = (bf16[2,2,32,1536]{3,2,0,1:T(8,128)(2,1)}, bf16[2,2,32,1536]{3,2,0,1:T(8,128)(2,1)}, u32[]{:S(2)}, u32[]{:S(2)}) collective-permute-start(bf16[2,2,32,1536]{3,2,0,1:T(8,128)(2,1)} %bitcast.457), channel_id=1, source_target_pairs={{0,2},{2,0},{1,3},{3,1},{4,6},{6,4},{5,7},{7,5},{8,10},{10,8},{9,1... | collective-permute-start | bytes 1179656 | tf_op jit(solution)/shard_map/ppermute | solution.py:439
  1063.6 117.1 %all-to-all-start.8 = ((f32[32,1,1624]{2,1,0:T(1,128)}), f32[32,1,1624]{2,1,0:T(1,128)}, u32[]{:S(2)}, u32[]{:S(2)}) async-start(f32[32,1,1624]{2,1,0:T(1,128)} %copy.239), calls=%async_computation.10 | async-start | bytes 425984 | tf_op jit(solution)/shard_map/all_to_all | solution.py:861
  1066.9 109.4 %collective-permute-start.29 = (bf16[768,1024]{1,0:T(8,128)(2,1)}, bf16[768,1024]{1,0:T(8,128)(2,1)}, u32[]{:S(2)}, u32[]{:S(2)}) collective-permute-start(bf16[768,1024]{1,0:T(8,128)(2,1)} %slice_bitcast_fusion.1), channel_id=1, source_target_pairs={{0,8},{8,0},{1,9},{9,1},{2,10},{10,2},{3,11},{11,3},{4,12},{12,4},... | collective-permute-start | bytes 4718600 | tf_op jit(solution)/shard_map/ppermute | solution.py:439
  1069.6 106.7 %collective-permute-start.30 = (bf16[256,1536]{1,0:T(8,128)(2,1)}, bf16[256,1536]{1,0:T(8,128)(2,1)}, u32[]{:S(2)}, u32[]{:S(2)}) collective-permute-start(bf16[256,1536]{1,0:T(8,128)(2,1)} %slice_bitcast_fusion.3), channel_id=1, source_target_pairs={{0,8},{8,0},{1,9},{9,1},{2,10},{10,2},{3,11},{11,3},{4,12},{12,4},... | collective-permute-start | bytes 2359304 | tf_op jit(solution)/shard_map/ppermute | solution.py:439
  1069.9 17.2 %collective-permute-start.46 = (bf16[2,2,96,768]{3,2,0,1:T(8,128)(2,1)}, bf16[2,2,96,768]{3,2,0,1:T(8,128)(2,1)S(1)}, u32[]{:S(2)}, u32[]{:S(2)}) collective-permute-start(bf16[2,2,96,768]{3,2,0,1:T(8,128)(2,1)} %bitcast.522), channel_id=1, source_target_pairs={{0,16},{16,0},{1,17},{17,1},{2,18},{18,2},{3,19},{19,3},{4,20},{20... | collective-permute-start | bytes 1769480 | tf_op jit(solution)/shard_map/ppermute | solution.py:439
  1071.6 115.7 %collective-permute-start.31 = (bf16[2,2,48,1664]{3,2,0,1:T(8,128)(2,1)}, bf16[2,2,48,1664]{3,2,0,1:T(8,128)(2,1)}, u32[]{:S(2)}, u32[]{:S(2)}) collective-permute-start(bf16[2,2,48,1664]{3,2,0,1:T(8,128)(2,1)} %bitcast.521), channel_id=1, source_target_pairs={{0,16},{16,0},{1,17},{17,1},{2,18},{18,2},{3,19},{19,3},{4,20},{20... | collective-permute-start | bytes 1916936 | tf_op jit(solution)/shard_map/ppermute | solution.py:439
  1071.9 117.0 %collective-permute-start.33 = (bf16[2,2,48,1792]{3,2,0,1:T(8,128)(2,1)}, bf16[2,2,48,1792]{3,2,0,1:T(8,128)(2,1)}, u32[]{:S(2)}, u32[]{:S(2)}) collective-permute-start(bf16[2,2,48,1792]{3,2,0,1:T(8,128)(2,1)} %bitcast.520), channel_id=1, source_target_pairs={{0,2},{2,0},{1,3},{3,1},{4,6},{6,4},{5,7},{7,5},{8,10},{10,8},{9,1... | collective-permute-start | bytes 2064392 | tf_op jit(solution)/shard_map/ppermute | solution.py:439
  1087.1 106.1 %collective-permute-start.41 = (bf16[2,48,1536]{2,1,0:T(8,128)(2,1)}, bf16[2,48,1536]{2,1,0:T(8,128)(2,1)}, u32[]{:S(2)}, u32[]{:S(2)}) collective-permute-start(bf16[2,48,1536]{2,1,0:T(8,128)(2,1)} %dynamic-slice_bitcast_fusion.7), channel_id=1, source_target_pairs={{0,4},{4,0},{1,5},{5,1},{2,6},{6,2},{3,7},{7,3},{8,12},{12,8},{9,1... | collective-permute-start | bytes 884744 | tf_op jit(solution)/shard_map/ppermute | solution.py:439
  1176.3 16.9 %collective-permute-start.37 = (bf16[2,48,1536]{2,1,0:T(8,128)(2,1)}, bf16[2,48,1536]{2,1,0:T(8,128)(2,1)}, u32[]{:S(2)}, u32[]{:S(2)}) collective-permute-start(bf16[2,48,1536]{2,1,0:T(8,128)(2,1)} %dynamic-slice_bitcast_fusion.8), channel_id=1, source_target_pairs={{0,4},{4,0},{1,5},{5,1},{2,6},{6,2},{3,7},{7,3},{8,12},{12,8},{9,1... | collective-permute-start | bytes 884744 | tf_op jit(solution)/shard_map/ppermute | solution.py:439
  1176.3 18.9 %collective-permute-start.51 = (bf16[2,96,768]{2,1,0:T(8,128)(2,1)}, bf16[2,96,768]{2,1,0:T(8,128)(2,1)}, u32[]{:S(2)}, u32[]{:S(2)}) collective-permute-start(bf16[2,96,768]{2,1,0:T(8,128)(2,1)} %dynamic-slice_bitcast_fusion.5), channel_id=1, source_target_pairs={{0,4},{4,0},{1,5},{5,1},{2,6},{6,2},{3,7},{7,3},{8,12},{12,8},{9,1... | collective-permute-start | bytes 884744 | tf_op jit(solution)/shard_map/ppermute | solution.py:439
  1180.7 83.1 %all-to-all-start.7 = ((bf16[2,256,1536]{2,1,0:T(8,128)(2,1)}), bf16[2,256,1536]{2,1,0:T(8,128)(2,1)}, u32[]{:S(2)}, u32[]{:S(2)}) async-start(bf16[2,256,1536]{2,1,0:T(8,128)(2,1)} %bitcast.485), calls=%async_computation.9 | async-start | bytes 3145728 | tf_op jit(solution)/shard_map/all_to_all | solution.py:855
  1188.9 21.7 %collective-permute-start.55 = (bf16[2,48,2048]{2,1,0:T(8,128)(2,1)S(1)}, bf16[2,48,2048]{2,1,0:T(8,128)(2,1)S(1)}, u32[]{:S(2)}, u32[]{:S(2)}) collective-permute-start(bf16[2,48,2048]{2,1,0:T(8,128)(2,1)S(1)} %copy-done.85), channel_id=1, source_target_pairs={{0,4},{4,0},{1,5},{5,1},{2,6},{6,2},{3,7},{7,3},{8,12},{12,8},{9,1... | collective-permute-start | bytes 1179656 | tf_op jit(solution)/shard_map/ppermute | solution.py:439
  1193.1 26.5 %collective-permute-start.59 = (bf16[2,32,1536]{2,1,0:T(8,128)(2,1)S(1)}, bf16[2,32,1536]{2,1,0:T(8,128)(2,1)S(1)}, u32[]{:S(2)}, u32[]{:S(2)}) collective-permute-start(bf16[2,32,1536]{2,1,0:T(8,128)(2,1)S(1)} %copy-done.105), channel_id=1, source_target_pairs={{0,4},{4,0},{1,5},{5,1},{2,6},{6,2},{3,7},{7,3},{8,12},{12,8},{9,1... | collective-permute-start | bytes 589832 | tf_op jit(solution)/shard_map/ppermute | solution.py:439
  1193.2 33.8 %collective-permute-start.32 = (bf16[2,48,1664]{2,1,0:T(8,128)(2,1)S(1)}, bf16[2,48,1664]{2,1,0:T(8,128)(2,1)S(1)}, u32[]{:S(2)}, u32[]{:S(2)}) collective-permute-start(bf16[2,48,1664]{2,1,0:T(8,128)(2,1)S(1)} %dynamic-slice_bitcast_fusion.4), channel_id=1, source_target_pairs={{0,4},{4,0},{1,5},{5,1},{2,6},{6,2},{3,7},{7,3},{8,12},{12,8},{9,1... | collective-permute-start | bytes 958472 | tf_op jit(solution)/shard_map/ppermute | solution.py:439
  1195.2 71.9 %collective-permute-start.34 = (bf16[2,48,1792]{2,1,0:T(8,128)(2,1)}, bf16[2,48,1792]{2,1,0:T(8,128)(2,1)}, u32[]{:S(2)}, u32[]{:S(2)}) collective-permute-start(bf16[2,48,1792]{2,1,0:T(8,128)(2,1)} %dynamic-slice_bitcast_fusion.3), channel_id=1, source_target_pairs={{0,4},{4,0},{1,5},{5,1},{2,6},{6,2},{3,7},{7,3},{8,12},{12,8},{9,1... | collective-permute-start | bytes 1032200 | tf_op jit(solution)/shard_map/ppermute | solution.py:439
  1199.1 40.7 %collective-permute-start.42 = (bf16[48,1536]{1,0:T(8,128)(2,1)S(1)}, bf16[48,1536]{1,0:T(8,128)(2,1)S(1)}, u32[]{:S(2)}, u32[]{:S(2)}) collective-permute-start(bf16[48,1536]{1,0:T(8,128)(2,1)S(1)} %dynamic-slice_bitcast_fusion.15), channel_id=1, source_target_pairs={{0,8},{8,0},{1,9},{9,1},{2,10},{10,2},{3,11},{11,3},{4,12},{12,4},... | collective-permute-start | bytes 442376 | tf_op jit(solution)/shard_map/ppermute | solution.py:439
  1210.7 44.9 %collective-permute-start.38 = (bf16[48,1536]{1,0:T(8,128)(2,1)S(1)}, bf16[48,1536]{1,0:T(8,128)(2,1)S(1)}, u32[]{:S(2)}, u32[]{:S(2)}) collective-permute-start(bf16[48,1536]{1,0:T(8,128)(2,1)S(1)} %dynamic-slice_bitcast_fusion.16), channel_id=1, source_target_pairs={{0,8},{8,0},{1,9},{9,1},{2,10},{10,2},{3,11},{11,3},{4,12},{12,4},... | collective-permute-start | bytes 442376 | tf_op jit(solution)/shard_map/ppermute | solution.py:439
  1219.6 23.8 %collective-permute-start.52 = (bf16[96,768]{1,0:T(8,128)(2,1)S(1)}, bf16[96,768]{1,0:T(8,128)(2,1)S(1)}, u32[]{:S(2)}, u32[]{:S(2)}) collective-permute-start(bf16[96,768]{1,0:T(8,128)(2,1)S(1)} %dynamic-slice_bitcast_fusion.13), channel_id=1, source_target_pairs={{0,8},{8,0},{1,9},{9,1},{2,10},{10,2},{3,11},{11,3},{4,12},{12,4},... | collective-permute-start | bytes 442376 | tf_op jit(solution)/shard_map/ppermute | solution.py:439
  1239.8 19.9 %collective-permute-start.56 = (bf16[48,2048]{1,0:T(8,128)(2,1)S(1)}, bf16[48,2048]{1,0:T(8,128)(2,1)S(1)}, u32[]{:S(2)}, u32[]{:S(2)}) collective-permute-start(bf16[48,2048]{1,0:T(8,128)(2,1)S(1)} %dynamic-slice_bitcast_fusion.10), channel_id=1, source_target_pairs={{0,8},{8,0},{1,9},{9,1},{2,10},{10,2},{3,11},{11,3},{4,12},{12,4},... | collective-permute-start | bytes 589832 | tf_op jit(solution)/shard_map/ppermute | solution.py:439
  1243.4 19.7 %collective-permute-start.43 = (bf16[48,1664]{1,0:T(8,128)(2,1)S(1)}, bf16[48,1664]{1,0:T(8,128)(2,1)S(1)}, u32[]{:S(2)}, u32[]{:S(2)}) collective-permute-start(bf16[48,1664]{1,0:T(8,128)(2,1)S(1)} %dynamic-slice_bitcast_fusion.12), channel_id=1, source_target_pairs={{0,8},{8,0},{1,9},{9,1},{2,10},{10,2},{3,11},{11,3},{4,12},{12,4},... | collective-permute-start | bytes 479240 | tf_op jit(solution)/shard_map/ppermute | solution.py:439
  1286.3 23.5 %all-to-all-start.5 = ((bf16[2,256,1536]{2,1,0:T(8,128)(2,1)}), bf16[2,256,1536]{2,1,0:T(8,128)(2,1)S(1)}, u32[]{:S(2)}, u32[]{:S(2)}) async-start(bf16[2,256,1536]{2,1,0:T(8,128)(2,1)} %bitcast.500), calls=%async_computation.7 | async-start | bytes 3145728 | tf_op jit(solution)/shard_map/all_to_all | solution.py:796
  (181 other events, 3970.8 us)
Sparse Core Ops, SparseCore 0:
  11.5 121.7 all-gather.6
  136.7 98.2 all-gather.8
  236.7 70.1 all-gather.12
  309.0 111.2 all-gather.10
  423.5 76.0 all-gather.14
  502.9 60.1 all-gather.16
  606.5 121.7 reduce-scatter.2
  769.5 193.5 reduce-scatter.4

commit v3 on v2

--- a/solution.py
+++ b/solution.py
@@ -626,16 +626,10 @@
     expert_ids = lax.broadcasted_iota(jnp.int32, (1, expert_count), 1)
     chosen = jnp.any(routes[:, :, None] == expert_ids[:, None, :], axis=1)
     routes_all = tell(jnp.where(valid, routes, -1)[None], GROUP)
-    up_low, down_low, out_low = lax.optimization_barrier(
-        (
-            to_low(expert_gate_up),
-            to_low(expert_down),
-            to_low(out_weight),
-            small_all,
-            routes_all,
-            dealt_in,
-        )
-    )[:3]
+    out_low = to_low(out_weight)
+    up_low, down_low = lax.optimization_barrier(
+        (to_low(expert_gate_up), to_low(expert_down), small_all, routes_all, dealt_in)
+    )[:2]
     my_place = lax.axis_index(GROUP)
     mine = my_place + peers * (
         lax.axis_index("e3") ^ lax.broadcasted_iota(jnp.int32, (1, halves, 1, 1), 1)
@@ -687,7 +681,7 @@
         gate_part,
         gated_scale_low.astype(jnp.float32),
     )
-    gated_low = gated_out.astype(jnp.bfloat16)
+    gated_low = after(gated_out.astype(jnp.bfloat16), up_both, down_both)
     w_out = spread_rows(out_low, "e1", "dp", (None, None, None, scanned, gated_low))
     middle = flat_in + dot(gated_low, w_out)
     normed_two, norm_two_back = jax.vjp(rms_scale, middle, gain_two.astype(jnp.float32))
@@ -805,32 +799,36 @@
         WeightGrad(normed_low, gate_cot_low[:, :gate_half], "e1", "dp").send().start(),
         WeightGrad(normed_low, gate_cot_low[:, gate_half:], "dp", "e1").send().start(),
     ]
-    ready = [grad.before for grad in shares + outs + ins]
+    (up_kept, up_came), down_part = expert_parts
+    up_sum = up_kept if up_came is None else add(up_kept, after(up_came, scan_cot))
+    up_came = swap(up_sum[1], "e3")
+    ready = [grad.before for grad in shares + outs + ins] + [up_sum[1]]
     mixed_cot, kernel_cot, shift_cot, skip_cot, step_cot, decay_cot = scan_backward(
         mixed, after(scan_cot, *ready), before, *scan_args, BLK
     )
     firsts = shares + outs + ins
-    mixed_cot = after(mixed_cot, moe_out, *[grad.sent for grad in outs + ins])
+    mixed_cot = after(mixed_cot, moe_out, up_came, *[grad.sent for grad in outs + ins])
     half_columns = mixed_cot.shape[1] // (2 * LANES) * LANES
     lasts = [
         WeightGrad(normed_low, mixed_cot[:, :half_columns], "e1", "dp").send().start(),
         WeightGrad(normed_low, mixed_cot[:, half_columns:], "dp", "e1").send().start(),
     ]
     gone = [grad.before for grad in lasts]
-    expert_sums = [
-        kept if came is None else add(kept, after(came, *gone)) for kept, came in expert_parts
-    ]
-    expert_came = [swap(block[1], "e3") for block in expert_sums]
+    down_kept, down_came = down_part
+    down_sum = down_kept if down_came is None else add(down_kept, after(down_came, *gone))
+    expert_sums = [up_sum, down_sum]
+    down_came = swap(down_sum[1], "e3")
+    expert_came = [up_came, down_came]
     for grad in firsts:
         grad.step(*gone).start()
     for grad in lasts:
-        grad.step(*[block[1] for block in expert_sums]).start()
+        grad.step(down_sum[1]).start()
     gone = [grad.before for grad in lasts]
     flat_norm_cot, gain_one_cot = norm_one_back(
         dot_right(after(gate_cot_low, *gone), w_gate)
         + dot_right(after(mixed_cot, *gone), w_scan)
     )
-    flat_norm_cot = after(flat_norm_cot, *expert_came)
+    flat_norm_cot = after(flat_norm_cot, down_came)
     for grad in firsts:
         grad.step(*gone).start()
     for grad in lasts:

time: 1330 us -> 1200 us (0.902)
  waiting for transfers between devices: 528 us -> 393 us
  local copies, waits for them, and re-layouts: 104 us -> 122 us
    ppermute x61, waiting for transfers between devices: 452 us -> 340 us  [swap(): return lax.ppermute(block, axis, [(0, 1), (1, 0)])]
    all_to_all x2, waiting for transfers between devices: 53 us -> 24.4 us  [local(): lax.all_to_all(jnp.take(block, inverse, axis=0), 'dp', split_axis=0, conc...]
  transfers between devices with their start and end apart: 77 -> 78, of which waited for: 27 -> 25; matrix products, arithmetic and copies ran while one was open for 41% -> 46% of each run, Pallas kernels for 8% -> 9%
where the time goes in v3:
time: 1200 us; the launch traced here: 1190 us
  waiting for transfers between devices  393 us (33%)
  matrix products  316 us (26%)
  other arithmetic  143 us (12%)
  local copies, waits for them, and re-layouts  122 us (10%)
  Pallas kernels  112 us (9%)
  starting transfers between devices  91.9 us (8%)
  between operations  17 us (1%)
    ppermute x61, waiting for transfers between devices, swap(): return lax.ppermute(block, axis, [(0, 1), (1, 0)])  340 us
    dot_general x38, matrix products, dot(): return jnp.dot(left_mat, right_mat, preferred_element_type=jnp.float32)  106 us
    pallas_call x1, Pallas kernels, scan_backward(): pl.pallas_call(partial(scan_back_kernel, width=taps.shape[0]), grid=(bloc...  74.5 us
    ppermute x61, starting transfers between devices, swap(): return lax.ppermute(block, axis, [(0, 1), (1, 0)])  55.9 us
    dot_general x6, matrix products, dot_right(): lax.dot_general(left_mat, right_mat, (((1,), (1,)), ((), ())), preferred_...  49.7 us
    pallas_call x1, Pallas kernels, scan_forward(): pl.pallas_call(partial(scan_kernel, width=taps.shape[0]), grid=(blocks,),...  37.6 us
    convert_element_type x28, other arithmetic, add(): (one.astype(jnp.float32) + other.astype(jnp.float32)).astype(one.dtype)  29.7 us
    dot_general x2, matrix products, place(): jnp.einsum('sect,escd->std', select, slots, preferred_element_type=jnp.fl...  27.5 us
  transfers between devices with their start and end apart: 78, of which 25 were waited for; matrix products, arithmetic and copies ran while one was open for 46% of the time, Pallas kernels for 9%

profile of v3, /device:TPU:0, one launch (start us, length us, event | category | flops | bytes accessed | tf_op | source)
XLA Modules:
  0.0 1194.9 jit_solution(10292335273049551664)
XLA Ops:
  15.3 4.4 all-to-all-start.4
  21.5 20.6 %all-to-all-done.4 = bf16[2,256,1536]{2,1,0:T(8,128)(2,1)S(1)} async-done(((bf16[2,256,1536]{2,1,0:T(8,128)(2,1)}), bf16[2,256,1536]{2,1,0:T(8,128)(2,1)S(1)}, u32[]{:S(2)}, u32[]{:S(2)}) %all-to-all-start.4) | async-done | bytes 1572896 | tf_op jit(solution)/shard_map/all_to_all | solution.py:605
  53.1 21.4 %collective-permute-done.2 = bf16[1,1,1,1,1,96,1536]{6,5,4,3,2,1,0:T(8,128)(2,1)S(1)} collective-permute-done((bf16[1,1,1,1,1,96,1536]{6,5,4,3,2,1,0:T(8,128)(2,1)S(1)}, bf16[1,1,1,1,1,96,1536]{6,5,4,3,2,1,0:T(8,128)(2,1)S(1)}, u32[]{:S(2)}, u32[]{:S(2)}) %collective-permute-start.2) | collective-permute-done | bytes 294944 | tf_op jit(solution)/shard_map/ppermute | solution.py:439
  81.1 3.7 all-to-all-start
  87.9 19.2 %collective-permute-done.3 = bf16[1,2,1,1,1,96,1536]{6,5,4,3,2,1,0:T(8,128)(2,1)S(1)} collective-permute-done((bf16[1,2,1,1,1,96,1536]{6,5,4,3,2,1,0:T(8,128)(2,1)}, bf16[1,2,1,1,1,96,1536]{6,5,4,3,2,1,0:T(8,128)(2,1)S(1)}, u32[]{:S(2)}, u32[]{:S(2)}) %collective-permute-start.3) | collective-permute-done | bytes 589856 | tf_op jit(solution)/shard_map/ppermute | solution.py:439
  114.0 3.7 all-to-all-done
  118.4 3.8 all-to-all-start.2
  125.6 16.9 %collective-permute-done.4 = bf16[1,2,2,1,1,96,1536]{6,5,4,3,2,1,0:T(8,128)(2,1)} collective-permute-done((bf16[1,2,2,1,1,96,1536]{6,5,4,3,2,1,0:T(8,128)(2,1)}, bf16[1,2,2,1,1,96,1536]{6,5,4,3,2,1,0:T(8,128)(2,1)}, u32[]{:S(2)}, u32[]{:S(2)}) %collective-permute-start.4) | collective-permute-done | bytes 1179680 | tf_op jit(solution)/shard_map/ppermute | solution.py:439
  154.2 12.1 %fusion.172.mixed.halo = f32[512,3456]{1,0:T(8,128)} fusion(bf16[512,1536]{1,0:T(8,128)(2,1)} %fusion.41, bf16[1536,3456]{1,0:T(8,128)(2,1)} %all-gather.7.cloned.1.call-done), kind=kOutput, calls=%fused_computation.427 | convolution fusion | flops 5435817984 | bytes 19267584 | tf_op jit(solution)/shard_map/dot_general | solution.py:435
  166.3 37.6 %scan_forward.1 = (f32[512,3072]{1,0:T(8,128)}, f32[4,128,3072]{2,1,0:T(8,128)}) custom-call(f32[512,3456]{1,0:T(8,128)} %fusion.172.mixed.halo, f32[4,3328]{1,0:T(4,128)S(1)} %bitcast.463, f32[1,3328]{1,0:T(1,128)S(1)} %reshape.1352.shift, f32[1,128]{1,0:T(1,128)S(1)} %pad.24.bias, f32[1,128]{1,0:T(1,128)S(1)} %pad.25.decay, ...), custom_call_target="tpu_custom_call" | custom-call | flops 1000000000 | bytes 120000000 | tf_op jit(solution)/shard_map/scan_forward/pallas_call | solution.py:294
  204.0 5.5 maximum_select_fusion.2
  217.3 56.4 %collective-permute-done = bf16[1,768,1024]{2,1,0:T(8,128)(2,1)} collective-permute-done((bf16[1,768,1024]{2,1,0:T(8,128)(2,1)}, bf16[1,768,1024]{2,1,0:T(8,128)(2,1)}, u32[]{:S(2)}, u32[]{:S(2)}) %collective-permute-start) | collective-permute-done | bytes 1572896 | tf_op jit(solution)/shard_map/ppermute | solution.py:439
  273.8 19.1 %collective-permute-done.1 = bf16[1,256,1536]{2,1,0:T(8,128)(2,1)S(1)} collective-permute-done((bf16[1,256,1536]{2,1,0:T(8,128)(2,1)}, bf16[1,256,1536]{2,1,0:T(8,128)(2,1)S(1)}, u32[]{:S(2)}, u32[]{:S(2)}) %collective-permute-start.1) | collective-permute-done | bytes 786464 | tf_op jit(solution)/shard_map/ppermute | solution.py:439
  295.7 12.6 %multiply_reduce_fusion.2 = (f32[512]{0:T(512)S(1)}, f32[512,3072]{1,0:T(8,128)S(1)}, f32[512,3072]{1,0:T(8,128)}) fusion(f32[512,3072]{1,0:T(8,128)} %get-tuple-element.70, bf16[512,1536]{1,0:T(8,128)(2,1)S(1)} %copy-done.34, bf16[1536,3072]{1,0:T(8,128)(2,1)} %all-gather.9.cloned.1.call-done), kind=kOutput, calls=%fused_computation.53 | convolution fusion | flops 4842847744 | bytes 29886464 | tf_op jit(solution)/shard_map/dot_general | solution.py:435
  309.9 10.1 maximum_select_fusion
  320.0 5.2 multiply_reduce_fusion.5
  337.3 10.0 all-gather.13.cloned.1.call-done
  347.3 11.6 convolution_convert_fusion.2
  364.9 36.0 %collective-permute-done.7 = bf16[2,768,1024]{2,1,0:T(8,128)(2,1)} collective-permute-done((bf16[2,768,1024]{2,1,0:T(8,128)(2,1)}, bf16[2,768,1024]{2,1,0:T(8,128)(2,1)}, u32[]{:S(2)}, u32[]{:S(2)}) %collective-permute-start.7) | collective-permute-done | bytes 3145760 | tf_op jit(solution)/shard_map/ppermute | solution.py:439
  400.9 33.8 %collective-permute-done.8 = bf16[2,256,1536]{2,1,0:T(8,128)(2,1)} collective-permute-done((bf16[2,256,1536]{2,1,0:T(8,128)(2,1)}, bf16[2,256,1536]{2,1,0:T(8,128)(2,1)}, u32[]{:S(2)}, u32[]{:S(2)}) %collective-permute-start.8) | collective-permute-done | bytes 1572896 | tf_op jit(solution)/shard_map/ppermute | solution.py:439
  434.7 11.4 fusion.6
  446.1 22.8 %fusion.4 = f32[2,8,224,1024]{3,2,1,0:T(8,128)} fusion(bf16[2,8,224,1536]{3,2,0,1:T(8,128)(2,1)} %fusion.6, bf16[2,768,1024]{2,1,0:T(8,128)(2,1)} %collective-permute-done.7, bf16[2,768,1024]{2,1,0:T(8,128)(2,1)} %constant_dynamic-update-slice_fusion, pred[]{:T(512)S(6)} %eq.49), kind=kOutput, calls=%fused_computation.18 | convolution fusion | flops 11302600704 | bytes 31981568 | tf_op jit(solution)/shard_map/escd,edf->escf/dot_general | solution.py:720
  468.9 7.8 multiply_convert_fusion
  476.7 14.0 %fusion.1 = (f32[2,8,224]{2,1,0:T(8,128)S(1)}, bf16[2,8,224,1536]{3,2,1,0:T(8,128)(2,1)}) fusion(bf16[8,1536,2,224]{1,3,0,2:T(8,128)(2,1)} %convolution_convert_fusion.2, bf16[2,8,224,512]{3,2,1,0:T(8,128)(2,1)} %multiply_convert_fusion, bf16[2,256,1536]{2,1,0:T(8,128)(2,1)} %collective-permute-done.8, bf16[2,256,1536]{2,1,0:T(8,128)(2,1)} %copy-done.98, ...), kind=kOutput, calls=%fused_computation.9 | convolution fusion | flops 5678821888 | bytes 28850176 | tf_op jit(solution)/shard_map/escf,efd->escd/dot_general | solution.py:725
  494.0 19.5 %fusion.99 = (f32[2,8,224,512]{3,2,1,0:T(8,128)}, f32[2,8,224,512]{3,2,1,0:T(8,128)}) fusion(f32[2,8,224,1024]{3,2,1,0:T(8,128)} %fusion.4, bf16[2,256,1536]{2,1,0:T(8,128)(2,1)} %collective-permute-done.8, bf16[2,256,1536]{2,1,0:T(8,128)(2,1)} %copy-done.98, pred[]{:T(512)S(6)} %eq.49, bf16[8,1536,2,224]{1,3,0,2:T(8,128)(2,1)} %convolution_convert_fusion.2, ...), kind=kOutput, calls=%fused_computation.208 | convolution fusion | flops 5689835520 | bytes 43530240 | tf_op jit(solution)/shard_map/escd,efd->escf/dot_general | solution.py:737
  513.6 21.6 %convolution_convert_fusion = bf16[2,8,224,1536]{3,2,0,1:T(8,128)(2,1)} fusion(bf16[2,768,1024]{2,1,0:T(8,128)(2,1)} %collective-permute-done.7, bf16[2,768,1024]{2,1,0:T(8,128)(2,1)} %constant_dynamic-update-slice_fusion, pred[]{:T(512)S(6)} %eq.49, f32[2,8,224,512]{3,2,1,0:T(8,128)} %get-tuple-element.201, f32[2,8,224,512]{3,2,1,0:T(8,128)} %get-tuple-element.200), kind=kOutput, calls=%fused_computation.14 | convolution fusion | flops 11315445760 | bytes 31981568 | tf_op jit(solution)/shard_map/escf,edf->escd/dot_general | solution.py:741
  535.2 14.2 %bitcast_convert_fusion = bf16[8,512,1536]{2,1,0:T(8,128)(2,1)} fusion(bf16[2,8,224,1536]{3,2,0,1:T(8,128)(2,1)} %convolution_convert_fusion, s32[8,2,512]{2,1,0:T(2,128)S(1)} %copy-done.121), kind=kOutput, calls=%fused_computation.6 | convolution fusion | flops 5645271040 | bytes 23625728 | tf_op jit(solution)/shard_map/sect,escd->std/dot_general | solution.py:713
  560.9 4.6 copy.231
  565.5 3.8 constant_dynamic-slice_fusion.10
  577.6 8.7 fusion.173
  586.3 7.1 fusion.133
  611.3 5.1 fusion.174
  617.9 3.7 add_convert_fusion.5
  621.5 19.8 %bitcast_convert_fusion.2 = bf16[2,1536,1024]{2,1,0:T(8,128)(2,1)} fusion(bf16[2,8,224,1536]{3,2,0,1:T(8,128)(2,1)} %fusion.6, f32[2,8,224,512]{3,2,1,0:T(8,128)} %get-tuple-element.201, f32[2,8,224,512]{3,2,1,0:T(8,128)} %get-tuple-element.200), kind=kOutput, calls=%fused_computation.16 | convolution fusion | flops 11284774912 | bytes 31981568 | tf_op jit(solution)/shard_map/escd,escf->edf/dot_general | solution.py:754
  641.4 3.9 dynamic-slice_bitcast_fusion
  646.8 3.9 all-to-all-start.6
  650.8 13.2 %bitcast_convert_fusion.1 = bf16[8,512,1536]{2,1,0:T(8,128)(2,1)} fusion(s32[8,2,512]{2,1,0:T(2,128)S(1)} %copy-done.122, bf16[2,8,224,1536]{3,2,1,0:T(8,128)(2,1)} %get-tuple-element.272, f32[2,8,224]{2,1,0:T(8,128)S(1)} %copy-done.144), kind=kOutput, calls=%fused_computation.7 | convolution fusion | flops 5661786112 | bytes 23640064 | tf_op jit(solution)/shard_map/sect,escd->std/dot_general | solution.py:713
  664.1 9.6 bitcast_convert_fusion.3
  687.2 4.4 multiply_reduce_fusion.3
  694.5 13.3 %multiply_reduce_fusion = (f32[3072]{0:T(1024)}, f32[512]{0:T(512)S(1)}, f32[512,3072]{1,0:T(8,128)}) fusion(f32[512,3072]{1,0:T(8,128)} %copy-done.21, f32[512]{0:T(512)S(1)} %copy-done.140, f32[3072]{0:T(1024)S(1)} %copy-done.124, bf16[512,1536]{1,0:T(8,128)(2,1)S(1)} %fusion.169, bf16[3072,1536]{1,0:T(8,128)(2,1)} %bitcast.480), kind=kOutput, calls=%fused_computation.50 | convolution fusion | flops 4841271808 | bytes 23621632 | tf_op jit(solution)/shard_map/dot_general | solution.py:401
  707.9 11.2 fusion.44
  731.5 8.8 collective-permute-done.10
  740.3 15.5 %collective-permute-done.12 = bf16[384,2048]{1,0:T(8,128)(2,1)S(1)} collective-permute-done((bf16[384,2048]{1,0:T(8,128)(2,1)}, bf16[384,2048]{1,0:T(8,128)(2,1)S(1)}, u32[]{:S(2)}, u32[]{:S(2)}) %collective-permute-start.12) | collective-permute-done | bytes 1572896 | tf_op jit(solution)/shard_map/ppermute | solution.py:439
  775.2 3.7 fusion.110
  782.5 74.5 %scan_backward.1 = (bf16[512,3456]{1,0:T(8,128)(2,1)}, f32[4,3328]{1,0:T(4,128)}, f32[1,3328]{1,0:T(1,128)}, f32[1,3072]{1,0:T(1,128)}, f32[1,128]{1,0:T(1,128)}, /*index=5*/f32[1,128]{1,0:T(1,128)}) custom-call(f32[512,3456]{1,0:T(8,128)} %fusion.172.mixed.halo, f32[512,3456]{1,0:T(8,128)} %fusion.172.mixed.halo, f32[512,3072]{1,0:T(8,128)} %get-tuple-element.86.y_cot, ...), custom_call_target="tpu_custom_call" | custom-call | flops 2000000000 | bytes 240000000 | tf_op jit(solution)/shard_map/scan_backward/pallas_call | solution.py:341
  858.2 8.8 collective-permute-done.21
  922.2 37.3 %collective-permute-done.25 = bf16[384,1664]{1,0:T(8,128)(2,1)S(1)} collective-permute-done((bf16[384,1664]{1,0:T(8,128)(2,1)S(1)}, bf16[384,1664]{1,0:T(8,128)(2,1)S(1)}, u32[]{:S(2)}, u32[]{:S(2)}) %collective-permute-start.25) | collective-permute-done | bytes 1277984 | tf_op jit(solution)/shard_map/ppermute | solution.py:439
  972.4 8.3 collective-permute-done.54
  981.6 11.7 collective-permute-done.46
  996.3 9.7 collective-permute-done.36
  1010.8 9.5 fusion.175
  1020.4 10.2 fusion.42
  1036.9 4.9 all-to-all-start.8
  1054.8 4.8 all-to-all-start.7
  1076.5 5.6 collective-permute-done.37
  1083.9 6.6 collective-permute-done.41
  1092.5 3.8 fusion.36
  1110.0 11.3 collective-permute-done.38
  1127.9 5.9 collective-permute-done.42
  1146.1 5.1 collective-permute-done.44
  1152.8 5.6 fusion.45
  1158.4 3.8 all-to-all-start.5
  1163.4 18.5 %all-to-all-done.5 = bf16[2,256,1536]{2,1,0:T(8,128)(2,1)S(1)} async-done(((bf16[2,256,1536]{2,1,0:T(8,128)(2,1)}), bf16[2,256,1536]{2,1,0:T(8,128)(2,1)S(1)}, u32[]{:S(2)}, u32[]{:S(2)}) %all-to-all-start.5) | async-done | bytes 1572896 | tf_op jit(solution)/shard_map/all_to_all | solution.py:790
  1183.9 3.9 broadcast_select_fusion
  (753 shorter events, 332.2 us)
Async XLA Ops:
  7.2 147.0 %all-gather.7.cloned.1.call-start = ((), (), s32[]{:S(2)}) async-start(), calls=%async_computation.11 | async-start | bytes 10948608 | tf_op jit(solution)/shard_map/all_gather | solution.py:417
  9.6 286.2 %all-gather.9.cloned.1.call-start = ((), (), s32[]{:S(2)}) async-start(), calls=%async_computation.12 | async-start | bytes 9732096 | tf_op jit(solution)/shard_map/all_gather | solution.py:417
  15.3 26.9 %all-to-all-start.4 = ((bf16[2,256,1536]{2,1,0:T(8,128)(2,1)}), bf16[2,256,1536]{2,1,0:T(8,128)(2,1)S(1)}, u32[]{:S(2)}, u32[]{:S(2)}) async-start(bf16[2,256,1536]{2,1,0:T(8,128)(2,1)} %get-tuple-element.266), calls=%async_computation.4 | async-start | bytes 3145728 | tf_op jit(solution)/shard_map/all_to_all | solution.py:605
  19.6 327.7 %all-gather.13.cloned.1.call-start = ((), (), s32[]{:S(2)}) async-start(), calls=%async_computation.14 | async-start | bytes 14155776 | tf_op jit(solution)/shard_map/all_gather | solution.py:417
  44.0 30.5 %collective-permute-start.2 = (bf16[1,1,1,1,1,96,1536]{6,5,4,3,2,1,0:T(8,128)(2,1)S(1)}, bf16[1,1,1,1,1,96,1536]{6,5,4,3,2,1,0:T(8,128)(2,1)S(1)}, u32[]{:S(2)}, u32[]{:S(2)}) collective-permute-start(bf16[1,1,1,1,1,96,1536]{6,5,4,3,2,1,0:T(8,128)(2,1)S(1)} %get-tuple-element.253), channel_id=1, source_target_pairs={{0,8},{8,0},{1,9},{9,1},{2,10},{10,2},{3,11},{11,3},{4,12},{12,4},... | collective-permute-start | bytes 884744 | tf_op jit(solution)/shard_map/ppermute | solution.py:439
  50.2 30.3 %all-to-all-start.1 = ((bf16[32,2,740]{2,1,0:T(2,128)(2,1)}), bf16[32,2,740]{2,1,0:T(2,128)(2,1)S(1)}, u32[]{:S(2)}, u32[]{:S(2)}) async-start(bf16[32,2,740]{2,1,0:T(2,128)(2,1)} %reshape.1447), calls=%async_computation.1 | async-start | bytes 196608 | tf_op jit(solution)/shard_map/all_to_all | solution.py:421
  75.4 31.7 %collective-permute-start.3 = (bf16[1,2,1,1,1,96,1536]{6,5,4,3,2,1,0:T(8,128)(2,1)}, bf16[1,2,1,1,1,96,1536]{6,5,4,3,2,1,0:T(8,128)(2,1)S(1)}, u32[]{:S(2)}, u32[]{:S(2)}) collective-permute-start(bf16[1,2,1,1,1,96,1536]{6,5,4,3,2,1,0:T(8,128)(2,1)} %maximum_select_fusion.10), channel_id=1, source_target_pairs={{0,4},{4,0},{1,5},{5,1},{2,6},{6,2},{3,7},{7,3},{8,12},{12,8},{9,1... | collective-permute-start | bytes 1769480 | tf_op jit(solution)/shard_map/ppermute | solution.py:439
  81.1 36.6 %all-to-all-start = ((bf16[2,256,1536]{2,1,0:T(8,128)(2,1)}), bf16[2,256,1536]{2,1,0:T(8,128)(2,1)S(1)}, u32[]{:S(2)}, u32[]{:S(2)}) async-start(bf16[2,256,1536]{2,1,0:T(8,128)(2,1)} %get-tuple-element.267), calls=%async_computation | async-start | bytes 3145728 | tf_op jit(solution)/shard_map/all_to_all | solution.py:605
  108.4 34.1 %collective-permute-start.4 = (bf16[1,2,2,1,1,96,1536]{6,5,4,3,2,1,0:T(8,128)(2,1)}, bf16[1,2,2,1,1,96,1536]{6,5,4,3,2,1,0:T(8,128)(2,1)}, u32[]{:S(2)}, u32[]{:S(2)}) collective-permute-start(bf16[1,2,2,1,1,96,1536]{6,5,4,3,2,1,0:T(8,128)(2,1)} %maximum_select_fusion.6), channel_id=1, source_target_pairs={{0,16},{16,0},{1,17},{17,1},{2,18},{18,2},{3,19},{19,3},{4,20},{20... | collective-permute-start | bytes 3538952 | tf_op jit(solution)/shard_map/ppermute | solution.py:439
  118.4 30.5 %all-to-all-start.2 = ((s32[8,512,6]{1,2,0:T(8,128)}), s32[8,512,6]{1,2,0:T(8,128)S(1)}, u32[]{:S(2)}, u32[]{:S(2)}) async-start(s32[8,512,6]{1,2,0:T(8,128)} %broadcast_in_dim.147), calls=%async_computation.2 | async-start | bytes 262144 | tf_op jit(solution)/shard_map/all_to_all | solution.py:421
  122.2 312.5 %all-gather.11.cloned.1.call-start = ((), (), s32[]{:S(2)}) async-start(), calls=%async_computation.13 | async-start | bytes 14155776 | tf_op jit(solution)/shard_map/all_gather | solution.py:417
  145.9 58.0 %collective-permute-start.5 = (bf16[2,2,2,1,1,96,1536]{6,5,4,3,2,1,0:T(8,128)(2,1)}, bf16[2,2,2,1,1,96,1536]{6,5,4,3,2,1,0:T(8,128)(2,1)}, u32[]{:S(2)}, u32[]{:S(2)}) collective-permute-start(bf16[2,2,2,1,1,96,1536]{6,5,4,3,2,1,0:T(8,128)(2,1)} %fusion.67), channel_id=1, source_target_pairs={{0,2},{2,0},{1,3},{3,1},{4,6},{6,4},{5,7},{7,5},{8,10},{10,8},{9,1... | collective-permute-start | bytes 7077896 | tf_op jit(solution)/shard_map/ppermute | solution.py:439
  149.0 124.8 %collective-permute-start = (bf16[1,768,1024]{2,1,0:T(8,128)(2,1)}, bf16[1,768,1024]{2,1,0:T(8,128)(2,1)}, u32[]{:S(2)}, u32[]{:S(2)}) collective-permute-start(bf16[1,768,1024]{2,1,0:T(8,128)(2,1)} %convert_element_type.790), channel_id=1, source_target_pairs={{0,8},{8,0},{1,9},{9,1},{2,10},{10,2},{3,11},{11,3},{4,12},{12,4},... | collective-permute-start | bytes 4718600 | tf_op jit(solution)/shard_map/ppermute | solution.py:439
  209.5 100.4 %collective-permute-start.6 = (bf16[2,2,2,2,1,96,1536]{6,5,4,3,2,1,0:T(8,128)(2,1)}, bf16[2,2,2,2,1,96,1536]{6,5,4,3,2,1,0:T(8,128)(2,1)}, u32[]{:S(2)}, u32[]{:S(2)}) collective-permute-start(bf16[2,2,2,2,1,96,1536]{6,5,4,3,2,1,0:T(8,128)(2,1)} %maximum_select_fusion.2), channel_id=1, source_target_pairs={{0,1},{1,0},{2,3},{3,2},{4,5},{5,4},{6,7},{7,6},{8,9},{9,8},{10,11... | collective-permute-start | bytes 14155784 | tf_op jit(solution)/shard_map/ppermute | solution.py:439
  209.5 83.4 %collective-permute-start.1 = (bf16[1,256,1536]{2,1,0:T(8,128)(2,1)}, bf16[1,256,1536]{2,1,0:T(8,128)(2,1)S(1)}, u32[]{:S(2)}, u32[]{:S(2)}) collective-permute-start(bf16[1,256,1536]{2,1,0:T(8,128)(2,1)} %convert_element_type.791), channel_id=1, source_target_pairs={{0,8},{8,0},{1,9},{9,1},{2,10},{10,2},{3,11},{11,3},{4,12},{12,4},... | collective-permute-start | bytes 2359304 | tf_op jit(solution)/shard_map/ppermute | solution.py:439
  326.8 250.8 %all-gather.15.cloned.1.call-start = ((), (), s32[]{:S(2)}) async-start(), calls=%async_computation.17 | async-start | bytes 6488064 | tf_op jit(solution)/shard_map/all_gather | solution.py:417
  328.6 257.7 %all-gather.17.cloned.1.call-start = ((), (), s32[]{:S(2)}) async-start(), calls=%async_computation.18 | async-start | bytes 3244032 | tf_op jit(solution)/shard_map/all_gather | solution.py:417
  329.5 71.4 %collective-permute-start.7 = (bf16[2,768,1024]{2,1,0:T(8,128)(2,1)}, bf16[2,768,1024]{2,1,0:T(8,128)(2,1)}, u32[]{:S(2)}, u32[]{:S(2)}) collective-permute-start(bf16[2,768,1024]{2,1,0:T(8,128)(2,1)} %constant_dynamic-update-slice_fusion), channel_id=1, source_target_pairs={{0,16},{16,0},{1,17},{17,1},{2,18},{18,2},{3,19},{19,3},{4,20},{20... | collective-permute-start | bytes 9437192 | tf_op jit(solution)/shard_map/ppermute | solution.py:439
  336.8 97.9 %collective-permute-start.8 = (bf16[2,256,1536]{2,1,0:T(8,128)(2,1)}, bf16[2,256,1536]{2,1,0:T(8,128)(2,1)}, u32[]{:S(2)}, u32[]{:S(2)}) collective-permute-start(bf16[2,256,1536]{2,1,0:T(8,128)(2,1)} %copy-done.98), channel_id=1, source_target_pairs={{0,16},{16,0},{1,17},{17,1},{2,18},{18,2},{3,19},{19,3},{4,20},{20... | collective-permute-start | bytes 4718600 | tf_op jit(solution)/shard_map/ppermute | solution.py:439
  361.5 129.3 %all-to-all-start.3 = ((f32[8,2,512]{2,1,0:T(2,128)}), f32[8,2,512]{2,1,0:T(2,128)S(1)}, u32[]{:S(2)}, u32[]{:S(2)}) async-start(f32[8,2,512]{2,1,0:T(2,128)} %select_bitcast_fusion.1), calls=%async_computation.3 | async-start | bytes 65536 | tf_op jit(solution)/shard_map/all_to_all | solution.py:701
  364.8 322.4 %reduce-scatter.3.cloned.1.call-start = ((), (), s32[]{:S(2)}) async-start(), calls=%async_computation.15 | async-start | bytes 14155776 | tf_op jit(solution)/shard_map/reduce_scatter | solution.py:431
  596.5 21.3 %collective-permute-start.11 = (bf16[384,2048]{1,0:T(8,128)(2,1)}, bf16[384,2048]{1,0:T(8,128)(2,1)}, u32[]{:S(2)}, u32[]{:S(2)}) collective-permute-start(bf16[384,2048]{1,0:T(8,128)(2,1)} %convolution_convert_fusion.13), channel_id=1, source_target_pairs={{0,1},{1,0},{2,3},{3,2},{4,5},{5,4},{6,7},{7,6},{8,9},{9,8},{10,11... | collective-permute-start | bytes 4718600 | tf_op jit(solution)/shard_map/ppermute | solution.py:439
  645.3 73.9 %collective-permute-start.17 = (bf16[2,768,1024]{2,1,0:T(8,128)(2,1)}, bf16[2,768,1024]{2,1,0:T(8,128)(2,1)}, u32[]{:S(2)}, u32[]{:S(2)}) collective-permute-start(bf16[2,768,1024]{2,1,0:T(8,128)(2,1)} %dynamic-slice_bitcast_fusion), channel_id=1, source_target_pairs={{0,16},{16,0},{1,17},{17,1},{2,18},{18,2},{3,19},{19,3},{4,20},{20... | collective-permute-start | bytes 9437192 | tf_op jit(solution)/shard_map/ppermute | solution.py:439
  646.8 29.8 %all-to-all-start.6 = ((f32[8,2,512]{2,1,0:T(2,128)}), f32[8,2,512]{2,1,0:T(2,128)}, u32[]{:S(2)}, u32[]{:S(2)}) async-start(f32[8,2,512]{2,1,0:T(2,128)} %get-tuple-element.196), calls=%async_computation.8 | async-start | bytes 65536 | tf_op jit(solution)/shard_map/all_to_all | solution.py:745
  650.7 502.0 %reduce-scatter.5.cloned.1.call-start = ((), (), s32[]{:S(2)}) async-start(), calls=%async_computation.16 | async-start | bytes 14155776 | tf_op jit(solution)/shard_map/reduce_scatter | solution.py:431
  719.2 36.6 %collective-permute-start.12 = (bf16[384,2048]{1,0:T(8,128)(2,1)}, bf16[384,2048]{1,0:T(8,128)(2,1)S(1)}, u32[]{:S(2)}, u32[]{:S(2)}) collective-permute-start(bf16[384,2048]{1,0:T(8,128)(2,1)} %add_convert_fusion.5), channel_id=1, source_target_pairs={{0,2},{2,0},{1,3},{3,1},{4,6},{6,4},{5,7},{7,5},{8,10},{10,8},{9,1... | collective-permute-start | bytes 4718600 | tf_op jit(solution)/shard_map/ppermute | solution.py:439
  721.0 19.3 %collective-permute-start.10 = (bf16[256,1536]{1,0:T(8,128)(2,1)}, bf16[256,1536]{1,0:T(8,128)(2,1)S(1)}, u32[]{:S(2)}, u32[]{:S(2)}) collective-permute-start(bf16[256,1536]{1,0:T(8,128)(2,1)} %add_convert_fusion.14), channel_id=1, source_target_pairs={{0,16},{16,0},{1,17},{17,1},{2,18},{18,2},{3,19},{19,3},{4,20},{20... | collective-permute-start | bytes 2359304 | tf_op jit(solution)/shard_map/ppermute | solution.py:439
  722.4 37.5 %collective-permute-start.14 = (bf16[768,768]{1,0:T(8,128)(2,1)S(1)}, bf16[768,768]{1,0:T(8,128)(2,1)S(1)}, u32[]{:S(2)}, u32[]{:S(2)}) collective-permute-start(bf16[768,768]{1,0:T(8,128)(2,1)S(1)} %convolution_convert_fusion.18), channel_id=1, source_target_pairs={{0,1},{1,0},{2,3},{3,2},{4,5},{5,4},{6,7},{7,6},{8,9},{9,8},{10,11... | collective-permute-start | bytes 3538952 | tf_op jit(solution)/shard_map/ppermute | solution.py:439
  726.8 35.5 %collective-permute-start.13 = (bf16[768,768]{1,0:T(8,128)(2,1)S(1)}, bf16[768,768]{1,0:T(8,128)(2,1)S(1)}, u32[]{:S(2)}, u32[]{:S(2)}) collective-permute-start(bf16[768,768]{1,0:T(8,128)(2,1)S(1)} %convolution_convert_fusion.19), channel_id=1, source_target_pairs={{0,1},{1,0},{2,3},{3,2},{4,5},{5,4},{6,7},{7,6},{8,9},{9,8},{10,11... | collective-permute-start | bytes 3538952 | tf_op jit(solution)/shard_map/ppermute | solution.py:439
  728.5 128.5 %collective-permute-start.18 = (bf16[768,1024]{1,0:T(8,128)(2,1)}, bf16[768,1024]{1,0:T(8,128)(2,1)}, u32[]{:S(2)}, u32[]{:S(2)}) collective-permute-start(bf16[768,1024]{1,0:T(8,128)(2,1)} %slice_bitcast_fusion.1), channel_id=1, source_target_pairs={{0,8},{8,0},{1,9},{9,1},{2,10},{10,2},{3,11},{11,3},{4,12},{12,4},... | collective-permute-start | bytes 4718600 | tf_op jit(solution)/shard_map/ppermute | solution.py:439
  761.7 95.5 %collective-permute-start.20 = (bf16[768,768]{1,0:T(8,128)(2,1)}, bf16[768,768]{1,0:T(8,128)(2,1)}, u32[]{:S(2)}, u32[]{:S(2)}) collective-permute-start(bf16[768,768]{1,0:T(8,128)(2,1)} %add_convert_fusion.10), channel_id=1, source_target_pairs={{0,16},{16,0},{1,17},{17,1},{2,18},{18,2},{3,19},{19,3},{4,20},{20... | collective-permute-start | bytes 3538952 | tf_op jit(solution)/shard_map/ppermute | solution.py:439
  764.1 93.5 %collective-permute-start.19 = (bf16[768,768]{1,0:T(8,128)(2,1)}, bf16[768,768]{1,0:T(8,128)(2,1)}, u32[]{:S(2)}, u32[]{:S(2)}) collective-permute-start(bf16[768,768]{1,0:T(8,128)(2,1)} %add_convert_fusion.11), channel_id=1, source_target_pairs={{0,2},{2,0},{1,3},{3,1},{4,6},{6,4},{5,7},{7,5},{8,10},{10,8},{9,1... | collective-permute-start | bytes 3538952 | tf_op jit(solution)/shard_map/ppermute | solution.py:439
  767.6 90.6 %collective-permute-start.22 = (bf16[384,1536]{1,0:T(8,128)(2,1)}, bf16[384,1536]{1,0:T(8,128)(2,1)}, u32[]{:S(2)}, u32[]{:S(2)}) collective-permute-start(bf16[384,1536]{1,0:T(8,128)(2,1)} %fusion.47), channel_id=1, source_target_pairs={{0,16},{16,0},{1,17},{17,1},{2,18},{18,2},{3,19},{19,3},{4,20},{20... | collective-permute-start | bytes 3538952 | tf_op jit(solution)/shard_map/ppermute | solution.py:439
  770.9 96.1 %collective-permute-start.21 = (bf16[384,1536]{1,0:T(8,128)(2,1)}, bf16[384,1536]{1,0:T(8,128)(2,1)}, u32[]{:S(2)}, u32[]{:S(2)}) collective-permute-start(bf16[384,1536]{1,0:T(8,128)(2,1)} %fusion.46), channel_id=1, source_target_pairs={{0,2},{2,0},{1,3},{3,1},{4,6},{6,4},{5,7},{7,5},{8,10},{10,8},{9,1... | collective-permute-start | bytes 3538952 | tf_op jit(solution)/shard_map/ppermute | solution.py:439
  857.1 41.6 %collective-permute-start.57 = (bf16[256,1536]{1,0:T(8,128)(2,1)}, bf16[256,1536]{1,0:T(8,128)(2,1)}, u32[]{:S(2)}, u32[]{:S(2)}) collective-permute-start(bf16[256,1536]{1,0:T(8,128)(2,1)} %convolution_convert_fusion.14), channel_id=1, source_target_pairs={{0,1},{1,0},{2,3},{3,2},{4,5},{5,4},{6,7},{7,6},{8,9},{9,8},{10,11... | collective-permute-start | bytes 2359304 | tf_op jit(solution)/shard_map/ppermute | solution.py:439
  857.1 39.1 %collective-permute-start.53 = (bf16[384,2048]{1,0:T(8,128)(2,1)}, bf16[384,2048]{1,0:T(8,128)(2,1)}, u32[]{:S(2)}, u32[]{:S(2)}) collective-permute-start(bf16[384,2048]{1,0:T(8,128)(2,1)} %convolution_convert_fusion.12), channel_id=1, source_target_pairs={{0,1},{1,0},{2,3},{3,2},{4,5},{5,4},{6,7},{7,6},{8,9},{9,8},{10,11... | collective-permute-start | bytes 4718600 | tf_op jit(solution)/shard_map/ppermute | solution.py:439
  857.6 47.7 %collective-permute-start.26 = (bf16[2,256,1536]{2,1,0:T(8,128)(2,1)}, bf16[2,256,1536]{2,1,0:T(8,128)(2,1)}, u32[]{:S(2)}, u32[]{:S(2)}) collective-permute-start(bf16[2,256,1536]{2,1,0:T(8,128)(2,1)} %dynamic-slice_bitcast_fusion.1), channel_id=1, source_target_pairs={{0,16},{16,0},{1,17},{17,1},{2,18},{18,2},{3,19},{19,3},{4,20},{20... | collective-permute-start | bytes 4718600 | tf_op jit(solution)/shard_map/ppermute | solution.py:439
  870.5 20.0 %collective-permute-start.24 = (bf16[384,1664]{1,0:T(8,128)(2,1)}, bf16[384,1664]{1,0:T(8,128)(2,1)}, u32[]{:S(2)}, u32[]{:S(2)}) collective-permute-start(bf16[384,1664]{1,0:T(8,128)(2,1)} %convolution_convert_fusion.6), channel_id=1, source_target_pairs={{0,1},{1,0},{2,3},{3,2},{4,5},{5,4},{6,7},{7,6},{8,9},{9,8},{10,11... | collective-permute-start | bytes 3833864 | tf_op jit(solution)/shard_map/ppermute | solution.py:439
  872.5 20.7 %collective-permute-start.27 = (bf16[384,1792]{1,0:T(8,128)(2,1)}, bf16[384,1792]{1,0:T(8,128)(2,1)}, u32[]{:S(2)}, u32[]{:S(2)}) collective-permute-start(bf16[384,1792]{1,0:T(8,128)(2,1)} %convolution_convert_fusion.11), channel_id=1, source_target_pairs={{0,1},{1,0},{2,3},{3,2},{4,5},{5,4},{6,7},{7,6},{8,9},{9,8},{10,11... | collective-permute-start | bytes 4128776 | tf_op jit(solution)/shard_map/ppermute | solution.py:439
  901.2 64.2 %collective-permute-start.28 = (bf16[384,1792]{1,0:T(8,128)(2,1)S(1)}, bf16[384,1792]{1,0:T(8,128)(2,1)S(1)}, u32[]{:S(2)}, u32[]{:S(2)}) collective-permute-start(bf16[384,1792]{1,0:T(8,128)(2,1)S(1)} %convolution_convert_fusion.10), channel_id=1, source_target_pairs={{0,1},{1,0},{2,3},{3,2},{4,5},{5,4},{6,7},{7,6},{8,9},{9,8},{10,11... | collective-permute-start | bytes 4128776 | tf_op jit(solution)/shard_map/ppermute | solution.py:439
  905.4 54.1 %collective-permute-start.23 = (bf16[384,1664]{1,0:T(8,128)(2,1)S(1)}, bf16[384,1664]{1,0:T(8,128)(2,1)S(1)}, u32[]{:S(2)}, u32[]{:S(2)}) collective-permute-start(bf16[384,1664]{1,0:T(8,128)(2,1)S(1)} %convolution_convert_fusion.7), channel_id=1, source_target_pairs={{0,1},{1,0},{2,3},{3,2},{4,5},{5,4},{6,7},{7,6},{8,9},{9,8},{10,11... | collective-permute-start | bytes 3833864 | tf_op jit(solution)/shard_map/ppermute | solution.py:439
  905.6 53.9 %collective-permute-start.25 = (bf16[384,1664]{1,0:T(8,128)(2,1)S(1)}, bf16[384,1664]{1,0:T(8,128)(2,1)S(1)}, u32[]{:S(2)}, u32[]{:S(2)}) collective-permute-start(bf16[384,1664]{1,0:T(8,128)(2,1)S(1)} %fusion.59), channel_id=1, source_target_pairs={{0,2},{2,0},{1,3},{3,1},{4,6},{6,4},{5,7},{7,5},{8,10},{10,8},{9,1... | collective-permute-start | bytes 3833864 | tf_op jit(solution)/shard_map/ppermute | solution.py:439
  910.8 54.6 %collective-permute-start.29 = (bf16[384,1792]{1,0:T(8,128)(2,1)S(1)}, bf16[384,1792]{1,0:T(8,128)(2,1)S(1)}, u32[]{:S(2)}, u32[]{:S(2)}) collective-permute-start(bf16[384,1792]{1,0:T(8,128)(2,1)S(1)} %fusion.50), channel_id=1, source_target_pairs={{0,16},{16,0},{1,17},{17,1},{2,18},{18,2},{3,19},{19,3},{4,20},{20... | collective-permute-start | bytes 4128776 | tf_op jit(solution)/shard_map/ppermute | solution.py:439
  915.3 55.7 %collective-permute-start.58 = (bf16[2,2,32,1536]{3,2,0,1:T(8,128)(2,1)S(1)}, bf16[2,2,32,1536]{3,2,0,1:T(8,128)(2,1)S(1)}, u32[]{:S(2)}, u32[]{:S(2)}) collective-permute-start(bf16[2,2,32,1536]{3,2,0,1:T(8,128)(2,1)S(1)} %bitcast.529), channel_id=1, source_target_pairs={{0,2},{2,0},{1,3},{3,1},{4,6},{6,4},{5,7},{7,5},{8,10},{10,8},{9,1... | collective-permute-start | bytes 1179656 | tf_op jit(solution)/shard_map/ppermute | solution.py:439
  959.5 88.3 %collective-permute-start.30 = (bf16[256,1536]{1,0:T(8,128)(2,1)}, bf16[256,1536]{1,0:T(8,128)(2,1)}, u32[]{:S(2)}, u32[]{:S(2)}) collective-permute-start(bf16[256,1536]{1,0:T(8,128)(2,1)} %slice_bitcast_fusion.3), channel_id=1, source_target_pairs={{0,8},{8,0},{1,9},{9,1},{2,10},{10,2},{3,11},{11,3},{4,12},{12,4},... | collective-permute-start | bytes 2359304 | tf_op jit(solution)/shard_map/ppermute | solution.py:439
  959.5 21.2 %collective-permute-start.54 = (bf16[2,2,48,2048]{3,2,0,1:T(8,128)(2,1)S(1)}, bf16[2,2,48,2048]{3,2,0,1:T(8,128)(2,1)S(1)}, u32[]{:S(2)}, u32[]{:S(2)}) collective-permute-start(bf16[2,2,48,2048]{3,2,0,1:T(8,128)(2,1)S(1)} %bitcast.513), channel_id=1, source_target_pairs={{0,16},{16,0},{1,17},{17,1},{2,18},{18,2},{3,19},{19,3},{4,20},{20... | collective-permute-start | bytes 2359304 | tf_op jit(solution)/shard_map/ppermute | solution.py:439
  965.4 28.0 %collective-permute-start.46 = (bf16[2,2,96,768]{3,2,0,1:T(8,128)(2,1)S(1)}, bf16[2,2,96,768]{3,2,0,1:T(8,128)(2,1)S(1)}, u32[]{:S(2)}, u32[]{:S(2)}) collective-permute-start(bf16[2,2,96,768]{3,2,0,1:T(8,128)(2,1)S(1)} %bitcast.520), channel_id=1, source_target_pairs={{0,16},{16,0},{1,17},{17,1},{2,18},{18,2},{3,19},{19,3},{4,20},{20... | collective-permute-start | bytes 1769480 | tf_op jit(solution)/shard_map/ppermute | solution.py:439
  965.4 30.0 %collective-permute-start.50 = (bf16[2,2,96,768]{3,2,0,1:T(8,128)(2,1)S(1)}, bf16[2,2,96,768]{3,2,0,1:T(8,128)(2,1)S(1)}, u32[]{:S(2)}, u32[]{:S(2)}) collective-permute-start(bf16[2,2,96,768]{3,2,0,1:T(8,128)(2,1)S(1)} %bitcast.521), channel_id=1, source_target_pairs={{0,2},{2,0},{1,3},{3,1},{4,6},{6,4},{5,7},{7,5},{8,10},{10,8},{9,1... | collective-permute-start | bytes 1769480 | tf_op jit(solution)/shard_map/ppermute | solution.py:439
  971.0 35.0 %collective-permute-start.36 = (bf16[2,2,48,1536]{3,2,0,1:T(8,128)(2,1)S(1)}, bf16[2,2,48,1536]{3,2,0,1:T(8,128)(2,1)S(1)}, u32[]{:S(2)}, u32[]{:S(2)}) collective-permute-start(bf16[2,2,48,1536]{3,2,0,1:T(8,128)(2,1)S(1)} %bitcast.522), channel_id=1, source_target_pairs={{0,16},{16,0},{1,17},{17,1},{2,18},{18,2},{3,19},{19,3},{4,20},{20... | collective-permute-start | bytes 1769480 | tf_op jit(solution)/shard_map/ppermute | solution.py:439
  980.7 27.3 %collective-permute-start.40 = (bf16[2,2,48,1536]{3,2,0,1:T(8,128)(2,1)S(1)}, bf16[2,2,48,1536]{3,2,0,1:T(8,128)(2,1)S(1)}, u32[]{:S(2)}, u32[]{:S(2)}) collective-permute-start(bf16[2,2,48,1536]{3,2,0,1:T(8,128)(2,1)S(1)} %bitcast.523), channel_id=1, source_target_pairs={{0,2},{2,0},{1,3},{3,1},{4,6},{6,4},{5,7},{7,5},{8,10},{10,8},{9,1... | collective-permute-start | bytes 1769480 | tf_op jit(solution)/shard_map/ppermute | solution.py:439
  993.3 68.1 %collective-permute-start.31 = (bf16[2,2,48,1664]{3,2,0,1:T(8,128)(2,1)}, bf16[2,2,48,1664]{3,2,0,1:T(8,128)(2,1)}, u32[]{:S(2)}, u32[]{:S(2)}) collective-permute-start(bf16[2,2,48,1664]{3,2,0,1:T(8,128)(2,1)} %bitcast.453), channel_id=1, source_target_pairs={{0,16},{16,0},{1,17},{17,1},{2,18},{18,2},{3,19},{19,3},{4,20},{20... | collective-permute-start | bytes 1916936 | tf_op jit(solution)/shard_map/ppermute | solution.py:439
  995.4 68.7 %collective-permute-start.33 = (bf16[2,2,48,1792]{3,2,0,1:T(8,128)(2,1)}, bf16[2,2,48,1792]{3,2,0,1:T(8,128)(2,1)}, u32[]{:S(2)}, u32[]{:S(2)}) collective-permute-start(bf16[2,2,48,1792]{3,2,0,1:T(8,128)(2,1)} %bitcast.452), channel_id=1, source_target_pairs={{0,2},{2,0},{1,3},{3,1},{4,6},{6,4},{5,7},{7,5},{8,10},{10,8},{9,1... | collective-permute-start | bytes 2064392 | tf_op jit(solution)/shard_map/ppermute | solution.py:439
  1006.0 61.2 %collective-permute-start.59 = (bf16[2,32,1536]{2,1,0:T(8,128)(2,1)}, bf16[2,32,1536]{2,1,0:T(8,128)(2,1)}, u32[]{:S(2)}, u32[]{:S(2)}) collective-permute-start(bf16[2,32,1536]{2,1,0:T(8,128)(2,1)} %dynamic-slice_bitcast_fusion.9), channel_id=1, source_target_pairs={{0,4},{4,0},{1,5},{5,1},{2,6},{6,2},{3,7},{7,3},{8,12},{12,8},{9,1... | collective-permute-start | bytes 589832 | tf_op jit(solution)/shard_map/ppermute | solution.py:439
  1008.8 59.6 %collective-permute-start.55 = (bf16[2,48,2048]{2,1,0:T(8,128)(2,1)}, bf16[2,48,2048]{2,1,0:T(8,128)(2,1)}, u32[]{:S(2)}, u32[]{:S(2)}) collective-permute-start(bf16[2,48,2048]{2,1,0:T(8,128)(2,1)} %dynamic-slice_bitcast_fusion.2), channel_id=1, source_target_pairs={{0,4},{4,0},{1,5},{5,1},{2,6},{6,2},{3,7},{7,3},{8,12},{12,8},{9,1... | collective-permute-start | bytes 1179656 | tf_op jit(solution)/shard_map/ppermute | solution.py:439
  1047.8 24.5 %collective-permute-start.47 = (bf16[2,96,768]{2,1,0:T(8,128)(2,1)}, bf16[2,96,768]{2,1,0:T(8,128)(2,1)}, u32[]{:S(2)}, u32[]{:S(2)}) collective-permute-start(bf16[2,96,768]{2,1,0:T(8,128)(2,1)} %dynamic-slice_bitcast_fusion.6), channel_id=1, source_target_pairs={{0,4},{4,0},{1,5},{5,1},{2,6},{6,2},{3,7},{7,3},{8,12},{12,8},{9,1... | collective-permute-start | bytes 884744 | tf_op jit(solution)/shard_map/ppermute | solution.py:439
  1054.8 49.0 %all-to-all-start.7 = ((bf16[2,256,1536]{2,1,0:T(8,128)(2,1)}), bf16[2,256,1536]{2,1,0:T(8,128)(2,1)}, u32[]{:S(2)}, u32[]{:S(2)}) async-start(bf16[2,256,1536]{2,1,0:T(8,128)(2,1)} %bitcast.487), calls=%async_computation.9 | async-start | bytes 3145728 | tf_op jit(solution)/shard_map/all_to_all | solution.py:853
  1067.2 23.3 %collective-permute-start.41 = (bf16[2,48,1536]{2,1,0:T(8,128)(2,1)S(1)}, bf16[2,48,1536]{2,1,0:T(8,128)(2,1)S(1)}, u32[]{:S(2)}, u32[]{:S(2)}) collective-permute-start(bf16[2,48,1536]{2,1,0:T(8,128)(2,1)S(1)} %copy-done.117), channel_id=1, source_target_pairs={{0,4},{4,0},{1,5},{5,1},{2,6},{6,2},{3,7},{7,3},{8,12},{12,8},{9,1... | collective-permute-start | bytes 884744 | tf_op jit(solution)/shard_map/ppermute | solution.py:439
  1068.4 32.1 %collective-permute-start.32 = (bf16[2,48,1664]{2,1,0:T(8,128)(2,1)S(1)}, bf16[2,48,1664]{2,1,0:T(8,128)(2,1)S(1)}, u32[]{:S(2)}, u32[]{:S(2)}) collective-permute-start(bf16[2,48,1664]{2,1,0:T(8,128)(2,1)S(1)} %dynamic-slice_bitcast_fusion.4), channel_id=1, source_target_pairs={{0,4},{4,0},{1,5},{5,1},{2,6},{6,2},{3,7},{7,3},{8,12},{12,8},{9,1... | collective-permute-start | bytes 958472 | tf_op jit(solution)/shard_map/ppermute | solution.py:439
  1072.2 66.4 %collective-permute-start.34 = (bf16[2,48,1792]{2,1,0:T(8,128)(2,1)}, bf16[2,48,1792]{2,1,0:T(8,128)(2,1)}, u32[]{:S(2)}, u32[]{:S(2)}) collective-permute-start(bf16[2,48,1792]{2,1,0:T(8,128)(2,1)} %dynamic-slice_bitcast_fusion.3), channel_id=1, source_target_pairs={{0,4},{4,0},{1,5},{5,1},{2,6},{6,2},{3,7},{7,3},{8,12},{12,8},{9,1... | collective-permute-start | bytes 1032200 | tf_op jit(solution)/shard_map/ppermute | solution.py:439
  1073.4 33.8 %collective-permute-start.60 = (bf16[32,1536]{1,0:T(8,128)(2,1)}, bf16[32,1536]{1,0:T(8,128)(2,1)}, u32[]{:S(2)}, u32[]{:S(2)}) collective-permute-start(bf16[32,1536]{1,0:T(8,128)(2,1)} %dynamic-slice_bitcast_fusion.17), channel_id=1, source_target_pairs={{0,8},{8,0},{1,9},{9,1},{2,10},{10,2},{3,11},{11,3},{4,12},{12,4},... | collective-permute-start | bytes 294920 | tf_op jit(solution)/shard_map/ppermute | solution.py:439
  1082.1 54.1 %collective-permute-start.56 = (bf16[48,2048]{1,0:T(8,128)(2,1)}, bf16[48,2048]{1,0:T(8,128)(2,1)}, u32[]{:S(2)}, u32[]{:S(2)}) collective-permute-start(bf16[48,2048]{1,0:T(8,128)(2,1)} %dynamic-slice_bitcast_fusion.10), channel_id=1, source_target_pairs={{0,8},{8,0},{1,9},{9,1},{2,10},{10,2},{3,11},{11,3},{4,12},{12,4},... | collective-permute-start | bytes 589832 | tf_op jit(solution)/shard_map/ppermute | solution.py:439
  1090.5 32.4 %collective-permute-start.48 = (bf16[96,768]{1,0:T(8,128)(2,1)}, bf16[96,768]{1,0:T(8,128)(2,1)}, u32[]{:S(2)}, u32[]{:S(2)}) collective-permute-start(bf16[96,768]{1,0:T(8,128)(2,1)} %dynamic-slice_bitcast_fusion.14), channel_id=1, source_target_pairs={{0,8},{8,0},{1,9},{9,1},{2,10},{10,2},{3,11},{11,3},{4,12},{12,4},... | collective-permute-start | bytes 442376 | tf_op jit(solution)/shard_map/ppermute | solution.py:439
  1100.5 26.3 %collective-permute-start.52 = (bf16[96,768]{1,0:T(8,128)(2,1)}, bf16[96,768]{1,0:T(8,128)(2,1)}, u32[]{:S(2)}, u32[]{:S(2)}) collective-permute-start(bf16[96,768]{1,0:T(8,128)(2,1)} %dynamic-slice_bitcast_fusion.13), channel_id=1, source_target_pairs={{0,8},{8,0},{1,9},{9,1},{2,10},{10,2},{3,11},{11,3},{4,12},{12,4},... | collective-permute-start | bytes 442376 | tf_op jit(solution)/shard_map/ppermute | solution.py:439
  1158.4 23.5 %all-to-all-start.5 = ((bf16[2,256,1536]{2,1,0:T(8,128)(2,1)}), bf16[2,256,1536]{2,1,0:T(8,128)(2,1)S(1)}, u32[]{:S(2)}, u32[]{:S(2)}) async-start(bf16[2,256,1536]{2,1,0:T(8,128)(2,1)} %bitcast.499), calls=%async_computation.7 | async-start | bytes 3145728 | tf_op jit(solution)/shard_map/all_to_all | solution.py:790
  (196 other events, 2658.5 us)
Sparse Core Ops, SparseCore 0:
  11.5 115.8 all-gather.6
  130.2 151.5 all-gather.8
  283.4 63.8 all-gather.12
  349.4 65.2 all-gather.10
  418.0 70.6 all-gather.14
  491.4 57.4 all-gather.16
  551.2 120.2 reduce-scatter.2
  775.3 171.2 reduce-scatter.4
